TPU v7x, 512 devices: a whole 4x4x16 slice. The times are simulated.
512 devices in a mesh: sample: 32 (over y, x, core), space: 16 (over z).
Axes of the slice: x: 4, y: 4, z: 16, core: 2. Of those that a mesh axis runs over, the one named last changes fastest.
Arguments:
- volumes: bfloat16 [32, 32, 64, 16, 128], P('sample', None, 'space'), may hold values from -360 to 360
- depth_kernel: float32 [32, 27], replicated, may hold values from -1.25 to 1.25
- point_weight: bfloat16 [32, 32], replicated, may hold values from -1 to 1
- cotangent: bfloat16 [32, 32, 64, 16, 128], P('sample', None, 'space'), may hold values from -4.1 to 4.1
Outputs:
- whitened: bfloat16 [32, 32, 64, 16, 128], P('sample', None, 'space')
- d_volumes: bfloat16 [32, 32, 64, 16, 128], P('sample', None, 'space')
- d_point: float32 [32, 32], replicated
- d_kernel: float32 [32, 27], replicated
All inputs are finite; a program needn't handle non-finite values.
Results may differ from a plain program's by a relative error of at most 0.0067.
Values may be sent and summed in bfloat16 or wider, within the bound.
No kernel may reach another device: no remote copies, remote signals or barrier semaphores. Data moves between devices by JAX's collectives and lax.ppermute only.
A program may use at most 64 MiB of HBM per device.

v0:
```python
from functools import partial
import math

import jax
import jax.numpy as jnp
from jax import lax
from jax.sharding import PartitionSpec as P

GSIZE = 16
NEWTON = 5
GROUPS = 2


epsilon = 1e-05
highest = lax.Precision.HIGHEST


def with_halo(block, sides, width):
    for axis, dim in sides:
        count = lax.axis_size(axis)
        forward = [(i, i + 1) for i in range(count - 1)]
        backward = [(target, source) for source, target in forward]
        low = lax.ppermute(
            lax.slice_in_dim(block, block.shape[dim] - width, None, axis=dim), axis, forward
        )
        high = lax.ppermute(lax.slice_in_dim(block, 0, width, axis=dim), axis, backward)
        block = jnp.concatenate([low, block, high], axis=dim)
    return block


def matmul_high(matrix, operand):
    return jnp.matmul(matrix, operand, precision=highest)


def contract_rows(matrix, operand):
    return jnp.einsum(
        "cv,dv->cd", matrix, operand, precision=highest, preferred_element_type=jnp.float32
    )


def contract_cols(matrix, operand):
    return jnp.einsum(
        "kc,kv->cv", matrix, operand, precision=highest, preferred_element_type=jnp.float32
    )


def block_diagonal(blocks):
    identity = jnp.eye(blocks.shape[0], dtype=blocks.dtype)
    full_size = blocks.shape[0] * blocks.shape[1]
    return jnp.einsum("gh,gij->gihj", identity, blocks, precision=highest).reshape(
        full_size, full_size
    )


def whiten_stats(first_sums, second_sums, voxel_count):
    groups = second_sums.shape[0]
    group_size = second_sums.shape[1]
    average = (first_sums / voxel_count).reshape(groups, group_size)
    identity = jnp.eye(group_size, dtype=second_sums.dtype)
    covariance = (
        second_sums / voxel_count - average[:, :, None] * average[:, None, :] + epsilon * identity
    )
    traces = jnp.trace(covariance, axis1=1, axis2=2)
    normed = covariance / traces[:, None, None]
    project = jnp.broadcast_to(identity, covariance.shape)
    for newton_step in range(NEWTON):
        cubed = matmul_high(matmul_high(project, project), project)
        project = 0.5 * (3.0 * project - matmul_high(cubed, normed))
    whiten_mat = project / jnp.sqrt(traces)[:, None, None]
    offset = jnp.einsum("gij,gj->gi", whiten_mat, average, precision=highest)
    return (whiten_mat, offset)


def adjoint_terms(pull_back, whiten_mat, grad_first, grad_second):
    d_first, d_second = pull_back(
        (grad_second, -grad_first.reshape(whiten_mat.shape[0], whiten_mat.shape[1]))
    )
    adjoint = block_diagonal(jnp.swapaxes(whiten_mat, 1, 2))
    symmetric = block_diagonal(d_second + jnp.swapaxes(d_second, 1, 2))
    return (d_first, adjoint, symmetric)


def gradient_signal(adjoint, d_first, symmetric, grad_part, mixed_part):
    first_term = jnp.dot(adjoint, grad_part, precision=highest, preferred_element_type=jnp.float32)
    third_term = jnp.dot(
        symmetric, mixed_part, precision=highest, preferred_element_type=jnp.float32
    )
    return first_term + d_first[:, None] + third_term


def pad_sides(extended):
    return jnp.pad(extended, ((0, 0), (0, 0), (1, 1), (1, 1)))


def tap_cells(padded, tap_index, depth_cells):
    plane_off = tap_index // 9
    row_off = tap_index // 3 % 3
    col_off = tap_index % 3
    height = padded.shape[2] - 2
    width_cells = padded.shape[3] - 2
    return padded[
        :,
        plane_off : plane_off + depth_cells,
        row_off : row_off + height,
        col_off : col_off + width_cells,
    ]


def depth_conv(extended, kernel, depth_cells):
    padded = pad_sides(extended)
    summed = jnp.zeros(
        (extended.shape[0], depth_cells, extended.shape[2], extended.shape[3]), jnp.float32
    )
    for tap_index in range(27):
        summed = summed + kernel[:, tap_index][:, None, None, None] * tap_cells(
            padded, tap_index, depth_cells
        ).astype(jnp.float32)
    return summed


def depth_adjoint(grad_ext, kernel, depth_cells):
    padded = pad_sides(grad_ext)
    height = grad_ext.shape[2]
    width_cells = grad_ext.shape[3]
    summed = jnp.zeros((grad_ext.shape[0], depth_cells, height, width_cells), jnp.float32)
    for tap_index in range(27):
        plane_off = 2 - tap_index // 9
        row_off = 2 - tap_index // 3 % 3
        col_off = 2 - tap_index % 3
        summed = (
            summed
            + kernel[:, tap_index][:, None, None, None]
            * padded[
                :,
                plane_off : plane_off + depth_cells,
                row_off : row_off + height,
                col_off : col_off + width_cells,
            ]
        )
    return summed


def on_device(volumes, depth_kernel, point_weight, cotangent):
    volume = volumes[0]
    grad_in = cotangent[0]
    channels, depth_cells, height, width_cells = volume.shape
    voxels = depth_cells * height * width_cells
    voxel_count = float(voxels * lax.axis_size("sample") * lax.axis_size("space"))
    grad_flat = grad_in.reshape(channels, voxels)
    extended = with_halo(volume, (("space", 1),), 1)
    hidden = (
        depth_conv(extended, depth_kernel, depth_cells)
        .astype(jnp.bfloat16)
        .reshape(channels, voxels)
    )
    mixed_out = jnp.dot(point_weight, hidden, preferred_element_type=jnp.float32).astype(
        jnp.bfloat16
    )
    grouped = mixed_out.reshape(GROUPS, GSIZE, voxels)
    local_first = jnp.sum(mixed_out.astype(jnp.float32), axis=1)
    local_second = jnp.einsum("giv,gjv->gij", grouped, grouped, preferred_element_type=jnp.float32)
    grad_first = jnp.sum(grad_flat.astype(jnp.float32), axis=1)
    grad_second = jnp.einsum(
        "giv,gjv->gij",
        grad_flat.reshape(GROUPS, GSIZE, voxels),
        grouped,
        preferred_element_type=jnp.float32,
    )
    padded_x = pad_sides(extended)
    weight_f = point_weight.astype(jnp.float32)
    stats_fn = partial(whiten_stats, voxel_count=voxel_count)
    first_sums, second_sums, grad_first, grad_second = lax.psum(
        (local_first, local_second, grad_first, grad_second), ("sample", "space")
    )
    (whiten_mat, offset), pull_back = jax.vjp(stats_fn, first_sums, second_sums)
    d_first, adjoint, symmetric = adjoint_terms(pull_back, whiten_mat, grad_first, grad_second)
    whitened = (
        jnp.dot(
            block_diagonal(whiten_mat),
            mixed_out,
            precision=highest,
            preferred_element_type=jnp.float32,
        )
        - offset.reshape(channels)[:, None]
    ).astype(jnp.bfloat16)
    d_mixed = gradient_signal(adjoint, d_first, symmetric, grad_flat, mixed_out)
    d_hidden = contract_cols(weight_f, d_mixed).reshape(channels, depth_cells, height, width_cells)
    grad_ext = with_halo(d_hidden, (("space", 1),), 1)
    kernel_terms = jnp.stack(
        [
            jnp.sum(
                d_hidden * tap_cells(padded_x, tap_index, depth_cells).astype(jnp.float32),
                axis=(1, 2, 3),
            )
            for tap_index in range(27)
        ],
        axis=1,
    )
    d_point, d_kernel = lax.psum(
        (contract_rows(d_mixed, hidden), kernel_terms), ("sample", "space")
    )
    d_volume = depth_adjoint(grad_ext, depth_kernel, depth_cells).astype(jnp.bfloat16)
    scale_out = 1.0 / math.sqrt(voxel_count)
    return (
        whitened.reshape(1, channels, depth_cells, height, width_cells),
        d_volume[None],
        d_point * scale_out,
        d_kernel * scale_out,
    )


def solution(mesh):
    in_specs = (
        P("sample", None, "space", None, None),
        P(),
        P(),
        P("sample", None, "space", None, None),
    )
    out_specs = (
        P("sample", None, "space", None, None),
        P("sample", None, "space", None, None),
        P(),
        P(),
    )
    return jax.shard_map(
        on_device, mesh=mesh, in_specs=in_specs, out_specs=out_specs, check_vma=False
    )
```

profile of v0, /device:TPU:1, one launch (start us, length us, event | category | flops | bytes accessed | tf_op | source)
XLA Modules:
  0.0 388.2 jit_solution(1286581559153312555)
XLA Ops:
  0.7 1.1 fusion.214
  1.8 4.4 %collective-permute-start = (bf16[32,1,16,128]{3,2,1,0:T(8,128)(2,1)S(1)}, bf16[32,1,16,128]{3,2,1,0:T(8,128)(2,1)S(1)}, u32[]{:S(2)}, u32[]{:S(2)}) collective-permute-start(bf16[32,1,16,128]{3,2,1,0:T(8,128)(2,1)S(1)} %get-tuple-element.77), channel_id=1, source_target_pairs={{0,1},{1,2},{2,3},{3,4},{4,5},{5,6},{6,7},{7,8},{8,9},{9,10},{10,1... | collective-permute-start | bytes 393224 | tf_op jit(solution)/shard_map/ppermute | solution.py:23
  6.1 1.3 collective-permute-start.1
  9.2 1.9 slice_reduce_fusion.25
  11.1 2.6 slice_reduce_fusion.26
  13.7 2.1 reshape_squeeze.3
  15.8 2.1 reshape_reshape_squeeze.3
  17.8 2.2 reshape.120
  22.5 3.0 select_maximum_fusion.2
  25.5 7.8 %fusion.59 = bf16[32,4,16,128]{3,2,1,0:T(8,128)(2,1)S(1)} fusion(bf16[32,4,16,128]{3,2,1,0:T(8,128)(2,1)S(1)} %bitcast.174, bf16[32,1,16,128]{3,2,1,0:T(8,128)(2,1)} %collective-permute-done.1, bf16[32,1,16,128]{3,2,1,0:T(8,128)(2,1)S(1)} %collective-permute-done, f32[32]{0:T(128)} %get-tuple-element.67, f32[32]{0:T(128)} %get-tuple-element.68, ...), kind=kLoop, calls=%fused_computation.140 | loop fusion | flops 21757952 | bytes 13897088 | tf_op jit(solution)/shard_map/convert_element_type | solution.py:153
  33.3 1.1 convert_reduce_fusion.1
  34.5 1.0 fusion.215
  36.4 111.9 %all-reduce.3 = (f32[32]{0:T(128)}, f32[2,16,16]{2,1,0:T(8,128)}, f32[2,16,16]{1,2,0:T(8,128)}, f32[32]{0:T(128)}) all-reduce(f32[32]{0:T(128)} %get-tuple-element.91, f32[2,16,16]{2,1,0:T(8,128)} %fusion.215, f32[2,16,16]{1,2,0:T(8,128)} %convolution_bitcast_fusion, ...), channel_id=1, replica_groups=mesh['sample'=32,'space'=16] {'sample','space'}, use_global_device_ids=true, to_apply=%region_2.3 | all-reduce | flops 1088 | bytes 8704 | tf_op jit(solution)/shard_map/psum | solution.py:172
  148.3 1.2 broadcast_multiply_fusion.3
  149.4 1.3 mul.759
  150.7 1.3 reshape.121
  152.0 1.1 neg.36
  153.1 1.3 neg.37
  154.4 1.3 reshape.123
  155.7 1.4 broadcast_multiply_fusion.2
  157.1 1.4 copy.70
  158.5 1.3 subtract_add_fusion
  159.9 1.4 copy.72
  162.7 1.6 fusion.212
  164.2 1.4 copy.73
  165.6 1.0 fusion.137
  168.7 1.5 fusion.211
  170.3 1.4 copy.77
  174.2 1.5 fusion.210
  175.7 1.4 copy.81
  179.6 1.5 fusion.209
  181.2 1.4 copy.85
  183.5 1.1 fusion.106
  186.2 1.0 fusion.108
  190.8 1.0 fusion.109
  198.2 1.6 fusion.208
  199.8 1.0 fusion.107
  205.4 1.6 multiply_reduce_fusion.2
  207.0 1.4 copy.125
  208.4 1.4 copy.89
  209.7 1.5 multiply_reduce_fusion.3
  211.3 1.4 copy.90
  214.2 1.4 multiply_reduce_fusion.1
  215.7 1.4 copy.126
  217.1 1.4 copy.91
  218.5 1.5 multiply_bitcast_fusion
  220.0 1.4 reshape.118
  221.4 1.4 reshape.117
  222.9 1.7 convolution_add_fusion.1
  224.6 1.3 convolution_add_fusion
  225.9 1.5 fusion.91
  227.3 1.4 fusion.90
  228.9 6.7 %fusion.60 = (f32[32]{0:T(128)S(1)}, f32[32]{0:T(128)S(1)}, f32[32]{0:T(128)}, f32[32]{0:T(128)}, f32[32]{0:T(128)}, /*index=5*/f32[32]{0:T(128)}, f32[32]{0:T(1...) fusion(f32[32,4,16,128]{3,2,1,0:T(8,128)S(1)} %bitcast.164, ...), kind=kLoop, calls=%fused_computation.141 | loop fusion | flops 14155200 | bytes 10488064 | tf_op jit(solution)/shard_map/reduce_sum | solution.py:191
  237.1 1.3 sub.49
  238.4 1.4 reshape.115
  239.8 4.3 %fusion.57 = (f32[32]{0:T(128)}, f32[32]{0:T(128)}, f32[32]{0:T(128)}, f32[32]{0:T(128)}, f32[32]{0:T(128)}, /*index=5*/f32[32]{0:T(128)}, f32[32]{0:T(128)}, f32[32]{0:T(128)}) fusion(f32[32,4,16,128]{3,2,1,0:T(8,128)S(1)} %bitcast.166, bf16[32,6,18,130]{3,2,1,0:T(8,128)(2,1)S(1)} %select_maximum_fusion.2, bf16[32,4,16,128]{3,2,1,0:T(8,128)(2,1)} %bitcast.172, ...), kind=kLoop, calls=%fused_computation.138 | loop fusion | flops 6815488 | bytes 4981760 | tf_op jit(solution)/shard_map/reduce_sum | solution.py:191
  244.4 2.8 stack.111
  247.2 99.9 %all-reduce.2 = (f32[32,32]{1,0:T(8,128)S(1)}, f32[32,27]{0,1:T(8,128)S(1)}) all-reduce(f32[32,32]{1,0:T(8,128)} %fusion.91, f32[32,27]{0,1:T(8,128)S(1)} %stack.111), channel_id=1, replica_groups=mesh['sample'=32,'space'=16] {'sample','space'}, use_global_device_ids=true, to_apply=%region_11.12 | all-reduce | flops 1888 | bytes 15104 | tf_op jit(solution)/shard_map/psum | solution.py:199
  347.1 3.3 collective-permute-start.2
  350.3 1.3 collective-permute-start.3
  351.6 1.6 fusion.5
  355.6 3.7 collective-permute-done.3
  359.3 3.4 select_maximum_fusion
  363.0 25.1 %fusion.94 = bf16[1,32,4,16,128]{4,3,2,1,0:T(8,128)(2,1)} fusion(f32[32,6,18,130]{3,2,1,0:T(8,128)} %select_maximum_fusion, f32[32]{0:T(128)S(1)} %copy-done.23, f32[32]{0:T(128)S(1)} %copy-done.24, f32[32]{0:T(128)S(1)} %copy-done.26, f32[32]{0:T(128)S(1)} %copy-done.27, f32[32,4,16,128]{3,2,1,0:T(8,128)S(1)} %bitcast.168, ...), kind=kLoop, calls=%fused_computation.206 | loop fusion | flops 14680064 | bytes 27266432 | tf_op jit(solution)/shard_map/broadcast_in_dim | solution.py:206
  (148 shorter events, 36.9 us)
Async XLA Ops:
  0.6 32.7 %copy-start = (bf16[32,32]{1,0:T(8,128)(2,1)S(1)}, bf16[32,32]{1,0:T(8,128)(2,1)}, u32[]{:S(2)}) copy-start(bf16[32,32]{1,0:T(8,128)(2,1)} %param.6) | copy-start | bytes 6148
  0.6 21.9 %copy-start.2 = (bf16[1,32,4,16,128]{4,3,2,1,0:T(8,128)(2,1)S(1)}, bf16[1,32,4,16,128]{4,3,2,1,0:T(8,128)(2,1)}, u32[]{:S(2)}) copy-start(bf16[1,32,4,16,128]{4,3,2,1,0:T(8,128)(2,1)} %param.4) | copy-start | bytes 1572868
  0.7 21.0 %copy-start.3 = (bf16[1,32,4,16,128]{4,3,2,1,0:T(8,128)(2,1)S(1)}, bf16[1,32,4,16,128]{4,3,2,1,0:T(8,128)(2,1)}, u32[]{:S(2)}) copy-start(bf16[1,32,4,16,128]{4,3,2,1,0:T(8,128)(2,1)} %param.7) | copy-start | bytes 1572868
  1.8 20.8 %collective-permute-start = (bf16[32,1,16,128]{3,2,1,0:T(8,128)(2,1)S(1)}, bf16[32,1,16,128]{3,2,1,0:T(8,128)(2,1)S(1)}, u32[]{:S(2)}, u32[]{:S(2)}) collective-permute-start(bf16[32,1,16,128]{3,2,1,0:T(8,128)(2,1)S(1)} %get-tuple-element.77), channel_id=1, source_target_pairs={{0,1},{1,2},{2,3},{3,4},{4,5},{5,6},{6,7},{7,8},{8,9},{9,10},{10,1... | collective-permute-start | bytes 393224 | tf_op jit(solution)/shard_map/ppermute | solution.py:23
  6.1 16.4 %collective-permute-start.1 = (bf16[32,1,16,128]{3,2,1,0:T(8,128)(2,1)S(1)}, bf16[32,1,16,128]{3,2,1,0:T(8,128)(2,1)}, u32[]{:S(2)}, u32[]{:S(2)}) collective-permute-start(bf16[32,1,16,128]{3,2,1,0:T(8,128)(2,1)S(1)} %get-tuple-element.78), channel_id=1, source_target_pairs={{1,0},{2,1},{3,2},{4,3},{5,4},{6,5},{7,6},{8,7},{9,8},{10,9},{11,1... | collective-permute-start | bytes 393224 | tf_op jit(solution)/shard_map/ppermute | solution.py:26
  25.5 9.9 %copy-start.5 = (bf16[2,16,8192]{2,1,0:T(8,128)(2,1)S(1)}, bf16[2,16,8192]{2,1,0:T(8,128)(2,1)}, u32[]{:S(2)}) copy-start(bf16[2,16,8192]{2,1,0:T(8,128)(2,1)} %reshape_reshape_squeeze.3) | copy-start | bytes 1572868
  34.5 191.4 %copy-start.1 = (bf16[8192,32]{0,1:T(8,128)(2,1)}, bf16[8192,32]{0,1:T(8,128)(2,1)S(1)}, u32[]{:S(2)}) copy-start(bf16[8192,32]{0,1:T(8,128)(2,1)S(1)} %get-tuple-element.92) | copy-start | bytes 1572868
  162.1 0.6 copy-start.16
  166.6 0.6 copy-start.10
  168.1 0.6 copy-start.13
  172.4 0.6 copy-start.6
  173.0 0.6 copy-start.11
  173.6 0.6 copy-start.14
  177.8 0.6 copy-start.7
  178.4 0.6 copy-start.12
  179.0 0.6 copy-start.15
  183.3 2.7 copy-start.8
  222.9 4.4 %copy-start.4 = (f32[32,8192]{1,0:T(8,128)S(1)}, f32[32,8192]{1,0:T(8,128)}, u32[]{:S(2)}) copy-start(f32[32,8192]{1,0:T(8,128)} %reshape.120) | copy-start | bytes 3145732
  228.9 7.5 %copy-start.9 = (f32[2,16,16]{1,2,0:T(8,128)S(1)}, f32[2,16,16]{1,2,0:T(8,128)}, u32[]{:S(2)}) copy-start(f32[2,16,16]{1,2,0:T(8,128)} %get-tuple-element.80) | copy-start | bytes 6148
  228.9 7.5 %copy-start.44 = (f32[2,16,1]{1,0,2:T(2,128)S(1)}, f32[2,16,1]{1,0,2:T(2,128)}, u32[]{:S(2)}) copy-start(f32[2,16,1]{1,0,2:T(2,128)} %reshape.121) | copy-start | bytes 388
  244.2 118.6 %copy-start.17 = (f32[32]{0:T(128)S(1)}, f32[32]{0:T(128)}, u32[]{:S(2)}) copy-start(f32[32]{0:T(128)} %get-tuple-element.61) | copy-start | bytes 388
  244.2 118.6 %copy-start.18 = (f32[32]{0:T(128)S(1)}, f32[32]{0:T(128)}, u32[]{:S(2)}) copy-start(f32[32]{0:T(128)} %get-tuple-element.62) | copy-start | bytes 388
  244.2 118.6 %copy-start.19 = (f32[32]{0:T(128)S(1)}, f32[32]{0:T(128)}, u32[]{:S(2)}) copy-start(f32[32]{0:T(128)} %get-tuple-element.63) | copy-start | bytes 388
  244.2 118.6 %copy-start.20 = (f32[32]{0:T(128)S(1)}, f32[32]{0:T(128)}, u32[]{:S(2)}) copy-start(f32[32]{0:T(128)} %get-tuple-element.64) | copy-start | bytes 388
  244.2 118.6 %copy-start.21 = (f32[32]{0:T(128)S(1)}, f32[32]{0:T(128)}, u32[]{:S(2)}) copy-start(f32[32]{0:T(128)} %get-tuple-element.65) | copy-start | bytes 388
  244.2 118.6 %copy-start.22 = (f32[32]{0:T(128)S(1)}, f32[32]{0:T(128)}, u32[]{:S(2)}) copy-start(f32[32]{0:T(128)} %get-tuple-element.66) | copy-start | bytes 388
  244.2 118.6 %copy-start.23 = (f32[32]{0:T(128)S(1)}, f32[32]{0:T(128)}, u32[]{:S(2)}) copy-start(f32[32]{0:T(128)} %get-tuple-element.67) | copy-start | bytes 388
  244.2 118.6 %copy-start.24 = (f32[32]{0:T(128)S(1)}, f32[32]{0:T(128)}, u32[]{:S(2)}) copy-start(f32[32]{0:T(128)} %get-tuple-element.68) | copy-start | bytes 388
  244.2 118.6 %copy-start.25 = (f32[32]{0:T(128)S(1)}, f32[32]{0:T(128)}, u32[]{:S(2)}) copy-start(f32[32]{0:T(128)} %get-tuple-element.42) | copy-start | bytes 388
  244.2 118.6 %copy-start.26 = (f32[32]{0:T(128)S(1)}, f32[32]{0:T(128)}, u32[]{:S(2)}) copy-start(f32[32]{0:T(128)} %get-tuple-element.43) | copy-start | bytes 388
  244.2 118.6 %copy-start.27 = (f32[32]{0:T(128)S(1)}, f32[32]{0:T(128)}, u32[]{:S(2)}) copy-start(f32[32]{0:T(128)} %get-tuple-element.44) | copy-start | bytes 388
  244.2 118.6 %copy-start.28 = (f32[32]{0:T(128)S(1)}, f32[32]{0:T(128)}, u32[]{:S(2)}) copy-start(f32[32]{0:T(128)} %get-tuple-element.45) | copy-start | bytes 388
  244.3 118.6 %copy-start.29 = (f32[32]{0:T(128)S(1)}, f32[32]{0:T(128)}, u32[]{:S(2)}) copy-start(f32[32]{0:T(128)} %get-tuple-element.46) | copy-start | bytes 388
  244.3 118.6 %copy-start.30 = (f32[32]{0:T(128)S(1)}, f32[32]{0:T(128)}, u32[]{:S(2)}) copy-start(f32[32]{0:T(128)} %get-tuple-element.47) | copy-start | bytes 388
  244.3 118.6 %copy-start.31 = (f32[32]{0:T(128)S(1)}, f32[32]{0:T(128)}, u32[]{:S(2)}) copy-start(f32[32]{0:T(128)} %get-tuple-element.48) | copy-start | bytes 388
  244.3 118.6 %copy-start.32 = (f32[32]{0:T(128)S(1)}, f32[32]{0:T(128)}, u32[]{:S(2)}) copy-start(f32[32]{0:T(128)} %get-tuple-element.49) | copy-start | bytes 388
  244.3 118.6 %copy-start.33 = (f32[32]{0:T(128)S(1)}, f32[32]{0:T(128)}, u32[]{:S(2)}) copy-start(f32[32]{0:T(128)} %get-tuple-element.50) | copy-start | bytes 388
  244.3 118.6 %copy-start.34 = (f32[32]{0:T(128)S(1)}, f32[32]{0:T(128)}, u32[]{:S(2)}) copy-start(f32[32]{0:T(128)} %get-tuple-element.51) | copy-start | bytes 388
  244.3 118.6 %copy-start.35 = (f32[32]{0:T(128)S(1)}, f32[32]{0:T(128)}, u32[]{:S(2)}) copy-start(f32[32]{0:T(128)} %get-tuple-element.52) | copy-start | bytes 388
  244.3 118.6 %copy-start.36 = (f32[32]{0:T(128)S(1)}, f32[32]{0:T(128)}, u32[]{:S(2)}) copy-start(f32[32]{0:T(128)} %get-tuple-element.53) | copy-start | bytes 388
  244.3 118.6 %copy-start.37 = (f32[32]{0:T(128)S(1)}, f32[32]{0:T(128)}, u32[]{:S(2)}) copy-start(f32[32]{0:T(128)} %get-tuple-element.54) | copy-start | bytes 388
  244.3 118.6 %copy-start.38 = (f32[32]{0:T(128)S(1)}, f32[32]{0:T(128)}, u32[]{:S(2)}) copy-start(f32[32]{0:T(128)} %get-tuple-element.55) | copy-start | bytes 388
  244.4 118.6 %copy-start.39 = (f32[32]{0:T(128)S(1)}, f32[32]{0:T(128)}, u32[]{:S(2)}) copy-start(f32[32]{0:T(128)} %get-tuple-element.56) | copy-start | bytes 388
  244.4 118.6 %copy-start.40 = (f32[32]{0:T(128)S(1)}, f32[32]{0:T(128)}, u32[]{:S(2)}) copy-start(f32[32]{0:T(128)} %get-tuple-element.57) | copy-start | bytes 388
  244.4 118.6 %copy-start.41 = (f32[32]{0:T(128)S(1)}, f32[32]{0:T(128)}, u32[]{:S(2)}) copy-start(f32[32]{0:T(128)} %get-tuple-element.58) | copy-start | bytes 388
  244.4 118.6 %copy-start.42 = (f32[32]{0:T(128)S(1)}, f32[32]{0:T(128)}, u32[]{:S(2)}) copy-start(f32[32]{0:T(128)} %get-tuple-element.59) | copy-start | bytes 388
  244.4 118.6 %copy-start.43 = (f32[32]{0:T(128)S(1)}, f32[32]{0:T(128)}, u32[]{:S(2)}) copy-start(f32[32]{0:T(128)} %get-tuple-element.60) | copy-start | bytes 388
  347.1 8.5 %collective-permute-start.2 = (f32[32,1,16,128]{3,2,1,0:T(8,128)}, f32[32,1,16,128]{3,2,1,0:T(8,128)S(1)}, u32[]{:S(2)}, u32[]{:S(2)}) collective-permute-start(f32[32,1,16,128]{3,2,1,0:T(8,128)} %get-tuple-element.75), channel_id=1, source_target_pairs={{0,1},{1,2},{2,3},{3,4},{4,5},{5,6},{6,7},{7,8},{8,9},{9,10},{10,1... | collective-permute-start | bytes 786440 | tf_op jit(solution)/shard_map/ppermute | solution.py:23
  350.3 9.0 %collective-permute-start.3 = (f32[32,1,16,128]{3,2,1,0:T(8,128)}, f32[32,1,16,128]{3,2,1,0:T(8,128)S(1)}, u32[]{:S(2)}, u32[]{:S(2)}) collective-permute-start(f32[32,1,16,128]{3,2,1,0:T(8,128)} %get-tuple-element.76), channel_id=1, source_target_pairs={{1,0},{2,1},{3,2},{4,3},{5,4},{6,5},{7,6},{8,7},{9,8},{10,9},{11,1... | collective-permute-start | bytes 786440 | tf_op jit(solution)/shard_map/ppermute | solution.py:26
where the time goes:
time: 394 us; the launch traced here: 388 us
  blocking collectives  212 us (54%)
  other arithmetic  67.2 us (17%)
  local copies, waits for them, and re-layouts  48.5 us (12%)
  matrix products  45.2 us (11%)
  starting transfers between devices  10.2 us (3%)
    psum x1, blocking collectives, on_device(): lax.psum((local_first, local_second, grad_first, grad_second), ('sample',...  112 us
    psum x1, blocking collectives, on_device(): lax.psum((contract_rows(d_mixed, hidden), kernel_terms), ('sample', 'spac...  99.9 us
    dot_general x40, matrix products, matmul_high(): return jnp.matmul(matrix, operand, precision=highest)  33.2 us
    broadcast_in_dim x1, other arithmetic, on_device(): d_volume[None]  25.1 us
    reduce_sum x2, other arithmetic, on_device(): jnp.sum(d_hidden * tap_cells(padded_x, tap_index, depth_cells).astype(jnp...  11 us
  transfers between devices with their start and end apart: 4, of which 2 were waited for; matrix products, arithmetic and copies ran while one was open for 5% of the time, Pallas kernels for 0%

commit v1 on v0

v1 whole, which is shorter than its diff:
```python
import math

import jax
import jax.numpy as jnp
from jax import lax
from jax.experimental import pallas as pl
from jax.experimental.pallas import tpu as pltpu
from jax.sharding import PartitionSpec as P

NEWTON = 5
EPSILON = 1e-05
C = 32
D = 4
H = 16
W = 128
HW = H * W
PW = (H + 2) * W
ROWS = 24
HIGH = lax.Precision.HIGHEST
F32 = jnp.float32
BF16 = jnp.bfloat16


def dot(a, b, dims=((1,), (0,)), precision=None):
    return lax.dot_general(
        a, b, (dims, ((), ())), precision=precision, preferred_element_type=F32
    )


def dot_high(a, b, dims=((1,), (0,))):
    return dot(a, b, dims, HIGH)


def iota(shape, dim):
    return lax.broadcasted_iota(jnp.int32, shape, dim)


def spread_taps(dk_ref, taps_ref, flip):
    for t in range(27):
        s = 26 - t if flip else t
        taps_ref[t] = jnp.broadcast_to(dk_ref[:, s : s + 1], (C, W))


def stencil(src_ref, taps_ref, dst_ref, planes):
    lane = iota((8, W), 1)
    for group in range(C // 8):
        rows = pl.ds(8 * group, 8)
        taps = [taps_ref[t, rows, :] for t in range(27)]

        def plane(p, carry):
            for h in range(H):
                parts = [None, None, None]
                for a in range(3):
                    for b in range(3):
                        cells = src_ref[p + a, rows, (h + b) * W : (h + b + 1) * W]
                        for e in range(3):
                            term = taps[9 * a + 3 * b + e] * cells
                            parts[e] = term if parts[e] is None else parts[e] + term
                left = jnp.where(lane == 0, 0.0, pltpu.roll(parts[0], 1, 1))
                right = jnp.where(lane == W - 1, 0.0, pltpu.roll(parts[2], W - 1, 1))
                dst_ref[p, rows, h * W : (h + 1) * W] = parts[1] + left + right
            return carry

        lax.fori_loop(0, planes, plane, 0)


def sums_kernel(x_ref, g_ref, lo_ref, hi_ref, dk_ref, w_ref, gm_ref, send_ref,
                xf_ref, xb_ref, hid_ref, taps_ref, right_ref, acc_ref):
    zeros = jnp.zeros((D + 4, C, W), F32)
    xf_ref[:, :, 0:W] = zeros
    xf_ref[:, :, PW - W : PW] = zeros
    xb_ref[:, :, 0:W] = zeros[: D + 2].astype(BF16)
    xb_ref[:, :, PW - W : PW] = zeros[: D + 2].astype(BF16)
    for p in range(D + 4):
        if p < 2:
            cells = lo_ref[:, p]
        elif p < D + 2:
            cells = x_ref[:, p - 2]
        else:
            cells = hi_ref[:, p - D - 2]
        cells = cells.reshape(C, HW)
        xf_ref[p, :, W : W + HW] = cells.astype(F32)
        if 1 <= p <= D + 2:
            xb_ref[p - 1, :, W : W + HW] = cells
    for p in range(D + 2):
        if p == 0:
            cells = lo_ref[:, 2]
        elif p <= D:
            cells = g_ref[:, p - 1]
        else:
            cells = hi_ref[:, 2]
        gm_ref[p, 0:C, :] = cells.reshape(C, HW)
    spread_taps(dk_ref, taps_ref, False)
    stencil(xf_ref, taps_ref, hid_ref, D + 2)

    def mix(p, carry):
        hidden = hid_ref[p].astype(BF16)
        gm_ref[p, C : 2 * C, :] = dot(w_ref[...], hidden).astype(BF16)
        return carry

    lax.fori_loop(0, D + 2, mix, 0)

    lane = iota((1, W), 1)
    row16 = iota((16, W), 0)
    lane16 = iota((16, W), 1)
    keep0 = (lane < W - 1).astype(F32).astype(BF16)
    keep2 = (lane > 0).astype(F32).astype(BF16)
    ones = jnp.where(
        ((row16 == 0) & (lane16 < W - 1)) | (row16 == 1) | ((row16 == 2) & (lane16 > 0)),
        1.0, 0.0,
    ).astype(BF16)
    for h in range(H):
        right_ref[192:208, h * W : (h + 1) * W] = ones
    acc_ref[...] = jnp.zeros(acc_ref.shape, F32)
    first = jnp.where(iota((16, HW), 0) == 0, 1.0, 0.0).astype(BF16)

    def gather(z, carry):
        for h in range(H):
            span = slice(h * W, (h + 1) * W)
            cells = gm_ref[z + 1, :, span]
            right_ref[0:64, span] = pltpu.roll(cells, W - 1, 1) * keep0
            right_ref[64:128, span] = cells
            right_ref[128:192, span] = pltpu.roll(cells, 1, 1) * keep2
        left = [
            xb_ref[z + a, :, b * W : b * W + HW] for a in range(3) for b in range(3)
        ]
        left += [hid_ref[z + 1].astype(BF16), gm_ref[z + 1, C : 2 * C, :], first]
        acc_ref[...] += dot(jnp.concatenate(left, axis=0), right_ref[...], ((1,), (1,)))
        return carry

    lax.fori_loop(0, D, gather, 0)

    def put(row, slab):
        send_ref[pl.ds(row, C, stride=ROWS), :] = slab

    lane = iota((C, W), 1)
    pad = jnp.zeros((C, 48), F32)
    tile1 = [
        jnp.concatenate([acc_ref[C * i : C * (i + 1), 128:208], pad], axis=1)
        for i in range(10)
    ]
    for ab in range(9):
        put(ab, acc_ref[C * ab : C * (ab + 1), 0:128])
    for i in range(4):
        put(9 + i, jnp.where(lane < 64, tile1[i], pltpu.roll(tile1[4 + i], 64, 1)))
    put(13, jnp.where(lane < 64, tile1[8], acc_ref[288:320, 0:128]))
    counts = jnp.broadcast_to(pltpu.roll(acc_ref[352:353, 0:128], 64, 1), (C, W))
    counts = jnp.where(lane < 64, counts, 0.0)
    for ab in range(9):
        own = jnp.where((lane >= 64) & (lane < 67), tile1[ab], 0.0)
        counts = counts + pltpu.roll(own, 3 * ab, 1)
    counts = counts + pltpu.roll(jnp.where(lane == 65, tile1[9], 0.0), 26, 1)
    put(14, counts)
    put(15, jnp.zeros((C, W), F32))
    row = iota((C, W), 0)
    stats = pltpu.roll(acc_ref[320:352, 0:128], 64, 1)
    second = pltpu.roll(stats, 96, 1)
    swapped = jnp.where(lane < 16, pltpu.roll(stats, 112, 1), pltpu.roll(stats, 16, 1))
    mine = (row < 16) == (lane < 16)
    table = jnp.where(lane < C, jnp.where(mine, second, swapped), 0.0)
    packed = table[0:8]
    for q in range(1, 4):
        packed = packed + pltpu.roll(table[8 * q : 8 * q + 8], 32 * q, 1)
    for r in range(8):
        put(16 + r, jnp.broadcast_to(packed[r : r + 1], (C, W)))


def whiten_terms(stats, count):
    gf_row = stats[14:15, 0:C]
    first_row = stats[14:15, C : 2 * C]
    packed = stats[16:24]
    table = jnp.concatenate([pltpu.roll(packed, (W - 32 * q) % W, 1) for q in range(4)], axis=0)
    table = table[:, 0:C]
    row = iota((C, C), 0)
    col = iota((C, C), 1)
    mine = (row < 16) == (col < 16)
    eye = (row == col).astype(F32)
    low = iota((1, C), 1) < 16
    second = jnp.where(mine, table, 0.0)
    other = jnp.concatenate([table[:, 16:32], table[:, 0:16]], axis=1)
    grad_mat = jnp.where(mine, other, 0.0).T

    def column(values):
        return jnp.sum(eye * values, axis=1, keepdims=True)

    def per_group(values):
        left = jnp.sum(jnp.where(low, values, 0.0), axis=1, keepdims=True)
        right = jnp.sum(jnp.where(low, 0.0, values), axis=1, keepdims=True)
        return jnp.where(low, left, right)

    avg = first_row / count
    avg_col = column(avg)
    cov = second / count - jnp.where(mine, avg_col * avg, 0.0) + EPSILON * eye
    trace = per_group(jnp.sum(cov * eye, axis=0, keepdims=True))
    normed = cov / trace
    project = 1.5 * eye - 0.5 * normed
    saved = []
    for step in range(NEWTON - 1):
        both = dot_high(project, jnp.concatenate([project, normed], axis=1))
        square, pn = both[:, 0:C], both[:, C : 2 * C]
        three = dot_high(square, jnp.concatenate([pn, project, normed], axis=1))
        saved.append((
            jnp.concatenate([project, square, three[:, C : 2 * C]], axis=0),
            jnp.concatenate([three[:, 2 * C : 3 * C], pn, normed], axis=0),
        ))
        project = 1.5 * project - 0.5 * three[:, 0:C]
    root = jnp.sqrt(trace)
    whiten = project / root
    offset_col = jnp.sum(whiten * avg, axis=1, keepdims=True)

    d_whiten = grad_mat - jnp.where(mine, column(gf_row) * avg, 0.0)
    d_project = d_whiten / root
    d_normed = jnp.zeros((C, C), F32)
    for powers, tail in reversed(saved):
        delta = -0.5 * d_project
        ahead = dot_high(powers, delta)
        d_normed = d_normed + ahead[2 * C : 3 * C]
        terms = jnp.concatenate([delta, ahead[0:C], ahead[C : 2 * C]], axis=1)
        d_project = 1.5 * d_project + dot_high(terms, tail)
    d_normed = d_normed - 0.5 * d_project
    d_trace = jnp.sum(-0.5 * d_whiten * whiten - d_normed * normed, axis=0, keepdims=True)
    d_trace = per_group(d_trace) / trace
    d_cov = d_normed / trace + d_trace * eye
    both = d_cov + d_cov.T
    d_avg = -(dot_high(gf_row, whiten) + dot_high(avg, both))
    return whiten, offset_col, both / count, d_avg / count, column


def grads_kernel(count, place_ref, pay_ref, gm_ref, dk_ref, w_ref, white_ref, dvol_ref, row_ref,
                 dh_ref, taps_ref, out_ref):
    stats = jnp.sum(pay_ref[...], axis=0)
    whiten, offset_col, symmetric, d_first, column = whiten_terms(stats, count)
    weight = w_ref[...].astype(F32)
    from_g = dot_high(weight, whiten, ((0,), (1,)))
    from_m = dot_high(weight, symmetric, ((0,), (0,)))
    bias = dot_high(d_first, weight)
    bias_col = column(bias)
    hidden_mat = jnp.concatenate([from_g, from_m], axis=1)
    full = jnp.concatenate(
        [hidden_mat, jnp.concatenate([jnp.zeros((C, C), F32), whiten], axis=1)], axis=0
    )
    coarse = full.astype(BF16)
    fine = (full - coarse.astype(F32)).astype(BF16)
    left = jnp.concatenate([coarse, fine], axis=1)

    mine = place_ref[0]
    pick = (iota((C, 1), 0) == mine).astype(F32)
    chosen = jnp.sum(pick * hidden_mat, axis=0, keepdims=True)
    chosen_bias = jnp.sum(pick * bias_col, axis=0, keepdims=True)
    prod = stats[0:16] * jnp.concatenate([chosen, chosen], axis=1)
    lane16 = iota((16, W), 1)
    row16 = iota((16, W), 0)
    low = jnp.sum(jnp.where(lane16 < 64, prod, 0.0), axis=1, keepdims=True)
    high = jnp.sum(jnp.where(lane16 < 64, 0.0, prod), axis=1, keepdims=True)
    to_low = jnp.where(row16 < 9, C + 3 * row16, C + 3 * (row16 - 9) + 2)
    to_low = jnp.where(row16 == 13, C + 26, jnp.where(row16 > 13, -1, to_low))
    to_high = jnp.where(row16 < 9, C + 3 * row16 + 1, C + 3 * (row16 - 5) + 2)
    to_high = jnp.where(row16 > 12, -1, to_high)
    taps_row = jnp.where(lane16 == to_low, low, 0.0) + jnp.where(lane16 == to_high, high, 0.0)
    taps_row = jnp.sum(taps_row, axis=0, keepdims=True)
    lane = iota((1, W), 1)
    ones_row = jnp.where((lane >= 64) & (lane < 91), stats[14:15], 0.0)
    taps_row = taps_row + chosen_bias * pltpu.roll(ones_row, W - 32, 1)
    hidden_sum = jnp.sum(jnp.where(lane == 91, stats[14:15], 0.0), axis=1, keepdims=True)
    pair = pltpu.roll(stats[13:14], 64, 1)[:, 0:64]
    point = dot_high(pair, jnp.concatenate([whiten, symmetric], axis=0)) + hidden_sum * d_first
    point = jnp.concatenate([point, jnp.zeros((1, W - C), F32)], axis=1)
    row = (taps_row + point) * (1.0 / math.sqrt(count))
    row_ref[...] = jnp.broadcast_to(row, (C, W))

    zeros = jnp.zeros((D + 2, C, W), F32)
    dh_ref[:, :, 0:W] = zeros
    dh_ref[:, :, PW - W : PW] = zeros
    inside_lo = place_ref[1].astype(F32)
    inside_hi = place_ref[2].astype(F32)

    for p in range(D + 2):
        cells = gm_ref[p]
        both = dot(left, jnp.concatenate([cells, cells], axis=0))
        d_hidden = both[0:C] + bias_col
        if p == 0:
            d_hidden = d_hidden * inside_lo
        elif p > D:
            d_hidden = d_hidden * inside_hi
        else:
            white = (both[C : 2 * C] - offset_col).astype(BF16)
            white_ref[:, p - 1] = white.reshape(C, H, W)
        dh_ref[p, :, W : W + HW] = d_hidden
    spread_taps(dk_ref, taps_ref, True)
    stencil(dh_ref, taps_ref, out_ref, D)
    for z in range(D):
        dvol_ref[:, z] = out_ref[z].astype(BF16).reshape(C, H, W)


def on_device(volumes, depth_kernel, point_weight, cotangent):
    x = volumes[0]
    g = cotangent[0]
    samples = lax.axis_size("sample")
    slabs = lax.axis_size("space")
    count = float(D * HW * samples * slabs)
    forward = [(i, i + 1) for i in range(slabs - 1)]
    backward = [(i + 1, i) for i in range(slabs - 1)]
    lo = lax.ppermute(jnp.concatenate([x[:, D - 2 :], g[:, D - 1 :]], axis=1), "space", forward)
    hi = lax.ppermute(jnp.concatenate([x[:, :2], g[:, :1]], axis=1), "space", backward)
    gm, send = pl.pallas_call(
        sums_kernel,
        out_shape=(
            jax.ShapeDtypeStruct((D + 2, 2 * C, HW), BF16),
            jax.ShapeDtypeStruct((C * ROWS, W), F32),
        ),
        scratch_shapes=[
            pltpu.VMEM((D + 4, C, PW), F32),
            pltpu.VMEM((D + 2, C, PW), BF16),
            pltpu.VMEM((D + 2, C, HW), F32),
            pltpu.VMEM((27, C, W), F32),
            pltpu.VMEM((208, HW), BF16),
            pltpu.VMEM((368, 208), F32),
        ],
        name="sums",
    )(x, g, lo, hi, depth_kernel, point_weight)
    parts = lax.all_to_all(send.reshape(C, ROWS, W), "sample", 0, 0)
    part = jnp.sum(parts, axis=0)
    pay = lax.all_to_all(jnp.broadcast_to(part, (slabs, ROWS, W)), "space", 0, 0)
    slab = lax.axis_index("space")
    place = jnp.stack([
        lax.axis_index("sample"),
        (slab > 0).astype(jnp.int32),
        (slab < slabs - 1).astype(jnp.int32),
    ])
    vmem = pl.BlockSpec(memory_space=pltpu.VMEM)
    white, d_volume, row = pl.pallas_call(
        lambda *refs: grads_kernel(count, *refs),
        in_specs=[pl.BlockSpec(memory_space=pltpu.SMEM)] + [vmem] * 4,
        out_shape=(
            jax.ShapeDtypeStruct((C, D, H, W), BF16),
            jax.ShapeDtypeStruct((C, D, H, W), BF16),
            jax.ShapeDtypeStruct((C, W), F32),
        ),
        scratch_shapes=[
            pltpu.VMEM((D + 2, C, PW), F32),
            pltpu.VMEM((27, C, W), F32),
            pltpu.VMEM((D, C, HW), F32),
        ],
        name="grads",
    )(place, pay, gm, depth_kernel, point_weight)
    rows = lax.all_to_all(row.reshape(C, 1, W), "sample", 0, 0).reshape(C, W)
    return white[None], d_volume[None], rows[:, 0:C].T, rows[:, C : C + 27]


def solution(mesh):
    split = P("sample", None, "space", None, None)
    return jax.shard_map(
        on_device,
        mesh=mesh,
        in_specs=(split, P(), P(), split),
        out_specs=(split, split, P(), P()),
        check_vma=False,
    )
```

time: 394 us -> 106 us (0.27); the launches traced: 388 us -> 105 us
  blocking collectives: 212 us -> 36 us
  other arithmetic: 67.2 us -> 0.67 us
  matrix products: 45.2 us -> 0 us
  local copies, waits for them, and re-layouts: 48.5 us -> 5.56 us
  Pallas kernels: 0 us -> 22 us
  waiting for transfers between devices: 3.9 us -> 20.2 us
  starting transfers between devices: 10.2 us -> 20.3 us
    psum x2 -> x0, blocking collectives: 212 us -> none  [the longest x1 112 us: on_device(): lax.psum((local_first, local_second, grad_first, grad_second), ('sample',...]
    dot_general x50 -> x0, matrix products: 45.2 us -> none  [the longest x40 33.2 us: matmul_high(): return jnp.matmul(matrix, operand, precision=highest)]
    all_to_all x0 -> x2, blocking collectives: none -> 36 us  [the longest x1 21.7 us: on_device(): parts = lax.all_to_all(send.reshape(C, ROWS, W), 'sample', 0, 0)]
    broadcast_in_dim x1 -> x0, other arithmetic: 25.1 us -> none  [on_device(): d_volume[None]]
    pallas_call x0 -> x2, Pallas kernels: none -> 22 us  [the longest x1 11.3 us: on_device(): pl.pallas_call(sums_kernel, out_shape=(jax.ShapeDtypeStruct((D + 2, 2 * C...]
    reduce_sum x6 -> x1, other arithmetic: 15.6 us -> 0.04 us  [on_device(): part = jnp.sum(parts, axis=0)]
    all_to_all x0 -> x1, starting transfers between devices: none -> 14.6 us  [on_device(): lax.all_to_all(jnp.broadcast_to(part, (slabs, ROWS, W)), 'space', 0, 0)]
    all_to_all x0 -> x1, waiting for transfers between devices: none -> 12.4 us  [on_device(): lax.all_to_all(jnp.broadcast_to(part, (slabs, ROWS, W)), 'space', 0, 0)]
  transfers between devices with their start and end apart: 4 -> 3, of which waited for: 2 -> 3; matrix products, arithmetic and copies ran while one was open for 5% -> 1% of each run, Pallas kernels for 0% -> 0%
where the time goes in v1:
time: 106 us; the launch traced here: 105 us
  blocking collectives  36 us (34%)
  Pallas kernels  22 us (21%)
  starting transfers between devices  20.3 us (19%)
  waiting for transfers between devices  20.2 us (19%)
  local copies, waits for them, and re-layouts  5.56 us (5%)
    all_to_all x1, blocking collectives, on_device(): parts = lax.all_to_all(send.reshape(C, ROWS, W), 'sample', 0, 0)  21.7 us
    all_to_all x1, starting transfers between devices, on_device(): lax.all_to_all(jnp.broadcast_to(part, (slabs, ROWS, W)), 'space', 0, 0)  14.6 us
    all_to_all x1, blocking collectives, on_device(): rows = lax.all_to_all(row.reshape(C, 1, W), 'sample', 0, 0).reshape(C, W)  14.3 us
    all_to_all x1, waiting for transfers between devices, on_device(): lax.all_to_all(jnp.broadcast_to(part, (slabs, ROWS, W)), 'space', 0, 0)  12.4 us
    pallas_call x1, Pallas kernels, on_device(): pl.pallas_call(sums_kernel, out_shape=(jax.ShapeDtypeStruct((D + 2, 2 * C...  11.3 us
    pallas_call x1, Pallas kernels, on_device(): pl.pallas_call(lambda *refs: grads_kernel(count, *refs), in_specs=[pl.Blo...  10.7 us
    ppermute x1, starting transfers between devices, on_device(): lax.ppermute(jnp.concatenate([x[:, D - 2:], g[:, D - 1:]], axis=1), 'spac...  4.38 us
    ppermute x1, waiting for transfers between devices, on_device(): lax.ppermute(jnp.concatenate([x[:, :2], g[:, :1]], axis=1), 'space', back...  4.22 us
  transfers between devices with their start and end apart: 3, of which 3 were waited for; matrix products, arithmetic and copies ran while one was open for 1% of the time, Pallas kernels for 0%

profile of v1, /device:TPU:1, one launch (start us, length us, event | category | flops | bytes accessed | tf_op | source)
XLA Modules:
  0.0 105.4 jit_solution(4683380170077626298)
XLA Ops:
  0.6 1.0 fusion.1
  1.6 1.1 %fusion = (bf16[32,2,16,128]{3,2,1,0:T(8,128)(2,1)S(1)}, bf16[32,2,16,128]{3,2,1,0:T(8,128)(2,1)S(1)}) fusion(bf16[32,4,16,128]{3,2,1,0:T(8,128)(2,1)} %bitcast.14), kind=kLoop, calls=%fused_computation.4 | loop fusion | bytes 1048576 | tf_op jit(solution)/shard_map/slice | solution.py:304
  2.8 4.4 %collective-permute-start = (bf16[32,3,16,128]{3,2,1,0:T(8,128)(2,1)S(1)}, bf16[32,3,16,128]{3,2,1,0:T(8,128)(2,1)S(1)}, u32[]{:S(2)}, u32[]{:S(2)}) collective-permute-start(bf16[32,3,16,128]{3,2,1,0:T(8,128)(2,1)S(1)} %pad_maximum_fusion), channel_id=1, source_target_pairs={{0,1},{1,2},{2,3},{3,4},{4,5},{5,6},{6,7},{7,8},{8,9},{9,10},{10,1... | collective-permute-start | bytes 1179656 | tf_op jit(solution)/shard_map/ppermute | solution.py:303
  7.2 1.3 %collective-permute-start.1 = (bf16[32,3,16,128]{3,2,1,0:T(8,128)(2,1)S(1)}, bf16[32,3,16,128]{3,2,1,0:T(8,128)(2,1)S(1)}, u32[]{:S(2)}, u32[]{:S(2)}) collective-permute-start(bf16[32,3,16,128]{3,2,1,0:T(8,128)(2,1)S(1)} %pad_maximum_fusion.1), channel_id=1, source_target_pairs={{1,0},{2,1},{3,2},{4,3},{5,4},{6,5},{7,6},{8,7},{9,8},{10,9},{11,1... | collective-permute-start | bytes 1179656 | tf_op jit(solution)/shard_map/ppermute | solution.py:304
  8.5 3.6 %collective-permute-done.lo_ref = bf16[32,3,16,128]{3,2,1,0:T(8,128)(2,1)S(1)} collective-permute-done((bf16[32,3,16,128]{3,2,1,0:T(8,128)(2,1)S(1)}, bf16[32,3,16,128]{3,2,1,0:T(8,128)(2,1)S(1)}, u32[]{:S(2)}, u32[]{:S(2)}) %collective-permute-start) | collective-permute-done | bytes 393248 | tf_op jit(solution)/shard_map/ppermute | solution.py:303
  12.1 0.0 copy-start.1
  12.1 4.2 %collective-permute-done.1.hi_ref = bf16[32,3,16,128]{3,2,1,0:T(8,128)(2,1)S(1)} collective-permute-done((bf16[32,3,16,128]{3,2,1,0:T(8,128)(2,1)S(1)}, bf16[32,3,16,128]{3,2,1,0:T(8,128)(2,1)S(1)}, u32[]{:S(2)}, u32[]{:S(2)}) %collective-permute-start.1) | collective-permute-done | bytes 393248 | tf_op jit(solution)/shard_map/ppermute | solution.py:304
  16.3 0.0 copy-done.1
  16.3 0.0 copy-start.2
  16.3 0.7 copy-done.2
  17.1 11.3 %sums.1 = (bf16[6,64,2048]{2,1,0:T(8,128)(2,1)}, f32[768,128]{1,0:T(8,128)}) custom-call(bf16[32,4,16,128]{3,2,1,0:T(8,128)(2,1)} %bitcast.15, bf16[32,4,16,128]{3,2,1,0:T(8,128)(2,1)} %bitcast.17, bf16[32,3,16,128]{3,2,1,0:T(8,128)(2,1)} %copy-done.1, bf16[32,3,16,128]{3,2,1,0:T(8,128)(2,1)} %copy-done.2, f32[32,27]{1,0:T(8,128)} %refs_3_.1, ...), custom_call_target="tpu_custom_call" | custom-call | tf_op jit(solution)/shard_map/sums/pallas_call | solution.py:305
  28.4 21.7 %all_to_all.15 = f32[32,24,128]{2,1,0:T(8,128)S(1)} all-to-all(f32[32,24,128]{2,1,0:T(8,128)} %bitcast.18), channel_id=1, replica_groups=mesh['sample'=32,'space'=16] {'sample'}, dimensions={0} | all-to-all | bytes 786432 | tf_op jit(solution)/shard_map/all_to_all | solution.py:321
  50.1 0.7 broadcast_in_dim.9
  50.8 14.6 %all-to-all-start.1 = ((f32[16,24,128]{2,1,0:T(8,128)}), f32[16,24,128]{2,1,0:T(8,128)S(1)}, u32[]{:S(2)}, u32[]{:S(2)}) async-start(f32[16,24,128]{2,1,0:T(8,128)} %broadcast_in_dim.9), calls=%async_computation.1 | async-start | bytes 393216 | tf_op jit(solution)/shard_map/all_to_all | solution.py:323
  65.4 0.6 pad_add_fusion.refs_0_
  66.0 12.4 %all-to-all-done.1.refs_1_ = f32[16,24,128]{2,1,0:T(8,128)S(1)} async-done(((f32[16,24,128]{2,1,0:T(8,128)}), f32[16,24,128]{2,1,0:T(8,128)S(1)}, u32[]{:S(2)}, u32[]{:S(2)}) %all-to-all-start.1) | async-done | bytes 196640 | tf_op jit(solution)/shard_map/all_to_all | solution.py:323
  78.4 0.0 copy-start
  78.4 0.7 copy-done
  79.1 10.7 %grads.1 = (bf16[32,4,16,128]{3,2,1,0:T(8,128)(2,1)}, bf16[32,4,16,128]{3,2,1,0:T(8,128)(2,1)}, f32[32,128]{1,0:T(8,128)}) custom-call(s32[3]{0:T(128)} %pad_add_fusion.refs_0_, f32[16,24,128]{2,1,0:T(8,128)} %copy-done, bf16[6,64,2048]{2,1,0:T(8,128)(2,1)} %get-tuple-element.10.refs_2_, f32[32,27]{1,0:T(8,128)} %refs_3_.1, bf16[32,32]{1,0:T(8,128)(2,1)} %refs_4_.1), custom_call_target="tpu_custom_call" | custom-call | tf_op jit(solution)/shard_map/grads/pallas_call | solution.py:331
  89.8 14.3 %all_to_all.16 = f32[32,1,128]{2,1,0:T(1,128)S(1)} all-to-all(f32[32,1,128]{2,1,0:T(1,128)} %bitcast.21), channel_id=1, replica_groups=mesh['sample'=32,'space'=16] {'sample'}, dimensions={0} | all-to-all | bytes 32768 | tf_op jit(solution)/shard_map/all_to_all | solution.py:346
  104.1 0.7 slice.29
  104.7 0.7 copy.10
  (4 shorter events, 0.1 us)
Async XLA Ops:
  2.8 9.3 %collective-permute-start = (bf16[32,3,16,128]{3,2,1,0:T(8,128)(2,1)S(1)}, bf16[32,3,16,128]{3,2,1,0:T(8,128)(2,1)S(1)}, u32[]{:S(2)}, u32[]{:S(2)}) collective-permute-start(bf16[32,3,16,128]{3,2,1,0:T(8,128)(2,1)S(1)} %pad_maximum_fusion), channel_id=1, source_target_pairs={{0,1},{1,2},{2,3},{3,4},{4,5},{5,6},{6,7},{7,8},{8,9},{9,10},{10,1... | collective-permute-start | bytes 1179656 | tf_op jit(solution)/shard_map/ppermute | solution.py:303
  7.2 9.1 %collective-permute-start.1 = (bf16[32,3,16,128]{3,2,1,0:T(8,128)(2,1)S(1)}, bf16[32,3,16,128]{3,2,1,0:T(8,128)(2,1)S(1)}, u32[]{:S(2)}, u32[]{:S(2)}) collective-permute-start(bf16[32,3,16,128]{3,2,1,0:T(8,128)(2,1)S(1)} %pad_maximum_fusion.1), channel_id=1, source_target_pairs={{1,0},{2,1},{3,2},{4,3},{5,4},{6,5},{7,6},{8,7},{9,8},{10,9},{11,1... | collective-permute-start | bytes 1179656 | tf_op jit(solution)/shard_map/ppermute | solution.py:304
  12.1 4.2 %copy-start.1 = (bf16[32,3,16,128]{3,2,1,0:T(8,128)(2,1)}, bf16[32,3,16,128]{3,2,1,0:T(8,128)(2,1)S(1)}, u32[]{:S(2)}) copy-start(bf16[32,3,16,128]{3,2,1,0:T(8,128)(2,1)S(1)} %collective-permute-done.lo_ref) | copy-start | bytes 1179652
  16.3 0.7 copy-start.2
  50.8 27.6 %all-to-all-start.1 = ((f32[16,24,128]{2,1,0:T(8,128)}), f32[16,24,128]{2,1,0:T(8,128)S(1)}, u32[]{:S(2)}, u32[]{:S(2)}) async-start(f32[16,24,128]{2,1,0:T(8,128)} %broadcast_in_dim.9), calls=%async_computation.1 | async-start | bytes 393216 | tf_op jit(solution)/shard_map/all_to_all | solution.py:323
  78.4 0.7 copy-start

commit v2 on v1

--- a/solution.py
+++ b/solution.py
@@ -6,6 +6,7 @@
 from jax.experimental import pallas as pl
 from jax.experimental.pallas import tpu as pltpu
 from jax.sharding import PartitionSpec as P
+
 
 NEWTON = 5
 EPSILON = 1e-05
@@ -41,7 +42,7 @@
         taps_ref[t] = jnp.broadcast_to(dk_ref[:, s : s + 1], (C, W))
 
 
-def stencil(src_ref, taps_ref, dst_ref, planes):
+def stencil(src_ref, taps_ref, dst_ref, planes, step=1):
     lane = iota((8, W), 1)
     for group in range(C // 8):
         rows = pl.ds(8 * group, 8)
@@ -52,7 +53,7 @@
                 parts = [None, None, None]
                 for a in range(3):
                     for b in range(3):
-                        cells = src_ref[p + a, rows, (h + b) * W : (h + b + 1) * W]
+                        cells = src_ref[step * p + a, rows, (h + b) * W : (h + b + 1) * W]
                         for e in range(3):
                             term = taps[9 * a + 3 * b + e] * cells
                             parts[e] = term if parts[e] is None else parts[e] + term
@@ -64,41 +65,19 @@
         lax.fori_loop(0, planes, plane, 0)
 
 
-def sums_kernel(x_ref, g_ref, lo_ref, hi_ref, dk_ref, w_ref, gm_ref, send_ref,
-                xf_ref, xb_ref, hid_ref, taps_ref, right_ref, acc_ref):
-    zeros = jnp.zeros((D + 4, C, W), F32)
+def slab_sums(xs, gs, step, dk_ref, w_ref, gm_refs, acc_ref,
+              xf_ref, xb_ref, hid_ref, taps_ref, right_ref):
+    zeros = jnp.zeros((len(xs), C, W), F32)
     xf_ref[:, :, 0:W] = zeros
     xf_ref[:, :, PW - W : PW] = zeros
-    xb_ref[:, :, 0:W] = zeros[: D + 2].astype(BF16)
-    xb_ref[:, :, PW - W : PW] = zeros[: D + 2].astype(BF16)
-    for p in range(D + 4):
-        if p < 2:
-            cells = lo_ref[:, p]
-        elif p < D + 2:
-            cells = x_ref[:, p - 2]
-        else:
-            cells = hi_ref[:, p - D - 2]
-        cells = cells.reshape(C, HW)
+    xb_ref[:, :, 0:W] = zeros.astype(BF16)
+    xb_ref[:, :, PW - W : PW] = zeros.astype(BF16)
+    for p, cells in enumerate(xs):
+        cells = cells().reshape(C, HW)
         xf_ref[p, :, W : W + HW] = cells.astype(F32)
-        if 1 <= p <= D + 2:
-            xb_ref[p - 1, :, W : W + HW] = cells
-    for p in range(D + 2):
-        if p == 0:
-            cells = lo_ref[:, 2]
-        elif p <= D:
-            cells = g_ref[:, p - 1]
-        else:
-            cells = hi_ref[:, 2]
-        gm_ref[p, 0:C, :] = cells.reshape(C, HW)
+        xb_ref[p, :, W : W + HW] = cells
     spread_taps(dk_ref, taps_ref, False)
-    stencil(xf_ref, taps_ref, hid_ref, D + 2)
-
-    def mix(p, carry):
-        hidden = hid_ref[p].astype(BF16)
-        gm_ref[p, C : 2 * C, :] = dot(w_ref[...], hidden).astype(BF16)
-        return carry
-
-    lax.fori_loop(0, D + 2, mix, 0)
+    stencil(xf_ref, taps_ref, hid_ref, 2, step)
 
     lane = iota((1, W), 1)
     row16 = iota((16, W), 0)
@@ -111,34 +90,47 @@
     ).astype(BF16)
     for h in range(H):
         right_ref[192:208, h * W : (h + 1) * W] = ones
-    acc_ref[...] = jnp.zeros(acc_ref.shape, F32)
     first = jnp.where(iota((16, HW), 0) == 0, 1.0, 0.0).astype(BF16)
-
-    def gather(z, carry):
+    for i in range(2):
+        hidden = hid_ref[i].astype(BF16)
+        mixed = dot(w_ref[...], hidden).astype(BF16)
+        gm_refs[i][0:C, :] = gs[i]().reshape(C, HW)
+        gm_refs[i][C : 2 * C, :] = mixed
         for h in range(H):
             span = slice(h * W, (h + 1) * W)
-            cells = gm_ref[z + 1, :, span]
+            cells = gm_refs[i][:, span]
             right_ref[0:64, span] = pltpu.roll(cells, W - 1, 1) * keep0
             right_ref[64:128, span] = cells
             right_ref[128:192, span] = pltpu.roll(cells, 1, 1) * keep2
         left = [
-            xb_ref[z + a, :, b * W : b * W + HW] for a in range(3) for b in range(3)
+            xb_ref[step * i + a, :, b * W : b * W + HW] for a in range(3) for b in range(3)
         ]
-        left += [hid_ref[z + 1].astype(BF16), gm_ref[z + 1, C : 2 * C, :], first]
-        acc_ref[...] += dot(jnp.concatenate(left, axis=0), right_ref[...], ((1,), (1,)))
-        return carry
-
-    lax.fori_loop(0, D, gather, 0)
+        left += [hidden, mixed, first]
+        acc_ref[:, 0:208] += dot(
+            jnp.concatenate(left, axis=0), right_ref[...], ((1,), (1,))
+        )
+
+
+def inner_kernel(x_ref, g_ref, dk_ref, w_ref, gm_ref, acc_ref, *scratch):
+    acc_ref[...] = jnp.zeros(acc_ref.shape, F32)
+    xs = [lambda p=p: x_ref[:, p] for p in range(D)]
+    gs = [lambda p=p: g_ref[:, p] for p in (1, 2)]
+    slab_sums(xs, gs, 1, dk_ref, w_ref, (gm_ref.at[0], gm_ref.at[1]), acc_ref, *scratch)
+
+
+def outer_kernel(x_ref, g_ref, lo_ref, hi_ref, dk_ref, w_ref, part_ref,
+                 gm_lo_ref, gm_hi_ref, send_ref, acc_ref, *scratch):
+    acc_ref[...] = part_ref[...]
+    xs = [lambda: lo_ref[:, 0]] + [lambda p=p: x_ref[:, p] for p in range(D)]
+    xs += [lambda: hi_ref[:, 0]]
+    gs = [lambda p=p: g_ref[:, p] for p in (0, 3)]
+    slab_sums(xs, gs, 3, dk_ref, w_ref, (gm_lo_ref, gm_hi_ref), acc_ref, *scratch)
 
     def put(row, slab):
         send_ref[pl.ds(row, C, stride=ROWS), :] = slab
 
     lane = iota((C, W), 1)
-    pad = jnp.zeros((C, 48), F32)
-    tile1 = [
-        jnp.concatenate([acc_ref[C * i : C * (i + 1), 128:208], pad], axis=1)
-        for i in range(10)
-    ]
+    tile1 = [acc_ref[C * i : C * (i + 1), 128:256] for i in range(10)]
     for ab in range(9):
         put(ab, acc_ref[C * ab : C * (ab + 1), 0:128])
     for i in range(4):
@@ -195,7 +187,7 @@
     normed = cov / trace
     project = 1.5 * eye - 0.5 * normed
     saved = []
-    for step in range(NEWTON - 1):
+    for _ in range(NEWTON - 1):
         both = dot_high(project, jnp.concatenate([project, normed], axis=1))
         square, pn = both[:, 0:C], both[:, C : 2 * C]
         three = dot_high(square, jnp.concatenate([pn, project, normed], axis=1))
@@ -226,22 +218,22 @@
     return whiten, offset_col, both / count, d_avg / count, column
 
 
-def grads_kernel(count, place_ref, pay_ref, gm_ref, dk_ref, w_ref, white_ref, dvol_ref, row_ref,
-                 dh_ref, taps_ref, out_ref):
+def terms_kernel(count, place_ref, pay_ref, w_ref, left_ref, shift_ref, row_ref):
     stats = jnp.sum(pay_ref[...], axis=0)
     whiten, offset_col, symmetric, d_first, column = whiten_terms(stats, count)
     weight = w_ref[...].astype(F32)
     from_g = dot_high(weight, whiten, ((0,), (1,)))
     from_m = dot_high(weight, symmetric, ((0,), (0,)))
-    bias = dot_high(d_first, weight)
-    bias_col = column(bias)
+    bias_col = column(dot_high(d_first, weight))
     hidden_mat = jnp.concatenate([from_g, from_m], axis=1)
     full = jnp.concatenate(
         [hidden_mat, jnp.concatenate([jnp.zeros((C, C), F32), whiten], axis=1)], axis=0
     )
     coarse = full.astype(BF16)
     fine = (full - coarse.astype(F32)).astype(BF16)
-    left = jnp.concatenate([coarse, fine], axis=1)
+    left_ref[...] = jnp.concatenate([coarse, fine], axis=1)
+    shift_ref[0:C] = jnp.broadcast_to(bias_col, (C, W))
+    shift_ref[C : 2 * C] = jnp.broadcast_to(-offset_col, (C, W))
 
     mine = place_ref[0]
     pick = (iota((C, 1), 0) == mine).astype(F32)
@@ -268,22 +260,28 @@
     row = (taps_row + point) * (1.0 / math.sqrt(count))
     row_ref[...] = jnp.broadcast_to(row, (C, W))
 
+
+def grads_kernel(place_ref, left_ref, shift_ref, lo_ref, first_ref, inner_ref, last_ref, hi_ref,
+                 dk_ref, white_ref, dvol_ref, dh_ref, taps_ref, out_ref):
     zeros = jnp.zeros((D + 2, C, W), F32)
     dh_ref[:, :, 0:W] = zeros
     dh_ref[:, :, PW - W : PW] = zeros
     inside_lo = place_ref[1].astype(F32)
     inside_hi = place_ref[2].astype(F32)
-
+    left = left_ref[...]
+    bias = shift_ref[0:C, 0:1]
+    minus_offset = shift_ref[C : 2 * C, 0:1]
+    planes = [lo_ref, first_ref, inner_ref.at[0], inner_ref.at[1], last_ref, hi_ref]
     for p in range(D + 2):
-        cells = gm_ref[p]
+        cells = planes[p][...]
         both = dot(left, jnp.concatenate([cells, cells], axis=0))
-        d_hidden = both[0:C] + bias_col
+        d_hidden = both[0:C] + bias
         if p == 0:
             d_hidden = d_hidden * inside_lo
         elif p > D:
             d_hidden = d_hidden * inside_hi
         else:
-            white = (both[C : 2 * C] - offset_col).astype(BF16)
+            white = (both[C : 2 * C] + minus_offset).astype(BF16)
             white_ref[:, p - 1] = white.reshape(C, H, W)
         dh_ref[p, :, W : W + HW] = d_hidden
     spread_taps(dk_ref, taps_ref, True)
@@ -292,7 +290,11 @@
         dvol_ref[:, z] = out_ref[z].astype(BF16).reshape(C, H, W)
 
 
-def on_device(volumes, depth_kernel, point_weight, cotangent):
+def cost(us):
+    return pl.CostEstimate(flops=int(us * 1e8), bytes_accessed=int(us * 1e6), transcendentals=0)
+
+
+def whole_step(volumes, depth_kernel, point_weight, cotangent):
     x = volumes[0]
     g = cotangent[0]
     samples = lax.axis_size("sample")
@@ -300,24 +302,39 @@
     count = float(D * HW * samples * slabs)
     forward = [(i, i + 1) for i in range(slabs - 1)]
     backward = [(i + 1, i) for i in range(slabs - 1)]
-    lo = lax.ppermute(jnp.concatenate([x[:, D - 2 :], g[:, D - 1 :]], axis=1), "space", forward)
-    hi = lax.ppermute(jnp.concatenate([x[:, :2], g[:, :1]], axis=1), "space", backward)
-    gm, send = pl.pallas_call(
-        sums_kernel,
+    scratch = lambda planes: [
+        pltpu.VMEM((planes, C, PW), F32),
+        pltpu.VMEM((planes, C, PW), BF16),
+        pltpu.VMEM((2, C, HW), F32),
+        pltpu.VMEM((27, C, W), F32),
+        pltpu.VMEM((208, HW), BF16),
+    ]
+    vmem = pl.BlockSpec(memory_space=pltpu.VMEM)
+    smem = pl.BlockSpec(memory_space=pltpu.SMEM)
+    shape = jax.ShapeDtypeStruct
+
+    x_lo = lax.ppermute(x[:, D - 1 :], "space", forward)
+    x_hi = lax.ppermute(x[:, :1], "space", backward)
+    gm_inner, acc = pl.pallas_call(
+        inner_kernel,
+        out_shape=(shape((2, 2 * C, HW), BF16), shape((368, 256), F32)),
+        scratch_shapes=scratch(D),
+        cost_estimate=cost(6),
+        name="inner",
+    )(x, g, depth_kernel, point_weight)
+    gm_first, gm_last, send = pl.pallas_call(
+        outer_kernel,
         out_shape=(
-            jax.ShapeDtypeStruct((D + 2, 2 * C, HW), BF16),
-            jax.ShapeDtypeStruct((C * ROWS, W), F32),
+            shape((2 * C, HW), BF16),
+            shape((2 * C, HW), BF16),
+            shape((C * ROWS, W), F32),
         ),
-        scratch_shapes=[
-            pltpu.VMEM((D + 4, C, PW), F32),
-            pltpu.VMEM((D + 2, C, PW), BF16),
-            pltpu.VMEM((D + 2, C, HW), F32),
-            pltpu.VMEM((27, C, W), F32),
-            pltpu.VMEM((208, HW), BF16),
-            pltpu.VMEM((368, 208), F32),
-        ],
-        name="sums",
-    )(x, g, lo, hi, depth_kernel, point_weight)
+        scratch_shapes=[pltpu.VMEM((368, 256), F32)] + scratch(D + 2),
+        cost_estimate=cost(6),
+        name="outer",
+    )(x, g, x_lo, x_hi, depth_kernel, point_weight, acc)
+    gm_lo = lax.ppermute(gm_last, "space", forward)
+    gm_hi = lax.ppermute(gm_first, "space", backward)
     parts = lax.all_to_all(send.reshape(C, ROWS, W), "sample", 0, 0)
     part = jnp.sum(parts, axis=0)
     pay = lax.all_to_all(jnp.broadcast_to(part, (slabs, ROWS, W)), "space", 0, 0)
@@ -327,30 +344,33 @@
         (slab > 0).astype(jnp.int32),
         (slab < slabs - 1).astype(jnp.int32),
     ])
-    vmem = pl.BlockSpec(memory_space=pltpu.VMEM)
-    white, d_volume, row = pl.pallas_call(
-        lambda *refs: grads_kernel(count, *refs),
-        in_specs=[pl.BlockSpec(memory_space=pltpu.SMEM)] + [vmem] * 4,
-        out_shape=(
-            jax.ShapeDtypeStruct((C, D, H, W), BF16),
-            jax.ShapeDtypeStruct((C, D, H, W), BF16),
-            jax.ShapeDtypeStruct((C, W), F32),
-        ),
+    left, shift, row = pl.pallas_call(
+        lambda *refs: terms_kernel(count, *refs),
+        in_specs=[smem] + [vmem] * 2,
+        out_shape=(shape((2 * C, 4 * C), BF16), shape((2 * C, W), F32), shape((C, W), F32)),
+        cost_estimate=cost(4),
+        name="terms",
+    )(place, pay, point_weight)
+    rows = lax.all_to_all(row.reshape(C, 1, W), "sample", 0, 0).reshape(C, W)
+    white, d_volume = pl.pallas_call(
+        grads_kernel,
+        in_specs=[smem] + [vmem] * 8,
+        out_shape=(shape((C, D, H, W), BF16), shape((C, D, H, W), BF16)),
         scratch_shapes=[
             pltpu.VMEM((D + 2, C, PW), F32),
             pltpu.VMEM((27, C, W), F32),
             pltpu.VMEM((D, C, HW), F32),
         ],
+        cost_estimate=cost(8),
         name="grads",
-    )(place, pay, gm, depth_kernel, point_weight)
-    rows = lax.all_to_all(row.reshape(C, 1, W), "sample", 0, 0).reshape(C, W)
+    )(place, left, shift, gm_lo, gm_first, gm_inner, gm_last, gm_hi, depth_kernel)
     return white[None], d_volume[None], rows[:, 0:C].T, rows[:, C : C + 27]
 
 
 def solution(mesh):
     split = P("sample", None, "space", None, None)
     return jax.shard_map(
-        on_device,
+        whole_step,
         mesh=mesh,
         in_specs=(split, P(), P(), split),
         out_specs=(split, split, P(), P()),

time: 106 us -> 93.8 us (0.88)
  blocking collectives: 36 us -> 18.7 us
  starting transfers between devices: 20.3 us -> 36 us
  waiting for transfers between devices: 20.2 us -> 7.74 us
  Pallas kernels: 22 us -> 24.1 us
    all_to_all x2 -> x1, blocking collectives: 36 us -> 18.7 us  [whole_step(): parts = lax.all_to_all(send.reshape(C, ROWS, W), 'sample', 0, 0)]
    all_to_all x1 -> x2, starting transfers between devices: 14.6 us -> 25.8 us  [the longest x1 16.3 us: whole_step(): lax.all_to_all(jnp.broadcast_to(part, (slabs, ROWS, W)), 'space', 0, 0)]
    ppermute x2 -> x4, waiting for transfers between devices: 7.82 us -> 0.01 us  [the longest x1 0.01 us: whole_step(): x_lo = lax.ppermute(x[:, D - 1:], 'space', forward)]
    all_to_all x1 -> x2, waiting for transfers between devices: 12.4 us -> 7.73 us  [the longest x1 7.72 us: whole_step(): lax.all_to_all(jnp.broadcast_to(part, (slabs, ROWS, W)), 'space', 0, 0)]
    ppermute x2 -> x4, starting transfers between devices: 5.68 us -> 10.2 us  [the longest x1 4.37 us: whole_step(): x_lo = lax.ppermute(x[:, D - 1:], 'space', forward)]
    pallas_call x2 -> x4, Pallas kernels: 22 us -> 24.1 us  [the longest x1 6.76 us: whole_step(): pl.pallas_call(outer_kernel, out_shape=(shape((2 * C, HW), BF16), shape((...]
    slice x3 -> x2, local copies, waits for them, and re-layouts: 2.75 us -> 1.68 us  [the longest x1 1 us: whole_step(): x_hi = lax.ppermute(x[:, :1], 'space', backward)]
    unnamed x7 -> x15, local copies, waits for them, and re-layouts: 2.12 us -> 2.86 us
  transfers between devices with their start and end apart: 3 -> 6, of which waited for: 3 -> 1; matrix products, arithmetic and copies ran while one was open for 1% -> 1% of each run, Pallas kernels for 0% -> 19%
where the time goes in v2:
time: 93.8 us; the launch traced here: 93.3 us
  starting transfers between devices  36 us (38%)
  Pallas kernels  24.1 us (26%)
  blocking collectives  18.7 us (20%)
  waiting for transfers between devices  7.74 us (8%)
  local copies, waits for them, and re-layouts  5.23 us (6%)
    all_to_all x1, blocking collectives, whole_step(): parts = lax.all_to_all(send.reshape(C, ROWS, W), 'sample', 0, 0)  18.7 us
    all_to_all x1, starting transfers between devices, whole_step(): lax.all_to_all(jnp.broadcast_to(part, (slabs, ROWS, W)), 'space', 0, 0)  16.3 us
    all_to_all x1, starting transfers between devices, whole_step(): rows = lax.all_to_all(row.reshape(C, 1, W), 'sample', 0, 0).reshape(C, W)  9.47 us
    all_to_all x1, waiting for transfers between devices, whole_step(): lax.all_to_all(jnp.broadcast_to(part, (slabs, ROWS, W)), 'space', 0, 0)  7.72 us
    pallas_call x1, Pallas kernels, whole_step(): pl.pallas_call(outer_kernel, out_shape=(shape((2 * C, HW), BF16), shape((...  6.76 us
    pallas_call x1, Pallas kernels, whole_step(): pl.pallas_call(grads_kernel, in_specs=[smem] + [vmem] * 8, out_shape=(sha...  6.26 us
    pallas_call x1, Pallas kernels, whole_step(): pl.pallas_call(lambda *refs: terms_kernel(count, *refs), in_specs=[smem]...  5.96 us
    pallas_call x1, Pallas kernels, whole_step(): pl.pallas_call(inner_kernel, out_shape=(shape((2, 2 * C, HW), BF16), shap...  5.14 us
  transfers between devices with their start and end apart: 6, of which 1 were waited for; matrix products, arithmetic and copies ran while one was open for 1% of the time, Pallas kernels for 19%

profile of v2, /device:TPU:1, one launch (start us, length us, event | category | flops | bytes accessed | tf_op | source)
XLA Modules:
  0.0 93.3 jit_solution(17061939478992308959)
XLA Ops:
  0.6 1.0 %fusion = (bf16[32,1,16,128]{3,2,1,0:T(8,128)(2,1)S(1)}, bf16[32,1,16,128]{3,2,1,0:T(8,128)(2,1)S(1)}) fusion(bf16[32,4,16,128]{3,2,1,0:T(8,128)(2,1)} %bitcast.17), kind=kLoop, calls=%fused_computation.2 | loop fusion | bytes 524288 | tf_op jit(solution)/shard_map/slice | solution.py:317
  1.6 4.4 %collective-permute-start = (bf16[32,1,16,128]{3,2,1,0:T(8,128)(2,1)S(1)}, bf16[32,1,16,128]{3,2,1,0:T(8,128)(2,1)S(1)}, u32[]{:S(2)}, u32[]{:S(2)}) collective-permute-start(bf16[32,1,16,128]{3,2,1,0:T(8,128)(2,1)S(1)} %get-tuple-element.33), channel_id=1, source_target_pairs={{0,1},{1,2},{2,3},{3,4},{4,5},{5,6},{6,7},{7,8},{8,9},{9,10},{10,1... | collective-permute-start | bytes 393224 | tf_op jit(solution)/shard_map/ppermute | solution.py:316
  6.0 1.3 %collective-permute-start.1 = (bf16[32,1,16,128]{3,2,1,0:T(8,128)(2,1)S(1)}, bf16[32,1,16,128]{3,2,1,0:T(8,128)(2,1)S(1)}, u32[]{:S(2)}, u32[]{:S(2)}) collective-permute-start(bf16[32,1,16,128]{3,2,1,0:T(8,128)(2,1)S(1)} %get-tuple-element.32), channel_id=1, source_target_pairs={{1,0},{2,1},{3,2},{4,3},{5,4},{6,5},{7,6},{8,7},{9,8},{10,9},{11,1... | collective-permute-start | bytes 393224 | tf_op jit(solution)/shard_map/ppermute | solution.py:317
  7.3 5.1 %inner.1 = (bf16[2,64,2048]{2,1,0:T(8,128)(2,1)}, f32[368,256]{1,0:T(8,128)}) custom-call(bf16[32,4,16,128]{3,2,1,0:T(8,128)(2,1)} %bitcast.18, bf16[32,4,16,128]{3,2,1,0:T(8,128)(2,1)} %bitcast.21, f32[32,27]{1,0:T(8,128)} %dk_ref.5, bf16[32,32]{1,0:T(8,128)(2,1)} %refs_2_.1), custom_call_target="tpu_custom_call" | custom-call | flops 600000000 | bytes 6000000 | tf_op jit(solution)/shard_map/inner/pallas_call | solution.py:318
  12.4 0.0 collective-permute-done.lo_ref
  12.5 0.0 copy-start.5
  12.5 0.0 collective-permute-done.1.hi_ref
  12.5 0.0 copy-start.6
  12.5 0.6 copy-done.5
  13.1 0.1 copy-done.6
  13.2 6.8 %outer.1 = (bf16[64,2048]{1,0:T(8,128)(2,1)}, bf16[64,2048]{1,0:T(8,128)(2,1)}, f32[768,128]{1,0:T(8,128)}) custom-call(bf16[32,4,16,128]{3,2,1,0:T(8,128)(2,1)} %bitcast.19, bf16[32,4,16,128]{3,2,1,0:T(8,128)(2,1)} %bitcast.22, bf16[32,1,16,128]{3,2,1,0:T(8,128)(2,1)} %copy-done.5, bf16[32,1,16,128]{3,2,1,0:T(8,128)(2,1)} %copy-done.6, f32[32,27]{1,0:T(8,128)} %dk_ref.5, ...), custom_call_target="tpu_custom_call" | custom-call | flops 600000000 | bytes 6000000 | tf_op jit(solution)/shard_map/outer/pallas_call | solution.py:325
  19.9 18.7 %all_to_all.15 = f32[32,24,128]{2,1,0:T(8,128)S(1)} all-to-all(f32[32,24,128]{2,1,0:T(8,128)} %bitcast.14), channel_id=1, replica_groups=mesh['sample'=32,'space'=16] {'sample'}, dimensions={0} | all-to-all | bytes 786432 | tf_op jit(solution)/shard_map/all_to_all | solution.py:338
  38.7 0.0 copy-start.2
  38.7 0.0 copy-start.1
  38.7 0.7 broadcast_in_dim.9
  39.4 16.3 %all-to-all-start.1 = ((f32[16,24,128]{2,1,0:T(8,128)}), f32[16,24,128]{2,1,0:T(8,128)S(1)}, u32[]{:S(2)}, u32[]{:S(2)}) async-start(f32[16,24,128]{2,1,0:T(8,128)} %broadcast_in_dim.9), calls=%async_computation.1 | async-start | bytes 393216 | tf_op jit(solution)/shard_map/all_to_all | solution.py:340
  55.7 0.0 copy-done.2
  55.7 3.3 %collective-permute-start.2 = (bf16[64,2048]{1,0:T(8,128)(2,1)S(1)}, bf16[64,2048]{1,0:T(8,128)(2,1)S(1)}, u32[]{:S(2)}, u32[]{:S(2)}) collective-permute-start(bf16[64,2048]{1,0:T(8,128)(2,1)S(1)} %copy-done.2), channel_id=1, source_target_pairs={{0,1},{1,2},{2,3},{3,4},{4,5},{5,6},{6,7},{7,8},{8,9},{9,10},{10,1... | collective-permute-start | bytes 786440 | tf_op jit(solution)/shard_map/ppermute | solution.py:336
  59.0 0.0 copy-done.1
  59.0 1.3 %collective-permute-start.3 = (bf16[64,2048]{1,0:T(8,128)(2,1)S(1)}, bf16[64,2048]{1,0:T(8,128)(2,1)S(1)}, u32[]{:S(2)}, u32[]{:S(2)}) collective-permute-start(bf16[64,2048]{1,0:T(8,128)(2,1)S(1)} %copy-done.1), channel_id=1, source_target_pairs={{1,0},{2,1},{3,2},{4,3},{5,4},{6,5},{7,6},{8,7},{9,8},{10,9},{11,1... | collective-permute-start | bytes 786440 | tf_op jit(solution)/shard_map/ppermute | solution.py:337
  60.3 0.7 pad_add_fusion.refs_0_.place_ref
  61.0 7.7 %all-to-all-done.1.refs_1_ = f32[16,24,128]{2,1,0:T(8,128)S(1)} async-done(((f32[16,24,128]{2,1,0:T(8,128)}), f32[16,24,128]{2,1,0:T(8,128)S(1)}, u32[]{:S(2)}, u32[]{:S(2)}) %all-to-all-start.1) | async-done | bytes 196640 | tf_op jit(solution)/shard_map/all_to_all | solution.py:340
  68.7 0.0 copy-start
  68.7 0.7 copy-done
  69.4 6.0 %terms.1 = (bf16[64,128]{1,0:T(8,128)(2,1)}, f32[64,128]{1,0:T(8,128)}, f32[32,128]{1,0:T(8,128)}) custom-call(s32[3]{0:T(128)} %pad_add_fusion.refs_0_.place_ref, f32[16,24,128]{2,1,0:T(8,128)} %copy-done, bf16[32,32]{1,0:T(8,128)(2,1)} %refs_2_.1), custom_call_target="tpu_custom_call" | custom-call | flops 400000000 | bytes 4000000 | tf_op jit(solution)/shard_map/terms/pallas_call | solution.py:347
  75.4 9.5 %all-to-all-start.2 = ((f32[32,1,128]{2,1,0:T(1,128)}), f32[32,1,128]{2,1,0:T(1,128)S(1)}, u32[]{:S(2)}, u32[]{:S(2)}) async-start(f32[32,1,128]{2,1,0:T(1,128)} %bitcast.20), calls=%async_computation.2 | async-start | bytes 32768 | tf_op jit(solution)/shard_map/all_to_all | solution.py:354
  84.8 0.0 collective-permute-done.2.lo_ref
  84.8 0.0 copy-start.3
  84.9 0.0 collective-permute-done.3.hi_ref
  84.9 0.0 copy-start.4
  84.9 0.7 copy-done.3
  85.6 0.1 copy-done.4
  85.7 6.3 %grads.1 = (bf16[32,4,16,128]{3,2,1,0:T(8,128)(2,1)}, bf16[32,4,16,128]{3,2,1,0:T(8,128)(2,1)}) custom-call(s32[3]{0:T(128)} %pad_add_fusion.refs_0_.place_ref, bf16[64,128]{1,0:T(8,128)(2,1)} %get-tuple-element.16.left_ref, f32[64,128]{1,0:T(8,128)} %get-tuple-element.17.shift_ref, bf16[64,2048]{1,0:T(8,128)(2,1)} %copy-done.3, ...), custom_call_target="tpu_custom_call" | custom-call | flops 800000000 | bytes 8000000 | tf_op jit(solution)/shard_map/grads/pallas_call | solution.py:355
  91.9 0.0 all-to-all-done.2
  91.9 0.7 slice.19
  92.6 0.7 copy.10
  (2 shorter events, 0.0 us)
Async XLA Ops:
  1.6 10.8 %collective-permute-start = (bf16[32,1,16,128]{3,2,1,0:T(8,128)(2,1)S(1)}, bf16[32,1,16,128]{3,2,1,0:T(8,128)(2,1)S(1)}, u32[]{:S(2)}, u32[]{:S(2)}) collective-permute-start(bf16[32,1,16,128]{3,2,1,0:T(8,128)(2,1)S(1)} %get-tuple-element.33), channel_id=1, source_target_pairs={{0,1},{1,2},{2,3},{3,4},{4,5},{5,6},{6,7},{7,8},{8,9},{9,10},{10,1... | collective-permute-start | bytes 393224 | tf_op jit(solution)/shard_map/ppermute | solution.py:316
  6.0 6.5 %collective-permute-start.1 = (bf16[32,1,16,128]{3,2,1,0:T(8,128)(2,1)S(1)}, bf16[32,1,16,128]{3,2,1,0:T(8,128)(2,1)S(1)}, u32[]{:S(2)}, u32[]{:S(2)}) collective-permute-start(bf16[32,1,16,128]{3,2,1,0:T(8,128)(2,1)S(1)} %get-tuple-element.32), channel_id=1, source_target_pairs={{1,0},{2,1},{3,2},{4,3},{5,4},{6,5},{7,6},{8,7},{9,8},{10,9},{11,1... | collective-permute-start | bytes 393224 | tf_op jit(solution)/shard_map/ppermute | solution.py:317
  12.5 0.7 copy-start.5
  12.5 0.7 copy-start.6
  38.7 17.1 %copy-start.2 = (bf16[64,2048]{1,0:T(8,128)(2,1)S(1)}, bf16[64,2048]{1,0:T(8,128)(2,1)}, u32[]{:S(2)}) copy-start(bf16[64,2048]{1,0:T(8,128)(2,1)} %get-tuple-element.18.last_ref) | copy-start | bytes 786436
  38.7 20.3 %copy-start.1 = (bf16[64,2048]{1,0:T(8,128)(2,1)S(1)}, bf16[64,2048]{1,0:T(8,128)(2,1)}, u32[]{:S(2)}) copy-start(bf16[64,2048]{1,0:T(8,128)(2,1)} %get-tuple-element.19.first_ref) | copy-start | bytes 786436
  39.4 29.3 %all-to-all-start.1 = ((f32[16,24,128]{2,1,0:T(8,128)}), f32[16,24,128]{2,1,0:T(8,128)S(1)}, u32[]{:S(2)}, u32[]{:S(2)}) async-start(f32[16,24,128]{2,1,0:T(8,128)} %broadcast_in_dim.9), calls=%async_computation.1 | async-start | bytes 393216 | tf_op jit(solution)/shard_map/all_to_all | solution.py:340
  55.7 29.1 %collective-permute-start.2 = (bf16[64,2048]{1,0:T(8,128)(2,1)S(1)}, bf16[64,2048]{1,0:T(8,128)(2,1)S(1)}, u32[]{:S(2)}, u32[]{:S(2)}) collective-permute-start(bf16[64,2048]{1,0:T(8,128)(2,1)S(1)} %copy-done.2), channel_id=1, source_target_pairs={{0,1},{1,2},{2,3},{3,4},{4,5},{5,6},{6,7},{7,8},{8,9},{9,10},{10,1... | collective-permute-start | bytes 786440 | tf_op jit(solution)/shard_map/ppermute | solution.py:336
  59.0 25.8 %collective-permute-start.3 = (bf16[64,2048]{1,0:T(8,128)(2,1)S(1)}, bf16[64,2048]{1,0:T(8,128)(2,1)S(1)}, u32[]{:S(2)}, u32[]{:S(2)}) collective-permute-start(bf16[64,2048]{1,0:T(8,128)(2,1)S(1)} %copy-done.1), channel_id=1, source_target_pairs={{1,0},{2,1},{3,2},{4,3},{5,4},{6,5},{7,6},{8,7},{9,8},{10,9},{11,1... | collective-permute-start | bytes 786440 | tf_op jit(solution)/shard_map/ppermute | solution.py:337
  68.7 0.7 copy-start
  75.4 16.6 %all-to-all-start.2 = ((f32[32,1,128]{2,1,0:T(1,128)}), f32[32,1,128]{2,1,0:T(1,128)S(1)}, u32[]{:S(2)}, u32[]{:S(2)}) async-start(f32[32,1,128]{2,1,0:T(1,128)} %bitcast.20), calls=%async_computation.2 | async-start | bytes 32768 | tf_op jit(solution)/shard_map/all_to_all | solution.py:354
  84.8 0.7 copy-start.3
  84.9 0.8 copy-start.4

commit v3 on v2

--- a/solution.py
+++ b/solution.py
@@ -6,7 +6,6 @@
 from jax.experimental import pallas as pl
 from jax.experimental.pallas import tpu as pltpu
 from jax.sharding import PartitionSpec as P
-
 
 NEWTON = 5
 EPSILON = 1e-05
@@ -111,6 +110,15 @@
         )
 
 
+def edges_kernel(x_ref, first_ref, last_ref, sems):
+    first = pltpu.make_async_copy(x_ref.at[:, 0], first_ref, sems.at[0])
+    last = pltpu.make_async_copy(x_ref.at[:, D - 1], last_ref, sems.at[1])
+    first.start()
+    last.start()
+    first.wait()
+    last.wait()
+
+
 def inner_kernel(x_ref, g_ref, dk_ref, w_ref, gm_ref, acc_ref, *scratch):
     acc_ref[...] = jnp.zeros(acc_ref.shape, F32)
     xs = [lambda p=p: x_ref[:, p] for p in range(D)]
@@ -121,8 +129,8 @@
 def outer_kernel(x_ref, g_ref, lo_ref, hi_ref, dk_ref, w_ref, part_ref,
                  gm_lo_ref, gm_hi_ref, send_ref, acc_ref, *scratch):
     acc_ref[...] = part_ref[...]
-    xs = [lambda: lo_ref[:, 0]] + [lambda p=p: x_ref[:, p] for p in range(D)]
-    xs += [lambda: hi_ref[:, 0]]
+    xs = [lambda: lo_ref[...]] + [lambda p=p: x_ref[:, p] for p in range(D)]
+    xs += [lambda: hi_ref[...]]
     gs = [lambda p=p: g_ref[:, p] for p in (0, 3)]
     slab_sums(xs, gs, 3, dk_ref, w_ref, (gm_lo_ref, gm_hi_ref), acc_ref, *scratch)
 
@@ -312,12 +320,20 @@
     vmem = pl.BlockSpec(memory_space=pltpu.VMEM)
     smem = pl.BlockSpec(memory_space=pltpu.SMEM)
     shape = jax.ShapeDtypeStruct
-
-    x_lo = lax.ppermute(x[:, D - 1 :], "space", forward)
-    x_hi = lax.ppermute(x[:, :1], "space", backward)
+    near = lambda array: pltpu.with_memory_space_constraint(array, pltpu.VMEM)
+
+    x_first, x_last = pl.pallas_call(
+        edges_kernel,
+        in_specs=[pl.BlockSpec(memory_space=pl.ANY)],
+        out_shape=(pltpu.VMEM((C, H, W), BF16), pltpu.VMEM((C, H, W), BF16)),
+        scratch_shapes=[pltpu.SemaphoreType.DMA((2,))],
+        name="edges",
+    )(x)
+    x_lo = lax.ppermute(x_last, "space", forward)
+    x_hi = lax.ppermute(x_first, "space", backward)
     gm_inner, acc = pl.pallas_call(
         inner_kernel,
-        out_shape=(shape((2, 2 * C, HW), BF16), shape((368, 256), F32)),
+        out_shape=(pltpu.VMEM((2, 2 * C, HW), BF16), pltpu.VMEM((368, 256), F32)),
         scratch_shapes=scratch(D),
         cost_estimate=cost(6),
         name="inner",
@@ -325,14 +341,14 @@
     gm_first, gm_last, send = pl.pallas_call(
         outer_kernel,
         out_shape=(
-            shape((2 * C, HW), BF16),
-            shape((2 * C, HW), BF16),
-            shape((C * ROWS, W), F32),
+            pltpu.VMEM((2 * C, HW), BF16),
+            pltpu.VMEM((2 * C, HW), BF16),
+            pltpu.VMEM((C * ROWS, W), F32),
         ),
         scratch_shapes=[pltpu.VMEM((368, 256), F32)] + scratch(D + 2),
         cost_estimate=cost(6),
         name="outer",
-    )(x, g, x_lo, x_hi, depth_kernel, point_weight, acc)
+    )(x, g, near(x_lo), near(x_hi), depth_kernel, point_weight, near(acc))
     gm_lo = lax.ppermute(gm_last, "space", forward)
     gm_hi = lax.ppermute(gm_first, "space", backward)
     parts = lax.all_to_all(send.reshape(C, ROWS, W), "sample", 0, 0)
@@ -347,10 +363,14 @@
     left, shift, row = pl.pallas_call(
         lambda *refs: terms_kernel(count, *refs),
         in_specs=[smem] + [vmem] * 2,
-        out_shape=(shape((2 * C, 4 * C), BF16), shape((2 * C, W), F32), shape((C, W), F32)),
+        out_shape=(
+            pltpu.VMEM((2 * C, 4 * C), BF16),
+            pltpu.VMEM((2 * C, W), F32),
+            pltpu.VMEM((C, W), F32),
+        ),
         cost_estimate=cost(4),
         name="terms",
-    )(place, pay, point_weight)
+    )(place, near(pay), point_weight)
     rows = lax.all_to_all(row.reshape(C, 1, W), "sample", 0, 0).reshape(C, W)
     white, d_volume = pl.pallas_call(
         grads_kernel,
@@ -363,7 +383,10 @@
         ],
         cost_estimate=cost(8),
         name="grads",
-    )(place, left, shift, gm_lo, gm_first, gm_inner, gm_last, gm_hi, depth_kernel)
+    )(
+        place, near(left), near(shift), near(gm_lo), near(gm_first), near(gm_inner),
+        near(gm_last), near(gm_hi), depth_kernel,
+    )
     return white[None], d_volume[None], rows[:, 0:C].T, rows[:, C : C + 27]
 
 

time: 93.8 us -> 89.2 us (0.951)
  local copies, waits for them, and re-layouts: 5.23 us -> 2.05 us
  Pallas kernels: 24.1 us -> 21.6 us
  waiting for transfers between devices: 7.74 us -> 9.34 us
    unnamed x15 -> x1, local copies, waits for them, and re-layouts: 2.86 us -> 0.68 us
    pallas_call x2 -> x3, Pallas kernels: 11.9 us -> 10.2 us  [the longest x1 4.82 us: whole_step(): pl.pallas_call(outer_kernel, out_shape=(pltpu.VMEM((2 * C, HW), BF16), pl...]
    all_to_all x1, waiting for transfers between devices: 0.01 us -> 1.37 us  [whole_step(): rows = lax.all_to_all(row.reshape(C, 1, W), 'sample', 0, 0).reshape(C, W)]
    slice x1 -> x0, local copies, waits for them, and re-layouts: 1 us -> none  [whole_step(): x_hi = lax.ppermute(x[:, :1], 'space', backward)]
  transfers between devices with their start and end apart: 6 -> 6, of which waited for: 1 -> 3; matrix products, arithmetic and copies ran while one was open for 1% -> 1% of each run, Pallas kernels for 19% -> 18%
where the time goes in v3:
time: 89.2 us; the launch traced here: 88.7 us
  starting transfers between devices  35.2 us (39%)
  Pallas kernels  21.6 us (24%)
  blocking collectives  19.1 us (21%)
  waiting for transfers between devices  9.34 us (10%)
  local copies, waits for them, and re-layouts  2.05 us (2%)
    all_to_all x1, blocking collectives, whole_step(): parts = lax.all_to_all(send.reshape(C, ROWS, W), 'sample', 0, 0)  19.1 us
    all_to_all x1, starting transfers between devices, whole_step(): lax.all_to_all(jnp.broadcast_to(part, (slabs, ROWS, W)), 'space', 0, 0)  15.5 us
    all_to_all x1, starting transfers between devices, whole_step(): rows = lax.all_to_all(row.reshape(C, 1, W), 'sample', 0, 0).reshape(C, W)  9.47 us
    all_to_all x1, waiting for transfers between devices, whole_step(): lax.all_to_all(jnp.broadcast_to(part, (slabs, ROWS, W)), 'space', 0, 0)  7.79 us
    pallas_call x1, Pallas kernels, whole_step(): pl.pallas_call(lambda *refs: terms_kernel(count, *refs), in_specs=[smem]...  5.73 us
    pallas_call x1, Pallas kernels, whole_step(): pl.pallas_call(grads_kernel, in_specs=[smem] + [vmem] * 8, out_shape=(sha...  5.62 us
    pallas_call x1, Pallas kernels, whole_step(): pl.pallas_call(outer_kernel, out_shape=(pltpu.VMEM((2 * C, HW), BF16), pl...  4.82 us
    pallas_call x1, Pallas kernels, whole_step(): pl.pallas_call(inner_kernel, out_shape=(pltpu.VMEM((2, 2 * C, HW), BF16),...  4.4 us
  transfers between devices with their start and end apart: 6, of which 3 were waited for; matrix products, arithmetic and copies ran while one was open for 1% of the time, Pallas kernels for 18%

profile of v3, /device:TPU:1, one launch (start us, length us, event | category | flops | bytes accessed | tf_op | source)
XLA Modules:
  0.0 88.7 jit_solution(5906089655682086916)
XLA Ops:
  0.6 1.0 %edges.1 = (bf16[32,16,128]{2,1,0:T(8,128)(2,1)S(1)}, bf16[32,16,128]{2,1,0:T(8,128)(2,1)S(1)}) custom-call(bf16[32,4,16,128]{3,2,1,0:T(8,128)(2,1)} %bitcast.15), custom_call_target="tpu_custom_call" | custom-call | tf_op jit(solution)/shard_map/edges/pallas_call | solution.py:325
  1.6 4.4 %collective-permute-start = (bf16[32,16,128]{2,1,0:T(8,128)(2,1)S(1)}, bf16[32,16,128]{2,1,0:T(8,128)(2,1)S(1)}, u32[]{:S(2)}, u32[]{:S(2)}) collective-permute-start(bf16[32,16,128]{2,1,0:T(8,128)(2,1)S(1)} %get-tuple-element.16), channel_id=1, source_target_pairs={{0,1},{1,2},{2,3},{3,4},{4,5},{5,6},{6,7},{7,8},{8,9},{9,10},{10,1... | collective-permute-start | bytes 393224 | tf_op jit(solution)/shard_map/ppermute | solution.py:332
  6.0 1.3 %collective-permute-start.1 = (bf16[32,16,128]{2,1,0:T(8,128)(2,1)S(1)}, bf16[32,16,128]{2,1,0:T(8,128)(2,1)S(1)}, u32[]{:S(2)}, u32[]{:S(2)}) collective-permute-start(bf16[32,16,128]{2,1,0:T(8,128)(2,1)S(1)} %get-tuple-element.17), channel_id=1, source_target_pairs={{1,0},{2,1},{3,2},{4,3},{5,4},{6,5},{7,6},{8,7},{9,8},{10,9},{11,1... | collective-permute-start | bytes 393224 | tf_op jit(solution)/shard_map/ppermute | solution.py:333
  7.3 4.4 %inner.1 = (bf16[2,64,2048]{2,1,0:T(8,128)(2,1)S(1)}, f32[368,256]{1,0:T(8,128)S(1)}) custom-call(bf16[32,4,16,128]{3,2,1,0:T(8,128)(2,1)} %bitcast.16, bf16[32,4,16,128]{3,2,1,0:T(8,128)(2,1)} %bitcast.20, f32[32,27]{1,0:T(8,128)} %dk_ref.5, bf16[32,32]{1,0:T(8,128)(2,1)} %refs_2_.1), custom_call_target="tpu_custom_call" | custom-call | flops 600000000 | bytes 6000000 | tf_op jit(solution)/shard_map/inner/pallas_call | solution.py:334
  11.7 0.0 collective-permute-done.lo_ref
  11.7 0.2 collective-permute-done.1.hi_ref
  11.9 4.8 %outer.1 = (bf16[64,2048]{1,0:T(8,128)(2,1)S(1)}, bf16[64,2048]{1,0:T(8,128)(2,1)S(1)}, f32[768,128]{1,0:T(8,128)S(1)}) custom-call(bf16[32,4,16,128]{3,2,1,0:T(8,128)(2,1)} %bitcast.17, bf16[32,4,16,128]{3,2,1,0:T(8,128)(2,1)} %bitcast.21, bf16[32,16,128]{2,1,0:T(8,128)(2,1)S(1)} %collective-permute-done.lo_ref, ...), custom_call_target="tpu_custom_call" | custom-call | flops 600000000 | bytes 6000000 | tf_op jit(solution)/shard_map/outer/pallas_call | solution.py:341
  16.7 19.1 %all_to_all.15 = f32[32,24,128]{2,1,0:T(8,128)S(1)} all-to-all(f32[32,24,128]{2,1,0:T(8,128)S(1)} %bitcast.14), channel_id=1, replica_groups=mesh['sample'=32,'space'=16] {'sample'}, dimensions={0} | all-to-all | bytes 786432 | tf_op jit(solution)/shard_map/all_to_all | solution.py:354
  35.9 0.7 broadcast_in_dim.9
  36.6 15.5 %all-to-all-start.1 = ((f32[16,24,128]{2,1,0:T(8,128)}), f32[16,24,128]{2,1,0:T(8,128)S(1)}, u32[]{:S(2)}, u32[]{:S(2)}) async-start(f32[16,24,128]{2,1,0:T(8,128)} %broadcast_in_dim.9), calls=%async_computation.1 | async-start | bytes 393216 | tf_op jit(solution)/shard_map/all_to_all | solution.py:356
  52.1 3.3 %collective-permute-start.2 = (bf16[64,2048]{1,0:T(8,128)(2,1)S(1)}, bf16[64,2048]{1,0:T(8,128)(2,1)S(1)}, u32[]{:S(2)}, u32[]{:S(2)}) collective-permute-start(bf16[64,2048]{1,0:T(8,128)(2,1)S(1)} %get-tuple-element.22.last_ref), channel_id=1, source_target_pairs={{0,1},{1,2},{2,3},{3,4},{4,5},{5,6},{6,7},{7,8},{8,9},{9,10},{10,1... | collective-permute-start | bytes 786440 | tf_op jit(solution)/shard_map/ppermute | solution.py:352
  55.4 1.3 %collective-permute-start.3 = (bf16[64,2048]{1,0:T(8,128)(2,1)S(1)}, bf16[64,2048]{1,0:T(8,128)(2,1)S(1)}, u32[]{:S(2)}, u32[]{:S(2)}) collective-permute-start(bf16[64,2048]{1,0:T(8,128)(2,1)S(1)} %get-tuple-element.23.first_ref), channel_id=1, source_target_pairs={{1,0},{2,1},{3,2},{4,3},{5,4},{6,5},{7,6},{8,7},{9,8},{10,9},{11,1... | collective-permute-start | bytes 786440 | tf_op jit(solution)/shard_map/ppermute | solution.py:353
  56.7 0.6 pad_add_fusion.refs_0_.place_ref
  57.3 7.8 %all-to-all-done.1.refs_1_ = f32[16,24,128]{2,1,0:T(8,128)S(1)} async-done(((f32[16,24,128]{2,1,0:T(8,128)}), f32[16,24,128]{2,1,0:T(8,128)S(1)}, u32[]{:S(2)}, u32[]{:S(2)}) %all-to-all-start.1) | async-done | bytes 196640 | tf_op jit(solution)/shard_map/all_to_all | solution.py:356
  65.1 5.7 %terms.1 = (bf16[64,128]{1,0:T(8,128)(2,1)S(1)}, f32[64,128]{1,0:T(8,128)S(1)}, f32[32,128]{1,0:T(8,128)}) custom-call(s32[3]{0:T(128)} %pad_add_fusion.refs_0_.place_ref, f32[16,24,128]{2,1,0:T(8,128)S(1)} %all-to-all-done.1.refs_1_, bf16[32,32]{1,0:T(8,128)(2,1)} %refs_2_.1), custom_call_target="tpu_custom_call" | custom-call | flops 400000000 | bytes 4000000 | tf_op jit(solution)/shard_map/terms/pallas_call | solution.py:363
  70.9 9.5 %all-to-all-start.2 = ((f32[32,1,128]{2,1,0:T(1,128)}), f32[32,1,128]{2,1,0:T(1,128)S(1)}, u32[]{:S(2)}, u32[]{:S(2)}) async-start(f32[32,1,128]{2,1,0:T(1,128)} %bitcast.9), calls=%async_computation.2 | async-start | bytes 32768 | tf_op jit(solution)/shard_map/all_to_all | solution.py:374
  80.3 0.0 collective-permute-done.2.lo_ref
  80.4 0.0 collective-permute-done.3.hi_ref
  80.4 5.6 %grads.1 = (bf16[32,4,16,128]{3,2,1,0:T(8,128)(2,1)}, bf16[32,4,16,128]{3,2,1,0:T(8,128)(2,1)}) custom-call(s32[3]{0:T(128)} %pad_add_fusion.refs_0_.place_ref, bf16[64,128]{1,0:T(8,128)(2,1)S(1)} %get-tuple-element.20.left_ref, f32[64,128]{1,0:T(8,128)S(1)} %get-tuple-element.21.shift_ref, bf16[64,2048]{1,0:T(8,128)(2,1)S(1)} %collective-permute-done.2.lo_ref, ...), custom_call_target="tpu_custom_call" | custom-call | flops 800000000 | bytes 8000000 | tf_op jit(solution)/shard_map/grads/pallas_call | solution.py:375
  86.0 1.4 %all-to-all-done.2 = f32[32,1,128]{2,1,0:T(1,128)S(1)} async-done(((f32[32,1,128]{2,1,0:T(1,128)}), f32[32,1,128]{2,1,0:T(1,128)S(1)}, u32[]{:S(2)}, u32[]{:S(2)}) %all-to-all-start.2) | async-done | bytes 16416 | tf_op jit(solution)/shard_map/all_to_all | solution.py:374
  87.3 0.7 slice.9
  88.0 0.7 copy.10
  (2 shorter events, 0.0 us)
Async XLA Ops:
  1.6 10.1 %collective-permute-start = (bf16[32,16,128]{2,1,0:T(8,128)(2,1)S(1)}, bf16[32,16,128]{2,1,0:T(8,128)(2,1)S(1)}, u32[]{:S(2)}, u32[]{:S(2)}) collective-permute-start(bf16[32,16,128]{2,1,0:T(8,128)(2,1)S(1)} %get-tuple-element.16), channel_id=1, source_target_pairs={{0,1},{1,2},{2,3},{3,4},{4,5},{5,6},{6,7},{7,8},{8,9},{9,10},{10,1... | collective-permute-start | bytes 393224 | tf_op jit(solution)/shard_map/ppermute | solution.py:332
  6.0 5.9 %collective-permute-start.1 = (bf16[32,16,128]{2,1,0:T(8,128)(2,1)S(1)}, bf16[32,16,128]{2,1,0:T(8,128)(2,1)S(1)}, u32[]{:S(2)}, u32[]{:S(2)}) collective-permute-start(bf16[32,16,128]{2,1,0:T(8,128)(2,1)S(1)} %get-tuple-element.17), channel_id=1, source_target_pairs={{1,0},{2,1},{3,2},{4,3},{5,4},{6,5},{7,6},{8,7},{9,8},{10,9},{11,1... | collective-permute-start | bytes 393224 | tf_op jit(solution)/shard_map/ppermute | solution.py:333
  36.6 28.6 %all-to-all-start.1 = ((f32[16,24,128]{2,1,0:T(8,128)}), f32[16,24,128]{2,1,0:T(8,128)S(1)}, u32[]{:S(2)}, u32[]{:S(2)}) async-start(f32[16,24,128]{2,1,0:T(8,128)} %broadcast_in_dim.9), calls=%async_computation.1 | async-start | bytes 393216 | tf_op jit(solution)/shard_map/all_to_all | solution.py:356
  52.1 28.2 %collective-permute-start.2 = (bf16[64,2048]{1,0:T(8,128)(2,1)S(1)}, bf16[64,2048]{1,0:T(8,128)(2,1)S(1)}, u32[]{:S(2)}, u32[]{:S(2)}) collective-permute-start(bf16[64,2048]{1,0:T(8,128)(2,1)S(1)} %get-tuple-element.22.last_ref), channel_id=1, source_target_pairs={{0,1},{1,2},{2,3},{3,4},{4,5},{5,6},{6,7},{7,8},{8,9},{9,10},{10,1... | collective-permute-start | bytes 786440 | tf_op jit(solution)/shard_map/ppermute | solution.py:352
  55.4 24.9 %collective-permute-start.3 = (bf16[64,2048]{1,0:T(8,128)(2,1)S(1)}, bf16[64,2048]{1,0:T(8,128)(2,1)S(1)}, u32[]{:S(2)}, u32[]{:S(2)}) collective-permute-start(bf16[64,2048]{1,0:T(8,128)(2,1)S(1)} %get-tuple-element.23.first_ref), channel_id=1, source_target_pairs={{1,0},{2,1},{3,2},{4,3},{5,4},{6,5},{7,6},{8,7},{9,8},{10,9},{11,1... | collective-permute-start | bytes 786440 | tf_op jit(solution)/shard_map/ppermute | solution.py:353
  70.9 16.5 %all-to-all-start.2 = ((f32[32,1,128]{2,1,0:T(1,128)}), f32[32,1,128]{2,1,0:T(1,128)S(1)}, u32[]{:S(2)}, u32[]{:S(2)}) async-start(f32[32,1,128]{2,1,0:T(1,128)} %bitcast.9), calls=%async_computation.2 | async-start | bytes 32768 | tf_op jit(solution)/shard_map/all_to_all | solution.py:374

commit v4 on v3

--- a/solution.py
+++ b/solution.py
@@ -43,25 +43,26 @@
 
 def stencil(src_ref, taps_ref, dst_ref, planes, step=1):
     lane = iota((8, W), 1)
-    for group in range(C // 8):
-        rows = pl.ds(8 * group, 8)
+
+    def plane(i, carry):
+        group = i // planes
+        p = i - group * planes
+        rows = pl.ds(pl.multiple_of(8 * group, 8), 8)
         taps = [taps_ref[t, rows, :] for t in range(27)]
-
-        def plane(p, carry):
-            for h in range(H):
-                parts = [None, None, None]
-                for a in range(3):
-                    for b in range(3):
-                        cells = src_ref[step * p + a, rows, (h + b) * W : (h + b + 1) * W]
-                        for e in range(3):
-                            term = taps[9 * a + 3 * b + e] * cells
-                            parts[e] = term if parts[e] is None else parts[e] + term
-                left = jnp.where(lane == 0, 0.0, pltpu.roll(parts[0], 1, 1))
-                right = jnp.where(lane == W - 1, 0.0, pltpu.roll(parts[2], W - 1, 1))
-                dst_ref[p, rows, h * W : (h + 1) * W] = parts[1] + left + right
-            return carry
-
-        lax.fori_loop(0, planes, plane, 0)
+        for h in range(H):
+            parts = [None, None, None]
+            for a in range(3):
+                for b in range(3):
+                    cells = src_ref[step * p + a, rows, (h + b) * W : (h + b + 1) * W]
+                    for e in range(3):
+                        term = taps[9 * a + 3 * b + e] * cells
+                        parts[e] = term if parts[e] is None else parts[e] + term
+            left = jnp.where(lane == 0, 0.0, pltpu.roll(parts[0], 1, 1))
+            right = jnp.where(lane == W - 1, 0.0, pltpu.roll(parts[2], W - 1, 1))
+            dst_ref[p, rows, h * W : (h + 1) * W] = parts[1] + left + right
+        return carry
+
+    lax.fori_loop(0, planes * (C // 8), plane, 0)
 
 
 def slab_sums(xs, gs, step, dk_ref, w_ref, gm_refs, acc_ref,
@@ -193,31 +194,24 @@
     cov = second / count - jnp.where(mine, avg_col * avg, 0.0) + EPSILON * eye
     trace = per_group(jnp.sum(cov * eye, axis=0, keepdims=True))
     normed = cov / trace
+    d_whiten = grad_mat - jnp.where(mine, column(gf_row) * avg, 0.0)
+
     project = 1.5 * eye - 0.5 * normed
-    saved = []
+    slope = -0.5 * d_whiten
     for _ in range(NEWTON - 1):
-        both = dot_high(project, jnp.concatenate([project, normed], axis=1))
-        square, pn = both[:, 0:C], both[:, C : 2 * C]
-        three = dot_high(square, jnp.concatenate([pn, project, normed], axis=1))
-        saved.append((
-            jnp.concatenate([project, square, three[:, C : 2 * C]], axis=0),
-            jnp.concatenate([three[:, 2 * C : 3 * C], pn, normed], axis=0),
-        ))
-        project = 1.5 * project - 0.5 * three[:, 0:C]
+        pair = jnp.concatenate([project, slope], axis=0)
+        squares = dot_high(pair, project)
+        scaled = dot_high(pair, normed)
+        square = squares[0:C]
+        d_square = squares[C : 2 * C] + dot_high(project, slope)
+        d_scaled = scaled[C : 2 * C] + dot_high(project, d_whiten)
+        cubes = dot_high(jnp.concatenate([square, d_square], axis=0), scaled[0:C])
+        slope = 1.5 * slope - 0.5 * (cubes[C : 2 * C] + dot_high(square, d_scaled))
+        project = 1.5 * project - 0.5 * cubes[0:C]
     root = jnp.sqrt(trace)
     whiten = project / root
     offset_col = jnp.sum(whiten * avg, axis=1, keepdims=True)
-
-    d_whiten = grad_mat - jnp.where(mine, column(gf_row) * avg, 0.0)
-    d_project = d_whiten / root
-    d_normed = jnp.zeros((C, C), F32)
-    for powers, tail in reversed(saved):
-        delta = -0.5 * d_project
-        ahead = dot_high(powers, delta)
-        d_normed = d_normed + ahead[2 * C : 3 * C]
-        terms = jnp.concatenate([delta, ahead[0:C], ahead[C : 2 * C]], axis=1)
-        d_project = 1.5 * d_project + dot_high(terms, tail)
-    d_normed = d_normed - 0.5 * d_project
+    d_normed = slope / root
     d_trace = jnp.sum(-0.5 * d_whiten * whiten - d_normed * normed, axis=0, keepdims=True)
     d_trace = per_group(d_trace) / trace
     d_cov = d_normed / trace + d_trace * eye
@@ -296,6 +290,12 @@
     stencil(dh_ref, taps_ref, out_ref, D)
     for z in range(D):
         dvol_ref[:, z] = out_ref[z].astype(BF16).reshape(C, H, W)
+
+
+def finish_kernel(rows_ref, point_ref, taps_ref):
+    rows = rows_ref[...]
+    point_ref[...] = rows[:, 0:C].T
+    taps_ref[...] = rows[:, C : C + 27]
 
 
 def cost(us):
@@ -387,7 +387,13 @@
         place, near(left), near(shift), near(gm_lo), near(gm_first), near(gm_inner),
         near(gm_last), near(gm_hi), depth_kernel,
     )
-    return white[None], d_volume[None], rows[:, 0:C].T, rows[:, C : C + 27]
+    d_point, d_kernel = pl.pallas_call(
+        finish_kernel,
+        out_shape=(shape((C, C), F32), shape((C, 27), F32)),
+        in_specs=[vmem],
+        name="finish",
+    )(near(rows))
+    return white[None], d_volume[None], d_point, d_kernel
 
 
 def solution(mesh):

time: 89.2 us -> 86.7 us (0.972)
  Pallas kernels: 21.6 us -> 20 us
  local copies, waits for them, and re-layouts: 2.05 us -> 0.69 us
    pallas_call x1, Pallas kernels: 5.73 us -> 4.16 us  [whole_step(): pl.pallas_call(lambda *refs: terms_kernel(count, *refs), in_specs=[smem]...]
  transfers between devices with their start and end apart: 6 -> 6, of which waited for: 3 -> 3; matrix products, arithmetic and copies ran while one was open for 1% -> 1% of each run, Pallas kernels for 18% -> 16%
where the time goes in v4:
time: 86.7 us; the launch traced here: 86.1 us
  starting transfers between devices  35.1 us (40%)
  Pallas kernels  20 us (23%)
  blocking collectives  19.1 us (22%)
  waiting for transfers between devices  9.79 us (11%)
    all_to_all x1, blocking collectives, whole_step(): parts = lax.all_to_all(send.reshape(C, ROWS, W), 'sample', 0, 0)  19.1 us
    all_to_all x1, starting transfers between devices, whole_step(): lax.all_to_all(jnp.broadcast_to(part, (slabs, ROWS, W)), 'space', 0, 0)  15.4 us
    all_to_all x1, starting transfers between devices, whole_step(): rows = lax.all_to_all(row.reshape(C, 1, W), 'sample', 0, 0).reshape(C, W)  9.45 us
    all_to_all x1, waiting for transfers between devices, whole_step(): lax.all_to_all(jnp.broadcast_to(part, (slabs, ROWS, W)), 'space', 0, 0)  7.76 us
    pallas_call x1, Pallas kernels, whole_step(): pl.pallas_call(grads_kernel, in_specs=[smem] + [vmem] * 8, out_shape=(sha...  5.29 us
    pallas_call x1, Pallas kernels, whole_step(): pl.pallas_call(outer_kernel, out_shape=(pltpu.VMEM((2 * C, HW), BF16), pl...  4.67 us
    ppermute x1, starting transfers between devices, whole_step(): x_lo = lax.ppermute(x_last, 'space', forward)  4.37 us
    pallas_call x1, Pallas kernels, whole_step(): pl.pallas_call(inner_kernel, out_shape=(pltpu.VMEM((2, 2 * C, HW), BF16),...  4.24 us
  transfers between devices with their start and end apart: 6, of which 3 were waited for; matrix products, arithmetic and copies ran while one was open for 1% of the time, Pallas kernels for 16%

profile of v4, /device:TPU:1, one launch (start us, length us, event | category | flops | bytes accessed | tf_op | source)
XLA Modules:
  0.0 86.1 jit_solution(9808963821608758685)
XLA Ops:
  0.6 1.0 %edges.1 = (bf16[32,16,128]{2,1,0:T(8,128)(2,1)S(1)}, bf16[32,16,128]{2,1,0:T(8,128)(2,1)S(1)}) custom-call(bf16[32,4,16,128]{3,2,1,0:T(8,128)(2,1)} %bitcast.14), custom_call_target="tpu_custom_call" | custom-call | tf_op jit(solution)/shard_map/edges/pallas_call | solution.py:325
  1.6 4.4 %collective-permute-start = (bf16[32,16,128]{2,1,0:T(8,128)(2,1)S(1)}, bf16[32,16,128]{2,1,0:T(8,128)(2,1)S(1)}, u32[]{:S(2)}, u32[]{:S(2)}) collective-permute-start(bf16[32,16,128]{2,1,0:T(8,128)(2,1)S(1)} %get-tuple-element.18), channel_id=1, source_target_pairs={{0,1},{1,2},{2,3},{3,4},{4,5},{5,6},{6,7},{7,8},{8,9},{9,10},{10,1... | collective-permute-start | bytes 393224 | tf_op jit(solution)/shard_map/ppermute | solution.py:332
  6.0 1.3 %collective-permute-start.1 = (bf16[32,16,128]{2,1,0:T(8,128)(2,1)S(1)}, bf16[32,16,128]{2,1,0:T(8,128)(2,1)S(1)}, u32[]{:S(2)}, u32[]{:S(2)}) collective-permute-start(bf16[32,16,128]{2,1,0:T(8,128)(2,1)S(1)} %get-tuple-element.19), channel_id=1, source_target_pairs={{1,0},{2,1},{3,2},{4,3},{5,4},{6,5},{7,6},{8,7},{9,8},{10,9},{11,1... | collective-permute-start | bytes 393224 | tf_op jit(solution)/shard_map/ppermute | solution.py:333
  7.3 4.2 %inner.1 = (bf16[2,64,2048]{2,1,0:T(8,128)(2,1)S(1)}, f32[368,256]{1,0:T(8,128)S(1)}) custom-call(bf16[32,4,16,128]{3,2,1,0:T(8,128)(2,1)} %bitcast.15, bf16[32,4,16,128]{3,2,1,0:T(8,128)(2,1)} %bitcast.17, f32[32,27]{1,0:T(8,128)} %dk_ref.5, bf16[32,32]{1,0:T(8,128)(2,1)} %refs_2_.1), custom_call_target="tpu_custom_call" | custom-call | flops 600000000 | bytes 6000000 | tf_op jit(solution)/shard_map/inner/pallas_call | solution.py:334
  11.5 0.0 collective-permute-done.lo_ref
  11.6 0.3 collective-permute-done.1.hi_ref
  11.9 4.7 %outer.1 = (bf16[64,2048]{1,0:T(8,128)(2,1)S(1)}, bf16[64,2048]{1,0:T(8,128)(2,1)S(1)}, f32[768,128]{1,0:T(8,128)S(1)}) custom-call(bf16[32,4,16,128]{3,2,1,0:T(8,128)(2,1)} %bitcast.16, bf16[32,4,16,128]{3,2,1,0:T(8,128)(2,1)} %bitcast.18, bf16[32,16,128]{2,1,0:T(8,128)(2,1)S(1)} %collective-permute-done.lo_ref, ...), custom_call_target="tpu_custom_call" | custom-call | flops 600000000 | bytes 6000000 | tf_op jit(solution)/shard_map/outer/pallas_call | solution.py:341
  16.6 19.1 %all_to_all.15 = f32[32,24,128]{2,1,0:T(8,128)S(1)} all-to-all(f32[32,24,128]{2,1,0:T(8,128)S(1)} %bitcast.12), channel_id=1, replica_groups=mesh['sample'=32,'space'=16] {'sample'}, dimensions={0} | all-to-all | bytes 786432 | tf_op jit(solution)/shard_map/all_to_all | solution.py:354
  35.7 0.7 broadcast_in_dim.9
  36.4 15.4 %all-to-all-start.1 = ((f32[16,24,128]{2,1,0:T(8,128)}), f32[16,24,128]{2,1,0:T(8,128)S(1)}, u32[]{:S(2)}, u32[]{:S(2)}) async-start(f32[16,24,128]{2,1,0:T(8,128)} %broadcast_in_dim.9), calls=%async_computation.1 | async-start | bytes 393216 | tf_op jit(solution)/shard_map/all_to_all | solution.py:356
  51.8 3.3 %collective-permute-start.2 = (bf16[64,2048]{1,0:T(8,128)(2,1)S(1)}, bf16[64,2048]{1,0:T(8,128)(2,1)S(1)}, u32[]{:S(2)}, u32[]{:S(2)}) collective-permute-start(bf16[64,2048]{1,0:T(8,128)(2,1)S(1)} %get-tuple-element.24.last_ref), channel_id=1, source_target_pairs={{0,1},{1,2},{2,3},{3,4},{4,5},{5,6},{6,7},{7,8},{8,9},{9,10},{10,1... | collective-permute-start | bytes 786440 | tf_op jit(solution)/shard_map/ppermute | solution.py:352
  55.1 1.3 %collective-permute-start.3 = (bf16[64,2048]{1,0:T(8,128)(2,1)S(1)}, bf16[64,2048]{1,0:T(8,128)(2,1)S(1)}, u32[]{:S(2)}, u32[]{:S(2)}) collective-permute-start(bf16[64,2048]{1,0:T(8,128)(2,1)S(1)} %get-tuple-element.25.first_ref), channel_id=1, source_target_pairs={{1,0},{2,1},{3,2},{4,3},{5,4},{6,5},{7,6},{8,7},{9,8},{10,9},{11,1... | collective-permute-start | bytes 786440 | tf_op jit(solution)/shard_map/ppermute | solution.py:353
  56.4 0.7 pad_add_fusion.refs_0_.place_ref
  57.1 7.8 %all-to-all-done.1.refs_1_ = f32[16,24,128]{2,1,0:T(8,128)S(1)} async-done(((f32[16,24,128]{2,1,0:T(8,128)}), f32[16,24,128]{2,1,0:T(8,128)S(1)}, u32[]{:S(2)}, u32[]{:S(2)}) %all-to-all-start.1) | async-done | bytes 196640 | tf_op jit(solution)/shard_map/all_to_all | solution.py:356
  64.8 4.2 %terms.1 = (bf16[64,128]{1,0:T(8,128)(2,1)S(1)}, f32[64,128]{1,0:T(8,128)S(1)}, f32[32,128]{1,0:T(8,128)}) custom-call(s32[3]{0:T(128)} %pad_add_fusion.refs_0_.place_ref, f32[16,24,128]{2,1,0:T(8,128)S(1)} %all-to-all-done.1.refs_1_, bf16[32,32]{1,0:T(8,128)(2,1)} %refs_2_.1), custom_call_target="tpu_custom_call" | custom-call | flops 400000000 | bytes 4000000 | tf_op jit(solution)/shard_map/terms/pallas_call | solution.py:363
  69.0 9.4 %all-to-all-start.2 = ((f32[32,1,128]{2,1,0:T(1,128)}), f32[32,1,128]{2,1,0:T(1,128)S(1)}, u32[]{:S(2)}, u32[]{:S(2)}) async-start(f32[32,1,128]{2,1,0:T(1,128)} %bitcast.9), calls=%async_computation.2 | async-start | bytes 32768 | tf_op jit(solution)/shard_map/all_to_all | solution.py:374
  78.4 0.0 collective-permute-done.2.lo_ref
  78.4 0.0 collective-permute-done.3.hi_ref
  78.5 5.3 %grads.1 = (bf16[32,4,16,128]{3,2,1,0:T(8,128)(2,1)}, bf16[32,4,16,128]{3,2,1,0:T(8,128)(2,1)}) custom-call(s32[3]{0:T(128)} %pad_add_fusion.refs_0_.place_ref, bf16[64,128]{1,0:T(8,128)(2,1)S(1)} %get-tuple-element.22.left_ref, f32[64,128]{1,0:T(8,128)S(1)} %get-tuple-element.23.shift_ref, bf16[64,2048]{1,0:T(8,128)(2,1)S(1)} %collective-permute-done.2.lo_ref, ...), custom_call_target="tpu_custom_call" | custom-call | flops 800000000 | bytes 8000000 | tf_op jit(solution)/shard_map/grads/pallas_call | solution.py:375
  83.7 1.7 %all-to-all-done.2 = f32[32,1,128]{2,1,0:T(1,128)S(1)} async-done(((f32[32,1,128]{2,1,0:T(1,128)}), f32[32,1,128]{2,1,0:T(1,128)S(1)}, u32[]{:S(2)}, u32[]{:S(2)}) %all-to-all-start.2) | async-done | bytes 16416 | tf_op jit(solution)/shard_map/all_to_all | solution.py:374
  85.4 0.7 finish.1
  (1 shorter events, 0.0 us)
Async XLA Ops:
  1.6 9.9 %collective-permute-start = (bf16[32,16,128]{2,1,0:T(8,128)(2,1)S(1)}, bf16[32,16,128]{2,1,0:T(8,128)(2,1)S(1)}, u32[]{:S(2)}, u32[]{:S(2)}) collective-permute-start(bf16[32,16,128]{2,1,0:T(8,128)(2,1)S(1)} %get-tuple-element.18), channel_id=1, source_target_pairs={{0,1},{1,2},{2,3},{3,4},{4,5},{5,6},{6,7},{7,8},{8,9},{9,10},{10,1... | collective-permute-start | bytes 393224 | tf_op jit(solution)/shard_map/ppermute | solution.py:332
  6.0 5.9 %collective-permute-start.1 = (bf16[32,16,128]{2,1,0:T(8,128)(2,1)S(1)}, bf16[32,16,128]{2,1,0:T(8,128)(2,1)S(1)}, u32[]{:S(2)}, u32[]{:S(2)}) collective-permute-start(bf16[32,16,128]{2,1,0:T(8,128)(2,1)S(1)} %get-tuple-element.19), channel_id=1, source_target_pairs={{1,0},{2,1},{3,2},{4,3},{5,4},{6,5},{7,6},{8,7},{9,8},{10,9},{11,1... | collective-permute-start | bytes 393224 | tf_op jit(solution)/shard_map/ppermute | solution.py:333
  36.4 28.4 %all-to-all-start.1 = ((f32[16,24,128]{2,1,0:T(8,128)}), f32[16,24,128]{2,1,0:T(8,128)S(1)}, u32[]{:S(2)}, u32[]{:S(2)}) async-start(f32[16,24,128]{2,1,0:T(8,128)} %broadcast_in_dim.9), calls=%async_computation.1 | async-start | bytes 393216 | tf_op jit(solution)/shard_map/all_to_all | solution.py:356
  51.8 26.6 %collective-permute-start.2 = (bf16[64,2048]{1,0:T(8,128)(2,1)S(1)}, bf16[64,2048]{1,0:T(8,128)(2,1)S(1)}, u32[]{:S(2)}, u32[]{:S(2)}) collective-permute-start(bf16[64,2048]{1,0:T(8,128)(2,1)S(1)} %get-tuple-element.24.last_ref), channel_id=1, source_target_pairs={{0,1},{1,2},{2,3},{3,4},{4,5},{5,6},{6,7},{7,8},{8,9},{9,10},{10,1... | collective-permute-start | bytes 786440 | tf_op jit(solution)/shard_map/ppermute | solution.py:352
  55.1 23.3 %collective-permute-start.3 = (bf16[64,2048]{1,0:T(8,128)(2,1)S(1)}, bf16[64,2048]{1,0:T(8,128)(2,1)S(1)}, u32[]{:S(2)}, u32[]{:S(2)}) collective-permute-start(bf16[64,2048]{1,0:T(8,128)(2,1)S(1)} %get-tuple-element.25.first_ref), channel_id=1, source_target_pairs={{1,0},{2,1},{3,2},{4,3},{5,4},{6,5},{7,6},{8,7},{9,8},{10,9},{11,1... | collective-permute-start | bytes 786440 | tf_op jit(solution)/shard_map/ppermute | solution.py:353
  69.0 16.5 %all-to-all-start.2 = ((f32[32,1,128]{2,1,0:T(1,128)}), f32[32,1,128]{2,1,0:T(1,128)S(1)}, u32[]{:S(2)}, u32[]{:S(2)}) async-start(f32[32,1,128]{2,1,0:T(1,128)} %bitcast.9), calls=%async_computation.2 | async-start | bytes 32768 | tf_op jit(solution)/shard_map/all_to_all | solution.py:374

commit v5 on v4

--- a/solution.py
+++ b/solution.py
@@ -15,6 +15,7 @@
 W = 128
 HW = H * W
 PW = (H + 2) * W
+SPAN = 512
 ROWS = 24
 HIGH = lax.Precision.HIGHEST
 F32 = jnp.float32
@@ -35,49 +36,64 @@
     return lax.broadcasted_iota(jnp.int32, shape, dim)
 
 
-def spread_taps(dk_ref, taps_ref, flip):
-    for t in range(27):
-        s = 26 - t if flip else t
-        taps_ref[t] = jnp.broadcast_to(dk_ref[:, s : s + 1], (C, W))
-
-
-def stencil(src_ref, taps_ref, dst_ref, planes, step=1):
-    lane = iota((8, W), 1)
-
-    def plane(i, carry):
-        group = i // planes
-        p = i - group * planes
-        rows = pl.ds(pl.multiple_of(8 * group, 8), 8)
-        taps = [taps_ref[t, rows, :] for t in range(27)]
-        for h in range(H):
-            parts = [None, None, None]
-            for a in range(3):
-                for b in range(3):
-                    cells = src_ref[step * p + a, rows, (h + b) * W : (h + b + 1) * W]
-                    for e in range(3):
-                        term = taps[9 * a + 3 * b + e] * cells
-                        parts[e] = term if parts[e] is None else parts[e] + term
-            left = jnp.where(lane == 0, 0.0, pltpu.roll(parts[0], 1, 1))
-            right = jnp.where(lane == W - 1, 0.0, pltpu.roll(parts[2], W - 1, 1))
-            dst_ref[p, rows, h * W : (h + 1) * W] = parts[1] + left + right
-        return carry
-
-    lax.fori_loop(0, planes * (C // 8), plane, 0)
+def two_terms(values):
+    coarse = values.astype(BF16)
+    return coarse, (values - coarse.astype(F32)).astype(BF16)
+
+
+def tap_matrices(dk_ref, flip):
+    row = iota((C, W), 0)
+    lane = iota((C, W), 1)
+    taps = [
+        jnp.broadcast_to(dk_ref[:, (26 - t if flip else t) : (27 - t if flip else t + 1)], (C, W))
+        for t in range(27)
+    ]
+    blocks = []
+    for e in range(3):
+        halves = []
+        for half in range(2):
+            block = jnp.zeros((C, W), F32)
+            for i in range(4):
+                block = jnp.where(lane == row + C * i, taps[3 * (4 * half + i) + e], block)
+            halves.append(block)
+        blocks.append(jnp.concatenate(halves, axis=1))
+    return jnp.concatenate(blocks, axis=0), taps[24:27]
+
+
+def stencil_rows(sums, last, last_taps):
+    lane = iota((C, W), 1)
+    rows = []
+    for i in range(last.shape[1] // W):
+        span = slice(i * W, (i + 1) * W)
+        parts = [sums[C * e : C * (e + 1), span] + last_taps[e] * last[:, span] for e in range(3)]
+        left = jnp.where(lane == 0, 0.0, pltpu.roll(parts[0], 1, 1))
+        right = jnp.where(lane == W - 1, 0.0, pltpu.roll(parts[2], W - 1, 1))
+        rows.append(parts[1] + left + right)
+    return jnp.concatenate(rows, axis=1)
+
+
+def offsets(ref, plane, start, width):
+    return [
+        ref[plane + a, :, start + b * W : start + b * W + width]
+        for a in range(3) for b in range(3)
+    ]
 
 
 def slab_sums(xs, gs, step, dk_ref, w_ref, gm_refs, acc_ref,
-              xf_ref, xb_ref, hid_ref, taps_ref, right_ref):
+              xb_ref, hid_ref, right_ref):
     zeros = jnp.zeros((len(xs), C, W), F32)
-    xf_ref[:, :, 0:W] = zeros
-    xf_ref[:, :, PW - W : PW] = zeros
     xb_ref[:, :, 0:W] = zeros.astype(BF16)
     xb_ref[:, :, PW - W : PW] = zeros.astype(BF16)
     for p, cells in enumerate(xs):
-        cells = cells().reshape(C, HW)
-        xf_ref[p, :, W : W + HW] = cells.astype(F32)
-        xb_ref[p, :, W : W + HW] = cells
-    spread_taps(dk_ref, taps_ref, False)
-    stencil(xf_ref, taps_ref, hid_ref, 2, step)
+        xb_ref[p, :, W : W + HW] = cells().reshape(C, HW)
+    matrix, last_taps = tap_matrices(dk_ref, False)
+    matrix = jnp.concatenate(two_terms(matrix), axis=0)
+    for i in range(2):
+        for start in range(0, HW, SPAN):
+            cells = offsets(xb_ref, step * i, start, SPAN)
+            both = dot(matrix, jnp.concatenate(cells[:8], axis=0))
+            rows = stencil_rows(both[:96] + both[96:], cells[8].astype(F32), last_taps)
+            hid_ref[i, :, start : start + SPAN] = rows.astype(BF16)
 
     lane = iota((1, W), 1)
     row16 = iota((16, W), 0)
@@ -92,7 +108,7 @@
         right_ref[192:208, h * W : (h + 1) * W] = ones
     first = jnp.where(iota((16, HW), 0) == 0, 1.0, 0.0).astype(BF16)
     for i in range(2):
-        hidden = hid_ref[i].astype(BF16)
+        hidden = hid_ref[i]
         mixed = dot(w_ref[...], hidden).astype(BF16)
         gm_refs[i][0:C, :] = gs[i]().reshape(C, HW)
         gm_refs[i][C : 2 * C, :] = mixed
@@ -102,18 +118,17 @@
             right_ref[0:64, span] = pltpu.roll(cells, W - 1, 1) * keep0
             right_ref[64:128, span] = cells
             right_ref[128:192, span] = pltpu.roll(cells, 1, 1) * keep2
-        left = [
-            xb_ref[step * i + a, :, b * W : b * W + HW] for a in range(3) for b in range(3)
-        ]
-        left += [hidden, mixed, first]
+        left = offsets(xb_ref, step * i, 0, HW) + [hidden, mixed, first]
         acc_ref[:, 0:208] += dot(
             jnp.concatenate(left, axis=0), right_ref[...], ((1,), (1,))
         )
 
 
-def edges_kernel(x_ref, first_ref, last_ref, sems):
-    first = pltpu.make_async_copy(x_ref.at[:, 0], first_ref, sems.at[0])
-    last = pltpu.make_async_copy(x_ref.at[:, D - 1], last_ref, sems.at[1])
+def edges_kernel(x_ref, near_ref, far_ref, sems):
+    even = lax.rem(lax.axis_index("space"), 2) == 0
+    plane = jnp.where(even, D - 1, 0)
+    first = pltpu.make_async_copy(x_ref.at[:, plane], near_ref, sems.at[0])
+    last = pltpu.make_async_copy(x_ref.at[:, D - 1 - plane], far_ref, sems.at[1])
     first.start()
     last.start()
     first.wait()
@@ -127,11 +142,13 @@
     slab_sums(xs, gs, 1, dk_ref, w_ref, (gm_ref.at[0], gm_ref.at[1]), acc_ref, *scratch)
 
 
-def outer_kernel(x_ref, g_ref, lo_ref, hi_ref, dk_ref, w_ref, part_ref,
+def outer_kernel(x_ref, g_ref, near_ref, far_ref, dk_ref, w_ref, part_ref,
                  gm_lo_ref, gm_hi_ref, send_ref, acc_ref, *scratch):
     acc_ref[...] = part_ref[...]
-    xs = [lambda: lo_ref[...]] + [lambda p=p: x_ref[:, p] for p in range(D)]
-    xs += [lambda: hi_ref[...]]
+    even = lax.rem(lax.axis_index("space"), 2) == 0
+    xs = [lambda: jnp.where(even, far_ref[...], near_ref[...])]
+    xs += [lambda p=p: x_ref[:, p] for p in range(D)]
+    xs += [lambda: jnp.where(even, near_ref[...], far_ref[...])]
     gs = [lambda p=p: g_ref[:, p] for p in (0, 3)]
     slab_sums(xs, gs, 3, dk_ref, w_ref, (gm_lo_ref, gm_hi_ref), acc_ref, *scratch)
 
@@ -264,10 +281,11 @@
 
 
 def grads_kernel(place_ref, left_ref, shift_ref, lo_ref, first_ref, inner_ref, last_ref, hi_ref,
-                 dk_ref, white_ref, dvol_ref, dh_ref, taps_ref, out_ref):
-    zeros = jnp.zeros((D + 2, C, W), F32)
-    dh_ref[:, :, 0:W] = zeros
-    dh_ref[:, :, PW - W : PW] = zeros
+                 dk_ref, white_ref, dvol_ref, coarse_ref, fine_ref, out_ref):
+    zeros = jnp.zeros((D + 2, C, W), BF16)
+    for ref in (coarse_ref, fine_ref):
+        ref[:, :, 0:W] = zeros
+        ref[:, :, PW - W : PW] = zeros
     inside_lo = place_ref[1].astype(F32)
     inside_hi = place_ref[2].astype(F32)
     left = left_ref[...]
@@ -285,11 +303,22 @@
         else:
             white = (both[C : 2 * C] + minus_offset).astype(BF16)
             white_ref[:, p - 1] = white.reshape(C, H, W)
-        dh_ref[p, :, W : W + HW] = d_hidden
-    spread_taps(dk_ref, taps_ref, True)
-    stencil(dh_ref, taps_ref, out_ref, D)
+        terms = two_terms(d_hidden)
+        coarse_ref[p, :, W : W + HW] = terms[0]
+        fine_ref[p, :, W : W + HW] = terms[1]
+    matrix, last_taps = tap_matrices(dk_ref, True)
+    terms = two_terms(matrix)
+    matrix = jnp.concatenate(terms, axis=0)
     for z in range(D):
-        dvol_ref[:, z] = out_ref[z].astype(BF16).reshape(C, H, W)
+        for start in range(0, HW, SPAN):
+            coarse = offsets(coarse_ref, z, start, SPAN)
+            fine = offsets(fine_ref, z, start, SPAN)
+            both = dot(matrix, jnp.concatenate(coarse[:8], axis=0))
+            rest = dot(terms[0], jnp.concatenate(fine[:8], axis=0))
+            last = coarse[8].astype(F32) + fine[8].astype(F32)
+            rows = stencil_rows(both[:96] + both[96:] + rest, last, last_taps)
+            out_ref[:, start : start + SPAN] = rows.astype(BF16)
+        dvol_ref[:, z] = out_ref[...].reshape(C, H, W)
 
 
 def finish_kernel(rows_ref, point_ref, taps_ref):
@@ -311,10 +340,8 @@
     forward = [(i, i + 1) for i in range(slabs - 1)]
     backward = [(i + 1, i) for i in range(slabs - 1)]
     scratch = lambda planes: [
-        pltpu.VMEM((planes, C, PW), F32),
         pltpu.VMEM((planes, C, PW), BF16),
-        pltpu.VMEM((2, C, HW), F32),
-        pltpu.VMEM((27, C, W), F32),
+        pltpu.VMEM((2, C, HW), BF16),
         pltpu.VMEM((208, HW), BF16),
     ]
     vmem = pl.BlockSpec(memory_space=pltpu.VMEM)
@@ -322,15 +349,17 @@
     shape = jax.ShapeDtypeStruct
     near = lambda array: pltpu.with_memory_space_constraint(array, pltpu.VMEM)
 
-    x_first, x_last = pl.pallas_call(
+    near_plane, far_plane = pl.pallas_call(
         edges_kernel,
         in_specs=[pl.BlockSpec(memory_space=pl.ANY)],
         out_shape=(pltpu.VMEM((C, H, W), BF16), pltpu.VMEM((C, H, W), BF16)),
         scratch_shapes=[pltpu.SemaphoreType.DMA((2,))],
         name="edges",
     )(x)
-    x_lo = lax.ppermute(x_last, "space", forward)
-    x_hi = lax.ppermute(x_first, "space", backward)
+    partners = [(i, i ^ 1) for i in range(slabs) if i ^ 1 < slabs]
+    others = [(i, i + 1 if i % 2 else i - 1) for i in range(1, slabs) if i % 2 == 0 or i + 1 < slabs]
+    near_plane = lax.ppermute(near_plane, "space", partners)
+    far_plane = lax.ppermute(far_plane, "space", others)
     gm_inner, acc = pl.pallas_call(
         inner_kernel,
         out_shape=(pltpu.VMEM((2, 2 * C, HW), BF16), pltpu.VMEM((368, 256), F32)),
@@ -348,7 +377,7 @@
         scratch_shapes=[pltpu.VMEM((368, 256), F32)] + scratch(D + 2),
         cost_estimate=cost(6),
         name="outer",
-    )(x, g, near(x_lo), near(x_hi), depth_kernel, point_weight, near(acc))
+    )(x, g, near(near_plane), near(far_plane), depth_kernel, point_weight, near(acc))
     gm_lo = lax.ppermute(gm_last, "space", forward)
     gm_hi = lax.ppermute(gm_first, "space", backward)
     parts = lax.all_to_all(send.reshape(C, ROWS, W), "sample", 0, 0)
@@ -377,9 +406,9 @@
         in_specs=[smem] + [vmem] * 8,
         out_shape=(shape((C, D, H, W), BF16), shape((C, D, H, W), BF16)),
         scratch_shapes=[
-            pltpu.VMEM((D + 2, C, PW), F32),
-            pltpu.VMEM((27, C, W), F32),
-            pltpu.VMEM((D, C, HW), F32),
+            pltpu.VMEM((D + 2, C, PW), BF16),
+            pltpu.VMEM((D + 2, C, PW), BF16),
+            pltpu.VMEM((C, HW), BF16),
         ],
         cost_estimate=cost(8),
         name="grads",

time: 86.7 us -> 85.2 us (0.983)
  Pallas kernels: 20 us -> 17 us
  starting transfers between devices: 35.1 us -> 36.9 us
    all_to_all x1, starting transfers between devices: 15.4 us -> 17.8 us  [whole_step(): lax.all_to_all(jnp.broadcast_to(part, (slabs, ROWS, W)), 'space', 0, 0)]
    pallas_call x1, Pallas kernels: 4.67 us -> 3.5 us  [whole_step(): pl.pallas_call(outer_kernel, out_shape=(pltpu.VMEM((2 * C, HW), BF16), pl...]
    pallas_call x1, Pallas kernels: 4.24 us -> 3.26 us  [whole_step(): pl.pallas_call(inner_kernel, out_shape=(pltpu.VMEM((2, 2 * C, HW), BF16),...]
  transfers between devices with their start and end apart: 6 -> 6, of which waited for: 3 -> 2; matrix products, arithmetic and copies ran while one was open for 1% -> 1% of each run, Pallas kernels for 16% -> 14%
where the time goes in v5:
time: 85.2 us; the launch traced here: 84.7 us
  starting transfers between devices  36.9 us (43%)
  blocking collectives  18.3 us (21%)
  Pallas kernels  17 us (20%)
  waiting for transfers between devices  10.3 us (12%)
    all_to_all x1, blocking collectives, whole_step(): parts = lax.all_to_all(send.reshape(C, ROWS, W), 'sample', 0, 0)  18.3 us
    all_to_all x1, starting transfers between devices, whole_step(): lax.all_to_all(jnp.broadcast_to(part, (slabs, ROWS, W)), 'space', 0, 0)  17.8 us
    all_to_all x1, starting transfers between devices, whole_step(): rows = lax.all_to_all(row.reshape(C, 1, W), 'sample', 0, 0).reshape(C, W)  9.46 us
    all_to_all x1, waiting for transfers between devices, whole_step(): lax.all_to_all(jnp.broadcast_to(part, (slabs, ROWS, W)), 'space', 0, 0)  7.76 us
    pallas_call x1, Pallas kernels, whole_step(): pl.pallas_call(grads_kernel, in_specs=[smem] + [vmem] * 8, out_shape=(sha...  4.44 us
    ppermute x1, starting transfers between devices, whole_step(): near_plane = lax.ppermute(near_plane, 'space', partners)  4.36 us
    pallas_call x1, Pallas kernels, whole_step(): pl.pallas_call(lambda *refs: terms_kernel(count, *refs), in_specs=[smem]...  4.15 us
    pallas_call x1, Pallas kernels, whole_step(): pl.pallas_call(outer_kernel, out_shape=(pltpu.VMEM((2 * C, HW), BF16), pl...  3.5 us
  transfers between devices with their start and end apart: 6, of which 2 were waited for; matrix products, arithmetic and copies ran while one was open for 1% of the time, Pallas kernels for 14%

profile of v5, /device:TPU:1, one launch (start us, length us, event | category | flops | bytes accessed | tf_op | source)
XLA Modules:
  0.0 84.7 jit_solution(12387064780874987424)
XLA Ops:
  0.6 1.0 %edges.1 = (bf16[32,16,128]{2,1,0:T(8,128)(2,1)S(1)}, bf16[32,16,128]{2,1,0:T(8,128)(2,1)S(1)}) custom-call(bf16[32,4,16,128]{3,2,1,0:T(8,128)(2,1)} %bitcast.14), custom_call_target="tpu_custom_call" | custom-call | tf_op jit(solution)/shard_map/edges/pallas_call | solution.py:352
  1.6 4.4 %collective-permute-start = (bf16[32,16,128]{2,1,0:T(8,128)(2,1)S(1)}, bf16[32,16,128]{2,1,0:T(8,128)(2,1)S(1)}, u32[]{:S(2)}, u32[]{:S(2)}) collective-permute-start(bf16[32,16,128]{2,1,0:T(8,128)(2,1)S(1)} %get-tuple-element.18), channel_id=1, source_target_pairs={{0,1},{1,0},{2,3},{3,2},{4,5},{5,4},{6,7},{7,6},{8,9},{9,8},{10,11... | collective-permute-start | bytes 393224 | tf_op jit(solution)/shard_map/ppermute | solution.py:361
  6.0 0.7 collective-permute-start.1
  6.7 3.3 %inner.1 = (bf16[2,64,2048]{2,1,0:T(8,128)(2,1)S(1)}, f32[368,256]{1,0:T(8,128)S(1)}) custom-call(bf16[32,4,16,128]{3,2,1,0:T(8,128)(2,1)} %bitcast.15, bf16[32,4,16,128]{3,2,1,0:T(8,128)(2,1)} %bitcast.17, f32[32,27]{1,0:T(8,128)} %dk_ref.5, bf16[32,32]{1,0:T(8,128)(2,1)} %refs_2_.1), custom_call_target="tpu_custom_call" | custom-call | flops 600000000 | bytes 6000000 | tf_op jit(solution)/shard_map/inner/pallas_call | solution.py:363
  9.9 0.0 collective-permute-done.near_ref
  10.0 0.0 collective-permute-done.1.far_ref
  10.0 3.5 %outer.1 = (bf16[64,2048]{1,0:T(8,128)(2,1)S(1)}, bf16[64,2048]{1,0:T(8,128)(2,1)S(1)}, f32[768,128]{1,0:T(8,128)S(1)}) custom-call(bf16[32,4,16,128]{3,2,1,0:T(8,128)(2,1)} %bitcast.16, bf16[32,4,16,128]{3,2,1,0:T(8,128)(2,1)} %bitcast.18, bf16[32,16,128]{2,1,0:T(8,128)(2,1)S(1)} %collective-permute-done.near_ref, ...), custom_call_target="tpu_custom_call" | custom-call | flops 600000000 | bytes 6000000 | tf_op jit(solution)/shard_map/outer/pallas_call | solution.py:370
  13.5 18.3 %all_to_all.15 = f32[32,24,128]{2,1,0:T(8,128)S(1)} all-to-all(f32[32,24,128]{2,1,0:T(8,128)S(1)} %bitcast.12), channel_id=1, replica_groups=mesh['sample'=32,'space'=16] {'sample'}, dimensions={0} | all-to-all | bytes 786432 | tf_op jit(solution)/shard_map/all_to_all | solution.py:383
  31.8 0.7 broadcast_in_dim.9
  32.5 17.8 %all-to-all-start.1 = ((f32[16,24,128]{2,1,0:T(8,128)}), f32[16,24,128]{2,1,0:T(8,128)S(1)}, u32[]{:S(2)}, u32[]{:S(2)}) async-start(f32[16,24,128]{2,1,0:T(8,128)} %broadcast_in_dim.9), calls=%async_computation.1 | async-start | bytes 393216 | tf_op jit(solution)/shard_map/all_to_all | solution.py:385
  50.3 3.3 %collective-permute-start.2 = (bf16[64,2048]{1,0:T(8,128)(2,1)S(1)}, bf16[64,2048]{1,0:T(8,128)(2,1)S(1)}, u32[]{:S(2)}, u32[]{:S(2)}) collective-permute-start(bf16[64,2048]{1,0:T(8,128)(2,1)S(1)} %get-tuple-element.24.last_ref), channel_id=1, source_target_pairs={{0,1},{1,2},{2,3},{3,4},{4,5},{5,6},{6,7},{7,8},{8,9},{9,10},{10,1... | collective-permute-start | bytes 786440 | tf_op jit(solution)/shard_map/ppermute | solution.py:381
  53.6 1.3 %collective-permute-start.3 = (bf16[64,2048]{1,0:T(8,128)(2,1)S(1)}, bf16[64,2048]{1,0:T(8,128)(2,1)S(1)}, u32[]{:S(2)}, u32[]{:S(2)}) collective-permute-start(bf16[64,2048]{1,0:T(8,128)(2,1)S(1)} %get-tuple-element.25.first_ref), channel_id=1, source_target_pairs={{1,0},{2,1},{3,2},{4,3},{5,4},{6,5},{7,6},{8,7},{9,8},{10,9},{11,1... | collective-permute-start | bytes 786440 | tf_op jit(solution)/shard_map/ppermute | solution.py:382
  54.9 0.7 pad_add_fusion.refs_0_.place_ref
  55.6 7.8 %all-to-all-done.1.refs_1_ = f32[16,24,128]{2,1,0:T(8,128)S(1)} async-done(((f32[16,24,128]{2,1,0:T(8,128)}), f32[16,24,128]{2,1,0:T(8,128)S(1)}, u32[]{:S(2)}, u32[]{:S(2)}) %all-to-all-start.1) | async-done | bytes 196640 | tf_op jit(solution)/shard_map/all_to_all | solution.py:385
  63.3 4.1 %terms.1 = (bf16[64,128]{1,0:T(8,128)(2,1)S(1)}, f32[64,128]{1,0:T(8,128)S(1)}, f32[32,128]{1,0:T(8,128)}) custom-call(s32[3]{0:T(128)} %pad_add_fusion.refs_0_.place_ref, f32[16,24,128]{2,1,0:T(8,128)S(1)} %all-to-all-done.1.refs_1_, bf16[32,32]{1,0:T(8,128)(2,1)} %refs_2_.1), custom_call_target="tpu_custom_call" | custom-call | flops 400000000 | bytes 4000000 | tf_op jit(solution)/shard_map/terms/pallas_call | solution.py:392
  67.5 9.5 %all-to-all-start.2 = ((f32[32,1,128]{2,1,0:T(1,128)}), f32[32,1,128]{2,1,0:T(1,128)S(1)}, u32[]{:S(2)}, u32[]{:S(2)}) async-start(f32[32,1,128]{2,1,0:T(1,128)} %bitcast.9), calls=%async_computation.2 | async-start | bytes 32768 | tf_op jit(solution)/shard_map/all_to_all | solution.py:403
  76.9 0.0 collective-permute-done.2.lo_ref
  77.0 0.0 collective-permute-done.3.hi_ref
  77.0 4.4 %grads.1 = (bf16[32,4,16,128]{3,2,1,0:T(8,128)(2,1)}, bf16[32,4,16,128]{3,2,1,0:T(8,128)(2,1)}) custom-call(s32[3]{0:T(128)} %pad_add_fusion.refs_0_.place_ref, bf16[64,128]{1,0:T(8,128)(2,1)S(1)} %get-tuple-element.22.left_ref, f32[64,128]{1,0:T(8,128)S(1)} %get-tuple-element.23.shift_ref, bf16[64,2048]{1,0:T(8,128)(2,1)S(1)} %collective-permute-done.2.lo_ref, ...), custom_call_target="tpu_custom_call" | custom-call | flops 800000000 | bytes 8000000 | tf_op jit(solution)/shard_map/grads/pallas_call | solution.py:404
  81.4 2.5 %all-to-all-done.2 = f32[32,1,128]{2,1,0:T(1,128)S(1)} async-done(((f32[32,1,128]{2,1,0:T(1,128)}), f32[32,1,128]{2,1,0:T(1,128)S(1)}, u32[]{:S(2)}, u32[]{:S(2)}) %all-to-all-start.2) | async-done | bytes 16416 | tf_op jit(solution)/shard_map/all_to_all | solution.py:403
  84.0 0.7 finish.1
  (1 shorter events, 0.0 us)
Async XLA Ops:
  1.6 8.3 %collective-permute-start = (bf16[32,16,128]{2,1,0:T(8,128)(2,1)S(1)}, bf16[32,16,128]{2,1,0:T(8,128)(2,1)S(1)}, u32[]{:S(2)}, u32[]{:S(2)}) collective-permute-start(bf16[32,16,128]{2,1,0:T(8,128)(2,1)S(1)} %get-tuple-element.18), channel_id=1, source_target_pairs={{0,1},{1,0},{2,3},{3,2},{4,5},{5,4},{6,7},{7,6},{8,9},{9,8},{10,11... | collective-permute-start | bytes 393224 | tf_op jit(solution)/shard_map/ppermute | solution.py:361
  6.0 4.0 %collective-permute-start.1 = (bf16[32,16,128]{2,1,0:T(8,128)(2,1)S(1)}, bf16[32,16,128]{2,1,0:T(8,128)(2,1)S(1)}, u32[]{:S(2)}, u32[]{:S(2)}) collective-permute-start(bf16[32,16,128]{2,1,0:T(8,128)(2,1)S(1)} %get-tuple-element.19), channel_id=1, source_target_pairs={{1,2},{2,1},{3,4},{4,3},{5,6},{6,5},{7,8},{8,7},{9,10},{10,9},{11,... | collective-permute-start | bytes 393224 | tf_op jit(solution)/shard_map/ppermute | solution.py:362
  32.5 30.9 %all-to-all-start.1 = ((f32[16,24,128]{2,1,0:T(8,128)}), f32[16,24,128]{2,1,0:T(8,128)S(1)}, u32[]{:S(2)}, u32[]{:S(2)}) async-start(f32[16,24,128]{2,1,0:T(8,128)} %broadcast_in_dim.9), calls=%async_computation.1 | async-start | bytes 393216 | tf_op jit(solution)/shard_map/all_to_all | solution.py:385
  50.3 26.6 %collective-permute-start.2 = (bf16[64,2048]{1,0:T(8,128)(2,1)S(1)}, bf16[64,2048]{1,0:T(8,128)(2,1)S(1)}, u32[]{:S(2)}, u32[]{:S(2)}) collective-permute-start(bf16[64,2048]{1,0:T(8,128)(2,1)S(1)} %get-tuple-element.24.last_ref), channel_id=1, source_target_pairs={{0,1},{1,2},{2,3},{3,4},{4,5},{5,6},{6,7},{7,8},{8,9},{9,10},{10,1... | collective-permute-start | bytes 786440 | tf_op jit(solution)/shard_map/ppermute | solution.py:381
  53.6 23.4 %collective-permute-start.3 = (bf16[64,2048]{1,0:T(8,128)(2,1)S(1)}, bf16[64,2048]{1,0:T(8,128)(2,1)S(1)}, u32[]{:S(2)}, u32[]{:S(2)}) collective-permute-start(bf16[64,2048]{1,0:T(8,128)(2,1)S(1)} %get-tuple-element.25.first_ref), channel_id=1, source_target_pairs={{1,0},{2,1},{3,2},{4,3},{5,4},{6,5},{7,6},{8,7},{9,8},{10,9},{11,1... | collective-permute-start | bytes 786440 | tf_op jit(solution)/shard_map/ppermute | solution.py:382
  67.5 16.5 %all-to-all-start.2 = ((f32[32,1,128]{2,1,0:T(1,128)}), f32[32,1,128]{2,1,0:T(1,128)S(1)}, u32[]{:S(2)}, u32[]{:S(2)}) async-start(f32[32,1,128]{2,1,0:T(1,128)} %bitcast.9), calls=%async_computation.2 | async-start | bytes 32768 | tf_op jit(solution)/shard_map/all_to_all | solution.py:403

commit v6 on v5

--- a/solution.py
+++ b/solution.py
@@ -6,6 +6,7 @@
 from jax.experimental import pallas as pl
 from jax.experimental.pallas import tpu as pltpu
 from jax.sharding import PartitionSpec as P
+
 
 NEWTON = 5
 EPSILON = 1e-05
@@ -72,25 +73,25 @@
     return jnp.concatenate(rows, axis=1)
 
 
-def offsets(ref, plane, start, width):
+def offsets(planes, start, width):
     return [
-        ref[plane + a, :, start + b * W : start + b * W + width]
-        for a in range(3) for b in range(3)
+        planes[a][:, start + b * W : start + b * W + width] for a in range(3) for b in range(3)
     ]
 
 
-def slab_sums(xs, gs, step, dk_ref, w_ref, gm_refs, acc_ref,
-              xb_ref, hid_ref, right_ref):
-    zeros = jnp.zeros((len(xs), C, W), F32)
-    xb_ref[:, :, 0:W] = zeros.astype(BF16)
-    xb_ref[:, :, PW - W : PW] = zeros.astype(BF16)
-    for p, cells in enumerate(xs):
-        xb_ref[p, :, W : W + HW] = cells().reshape(C, HW)
+def fill_plane(ref, cells):
+    zeros = jnp.zeros((C, W), BF16)
+    ref[:, 0:W] = zeros
+    ref[:, PW - W : PW] = zeros
+    ref[:, W : W + HW] = cells.reshape(C, HW)
+
+
+def slab_sums(triples, gs, dk_ref, w_ref, gm_refs, acc_ref, hid_ref, right_ref):
     matrix, last_taps = tap_matrices(dk_ref, False)
     matrix = jnp.concatenate(two_terms(matrix), axis=0)
     for i in range(2):
         for start in range(0, HW, SPAN):
-            cells = offsets(xb_ref, step * i, start, SPAN)
+            cells = offsets(triples[i], start, SPAN)
             both = dot(matrix, jnp.concatenate(cells[:8], axis=0))
             rows = stencil_rows(both[:96] + both[96:], cells[8].astype(F32), last_taps)
             hid_ref[i, :, start : start + SPAN] = rows.astype(BF16)
@@ -110,7 +111,7 @@
     for i in range(2):
         hidden = hid_ref[i]
         mixed = dot(w_ref[...], hidden).astype(BF16)
-        gm_refs[i][0:C, :] = gs[i]().reshape(C, HW)
+        gm_refs[i][0:C, :] = gs[i]()
         gm_refs[i][C : 2 * C, :] = mixed
         for h in range(H):
             span = slice(h * W, (h + 1) * W)
@@ -118,7 +119,7 @@
             right_ref[0:64, span] = pltpu.roll(cells, W - 1, 1) * keep0
             right_ref[64:128, span] = cells
             right_ref[128:192, span] = pltpu.roll(cells, 1, 1) * keep2
-        left = offsets(xb_ref, step * i, 0, HW) + [hidden, mixed, first]
+        left = offsets(triples[i], 0, HW) + [hidden, mixed, first]
         acc_ref[:, 0:208] += dot(
             jnp.concatenate(left, axis=0), right_ref[...], ((1,), (1,))
         )
@@ -135,22 +136,29 @@
     last.wait()
 
 
-def inner_kernel(x_ref, g_ref, dk_ref, w_ref, gm_ref, acc_ref, *scratch):
+def inner_kernel(x_ref, g_ref, dk_ref, w_ref, gm_ref, acc_ref, own_ref, edge_ref, *scratch):
     acc_ref[...] = jnp.zeros(acc_ref.shape, F32)
-    xs = [lambda p=p: x_ref[:, p] for p in range(D)]
-    gs = [lambda p=p: g_ref[:, p] for p in (1, 2)]
-    slab_sums(xs, gs, 1, dk_ref, w_ref, (gm_ref.at[0], gm_ref.at[1]), acc_ref, *scratch)
-
-
-def outer_kernel(x_ref, g_ref, near_ref, far_ref, dk_ref, w_ref, part_ref,
-                 gm_lo_ref, gm_hi_ref, send_ref, acc_ref, *scratch):
+    for p in range(D):
+        fill_plane(own_ref.at[p], x_ref[:, p])
+    for i, p in enumerate((0, D - 1)):
+        edge_ref[i] = g_ref[:, p].reshape(C, HW)
+    triples = [[own_ref.at[i + a] for a in range(3)] for i in range(2)]
+    gs = [lambda p=p: g_ref[:, p].reshape(C, HW) for p in (1, 2)]
+    slab_sums(triples, gs, dk_ref, w_ref, (gm_ref.at[0], gm_ref.at[1]), acc_ref, *scratch)
+
+
+def outer_kernel(own_ref, edge_ref, near_ref, far_ref, dk_ref, w_ref, part_ref,
+                 gm_lo_ref, gm_hi_ref, send_ref, acc_ref, halo_ref, *scratch):
     acc_ref[...] = part_ref[...]
     even = lax.rem(lax.axis_index("space"), 2) == 0
-    xs = [lambda: jnp.where(even, far_ref[...], near_ref[...])]
-    xs += [lambda p=p: x_ref[:, p] for p in range(D)]
-    xs += [lambda: jnp.where(even, near_ref[...], far_ref[...])]
-    gs = [lambda p=p: g_ref[:, p] for p in (0, 3)]
-    slab_sums(xs, gs, 3, dk_ref, w_ref, (gm_lo_ref, gm_hi_ref), acc_ref, *scratch)
+    fill_plane(halo_ref.at[0], jnp.where(even, far_ref[...], near_ref[...]))
+    fill_plane(halo_ref.at[1], jnp.where(even, near_ref[...], far_ref[...]))
+    triples = [
+        [halo_ref.at[0], own_ref.at[0], own_ref.at[1]],
+        [own_ref.at[2], own_ref.at[3], halo_ref.at[1]],
+    ]
+    gs = [lambda i=i: edge_ref[i] for i in range(2)]
+    slab_sums(triples, gs, dk_ref, w_ref, (gm_lo_ref, gm_hi_ref), acc_ref, *scratch)
 
     def put(row, slab):
         send_ref[pl.ds(row, C, stride=ROWS), :] = slab
@@ -311,8 +319,8 @@
     matrix = jnp.concatenate(terms, axis=0)
     for z in range(D):
         for start in range(0, HW, SPAN):
-            coarse = offsets(coarse_ref, z, start, SPAN)
-            fine = offsets(fine_ref, z, start, SPAN)
+            coarse = offsets([coarse_ref.at[z + a] for a in range(3)], start, SPAN)
+            fine = offsets([fine_ref.at[z + a] for a in range(3)], start, SPAN)
             both = dot(matrix, jnp.concatenate(coarse[:8], axis=0))
             rest = dot(terms[0], jnp.concatenate(fine[:8], axis=0))
             last = coarse[8].astype(F32) + fine[8].astype(F32)
@@ -339,11 +347,7 @@
     count = float(D * HW * samples * slabs)
     forward = [(i, i + 1) for i in range(slabs - 1)]
     backward = [(i + 1, i) for i in range(slabs - 1)]
-    scratch = lambda planes: [
-        pltpu.VMEM((planes, C, PW), BF16),
-        pltpu.VMEM((2, C, HW), BF16),
-        pltpu.VMEM((208, HW), BF16),
-    ]
+    scratch = [pltpu.VMEM((2, C, HW), BF16), pltpu.VMEM((208, HW), BF16)]
     vmem = pl.BlockSpec(memory_space=pltpu.VMEM)
     smem = pl.BlockSpec(memory_space=pltpu.SMEM)
     shape = jax.ShapeDtypeStruct
@@ -360,10 +364,15 @@
     others = [(i, i + 1 if i % 2 else i - 1) for i in range(1, slabs) if i % 2 == 0 or i + 1 < slabs]
     near_plane = lax.ppermute(near_plane, "space", partners)
     far_plane = lax.ppermute(far_plane, "space", others)
-    gm_inner, acc = pl.pallas_call(
+    gm_inner, acc, own, edge = pl.pallas_call(
         inner_kernel,
-        out_shape=(pltpu.VMEM((2, 2 * C, HW), BF16), pltpu.VMEM((368, 256), F32)),
-        scratch_shapes=scratch(D),
+        out_shape=(
+            pltpu.VMEM((2, 2 * C, HW), BF16),
+            pltpu.VMEM((368, 256), F32),
+            pltpu.VMEM((D, C, PW), BF16),
+            pltpu.VMEM((2, C, HW), BF16),
+        ),
+        scratch_shapes=scratch,
         cost_estimate=cost(6),
         name="inner",
     )(x, g, depth_kernel, point_weight)
@@ -374,15 +383,18 @@
             pltpu.VMEM((2 * C, HW), BF16),
             pltpu.VMEM((C * ROWS, W), F32),
         ),
-        scratch_shapes=[pltpu.VMEM((368, 256), F32)] + scratch(D + 2),
+        scratch_shapes=[pltpu.VMEM((368, 256), F32), pltpu.VMEM((2, C, PW), BF16)] + scratch,
         cost_estimate=cost(6),
         name="outer",
-    )(x, g, near(near_plane), near(far_plane), depth_kernel, point_weight, near(acc))
+    )(
+        near(own), near(edge), near(near_plane), near(far_plane), depth_kernel, point_weight,
+        near(acc),
+    )
     gm_lo = lax.ppermute(gm_last, "space", forward)
     gm_hi = lax.ppermute(gm_first, "space", backward)
     parts = lax.all_to_all(send.reshape(C, ROWS, W), "sample", 0, 0)
-    part = jnp.sum(parts, axis=0)
-    pay = lax.all_to_all(jnp.broadcast_to(part, (slabs, ROWS, W)), "space", 0, 0)
+    part = jnp.broadcast_to(jnp.sum(parts, axis=0), (slabs, ROWS, W))
+    pay = lax.all_to_all(part, "space", 0, 0)
     slab = lax.axis_index("space")
     place = jnp.stack([
         lax.axis_index("sample"),

time: 85.2 us -> 84.8 us (level)
  no operation moved by 1% of the time
where the time goes in v6:
time: 84.8 us; the launch traced here: 84.1 us
  starting transfers between devices  36.9 us (44%)
  blocking collectives  18.1 us (21%)
  Pallas kernels  16.6 us (20%)
  waiting for transfers between devices  10.3 us (12%)
    all_to_all x1, blocking collectives, whole_step(): parts = lax.all_to_all(send.reshape(C, ROWS, W), 'sample', 0, 0)  18.1 us
    all_to_all x1, starting transfers between devices, whole_step(): pay = lax.all_to_all(part, 'space', 0, 0)  17.8 us
    all_to_all x1, starting transfers between devices, whole_step(): rows = lax.all_to_all(row.reshape(C, 1, W), 'sample', 0, 0).reshape(C, W)  9.48 us
    all_to_all x1, waiting for transfers between devices, whole_step(): pay = lax.all_to_all(part, 'space', 0, 0)  7.78 us
    pallas_call x1, Pallas kernels, whole_step(): pl.pallas_call(grads_kernel, in_specs=[smem] + [vmem] * 8, out_shape=(sha...  4.42 us
    ppermute x1, starting transfers between devices, whole_step(): near_plane = lax.ppermute(near_plane, 'space', partners)  4.36 us
    pallas_call x1, Pallas kernels, whole_step(): pl.pallas_call(lambda *refs: terms_kernel(count, *refs), in_specs=[smem]...  4.15 us
    pallas_call x1, Pallas kernels, whole_step(): pl.pallas_call(inner_kernel, out_shape=(pltpu.VMEM((2, 2 * C, HW), BF16),...  3.34 us
  transfers between devices with their start and end apart: 6, of which 2 were waited for; matrix products, arithmetic and copies ran while one was open for 1% of the time, Pallas kernels for 14%

profile of v6, /device:TPU:1, one launch (start us, length us, event | category | flops | bytes accessed | tf_op | source)
XLA Modules:
  0.0 84.1 jit_solution(2840156794988540185)
XLA Ops:
  0.6 1.0 %edges.1 = (bf16[32,16,128]{2,1,0:T(8,128)(2,1)S(1)}, bf16[32,16,128]{2,1,0:T(8,128)(2,1)S(1)}) custom-call(bf16[32,4,16,128]{3,2,1,0:T(8,128)(2,1)} %bitcast.14), custom_call_target="tpu_custom_call" | custom-call | tf_op jit(solution)/shard_map/edges/pallas_call | solution.py:356
  1.6 4.4 %collective-permute-start = (bf16[32,16,128]{2,1,0:T(8,128)(2,1)S(1)}, bf16[32,16,128]{2,1,0:T(8,128)(2,1)S(1)}, u32[]{:S(2)}, u32[]{:S(2)}) collective-permute-start(bf16[32,16,128]{2,1,0:T(8,128)(2,1)S(1)} %get-tuple-element.22), channel_id=1, source_target_pairs={{0,1},{1,0},{2,3},{3,2},{4,5},{5,4},{6,7},{7,6},{8,9},{9,8},{10,11... | collective-permute-start | bytes 393224 | tf_op jit(solution)/shard_map/ppermute | solution.py:365
  6.0 0.7 collective-permute-start.1
  6.7 3.3 %inner.1 = (bf16[2,64,2048]{2,1,0:T(8,128)(2,1)S(1)}, f32[368,256]{1,0:T(8,128)S(1)}, bf16[4,32,2304]{2,1,0:T(8,128)(2,1)S(1)}, bf16[2,32,2048]{2,1,0:T(8,128)(2,1)S(1)}) custom-call(bf16[32,4,16,128]{3,2,1,0:T(8,128)(2,1)} %bitcast.15, bf16[32,4,16,128]{3,2,1,0:T(8,128)(2,1)} %bitcast.16, f32[32,27]{1,0:T(8,128)} %dk_ref.5, bf16[32,32]{1,0:T(8,128)(2,1)} %refs_2_.1), custom_call_target="tpu_custom_call" | custom-call | flops 600000000 | bytes 6000000 | tf_op jit(solution)/shard_map/inner/pallas_call | solution.py:367
  10.0 0.0 copy-start
  10.0 0.0 collective-permute-done.near_ref
  10.1 0.0 collective-permute-done.1.far_ref
  10.1 3.0 %outer.1 = (bf16[64,2048]{1,0:T(8,128)(2,1)S(1)}, bf16[64,2048]{1,0:T(8,128)(2,1)S(1)}, f32[768,128]{1,0:T(8,128)S(1)}) custom-call(bf16[4,32,2304]{2,1,0:T(8,128)(2,1)S(1)} %get-tuple-element.20.own_ref, bf16[2,32,2048]{2,1,0:T(8,128)(2,1)S(1)} %get-tuple-element.21.edge_ref, bf16[32,16,128]{2,1,0:T(8,128)(2,1)S(1)} %collective-permute-done.near_ref, ...), custom_call_target="tpu_custom_call" | custom-call | flops 600000000 | bytes 6000000 | tf_op jit(solution)/shard_map/outer/pallas_call | solution.py:379
  13.1 0.0 copy-done
  13.1 18.1 %all_to_all.15 = f32[32,24,128]{2,1,0:T(8,128)S(1)} all-to-all(f32[32,24,128]{2,1,0:T(8,128)S(1)} %bitcast.12), channel_id=1, replica_groups=mesh['sample'=32,'space'=16] {'sample'}, dimensions={0} | all-to-all | bytes 786432 | tf_op jit(solution)/shard_map/all_to_all | solution.py:395
  31.3 0.7 broadcast_in_dim.9
  31.9 17.8 %all-to-all-start.1 = ((f32[16,24,128]{2,1,0:T(8,128)}), f32[16,24,128]{2,1,0:T(8,128)S(1)}, u32[]{:S(2)}, u32[]{:S(2)}) async-start(f32[16,24,128]{2,1,0:T(8,128)} %broadcast_in_dim.9), calls=%async_computation.1 | async-start | bytes 393216 | tf_op jit(solution)/shard_map/all_to_all | solution.py:397
  49.8 3.3 %collective-permute-start.2 = (bf16[64,2048]{1,0:T(8,128)(2,1)S(1)}, bf16[64,2048]{1,0:T(8,128)(2,1)S(1)}, u32[]{:S(2)}, u32[]{:S(2)}) collective-permute-start(bf16[64,2048]{1,0:T(8,128)(2,1)S(1)} %get-tuple-element.28.last_ref), channel_id=1, source_target_pairs={{0,1},{1,2},{2,3},{3,4},{4,5},{5,6},{6,7},{7,8},{8,9},{9,10},{10,1... | collective-permute-start | bytes 786440 | tf_op jit(solution)/shard_map/ppermute | solution.py:393
  53.1 1.3 %collective-permute-start.3 = (bf16[64,2048]{1,0:T(8,128)(2,1)S(1)}, bf16[64,2048]{1,0:T(8,128)(2,1)S(1)}, u32[]{:S(2)}, u32[]{:S(2)}) collective-permute-start(bf16[64,2048]{1,0:T(8,128)(2,1)S(1)} %get-tuple-element.29.first_ref), channel_id=1, source_target_pairs={{1,0},{2,1},{3,2},{4,3},{5,4},{6,5},{7,6},{8,7},{9,8},{10,9},{11,1... | collective-permute-start | bytes 786440 | tf_op jit(solution)/shard_map/ppermute | solution.py:394
  54.4 0.6 pad_add_fusion.refs_0_.place_ref
  55.0 0.0 copy-start.1
  55.0 7.8 %all-to-all-done.1.refs_1_ = f32[16,24,128]{2,1,0:T(8,128)S(1)} async-done(((f32[16,24,128]{2,1,0:T(8,128)}), f32[16,24,128]{2,1,0:T(8,128)S(1)}, u32[]{:S(2)}, u32[]{:S(2)}) %all-to-all-start.1) | async-done | bytes 196640 | tf_op jit(solution)/shard_map/all_to_all | solution.py:397
  62.8 4.1 %terms.1 = (bf16[64,128]{1,0:T(8,128)(2,1)S(1)}, f32[64,128]{1,0:T(8,128)S(1)}, f32[32,128]{1,0:T(8,128)}) custom-call(s32[3]{0:T(128)} %pad_add_fusion.refs_0_.place_ref, f32[16,24,128]{2,1,0:T(8,128)S(1)} %all-to-all-done.1.refs_1_, bf16[32,32]{1,0:T(8,128)(2,1)} %refs_2_.1), custom_call_target="tpu_custom_call" | custom-call | flops 400000000 | bytes 4000000 | tf_op jit(solution)/shard_map/terms/pallas_call | solution.py:404
  66.9 9.5 %all-to-all-start.2 = ((f32[32,1,128]{2,1,0:T(1,128)}), f32[32,1,128]{2,1,0:T(1,128)S(1)}, u32[]{:S(2)}, u32[]{:S(2)}) async-start(f32[32,1,128]{2,1,0:T(1,128)} %bitcast.9), calls=%async_computation.2 | async-start | bytes 32768 | tf_op jit(solution)/shard_map/all_to_all | solution.py:415
  76.4 0.0 collective-permute-done.2.lo_ref
  76.4 0.0 collective-permute-done.3.hi_ref
  76.5 0.0 copy-done.1
  76.5 4.4 %grads.1 = (bf16[32,4,16,128]{3,2,1,0:T(8,128)(2,1)}, bf16[32,4,16,128]{3,2,1,0:T(8,128)(2,1)}) custom-call(s32[3]{0:T(128)} %pad_add_fusion.refs_0_.place_ref, bf16[64,128]{1,0:T(8,128)(2,1)S(1)} %get-tuple-element.26.left_ref, f32[64,128]{1,0:T(8,128)S(1)} %get-tuple-element.27.shift_ref, bf16[64,2048]{1,0:T(8,128)(2,1)S(1)} %collective-permute-done.2.lo_ref, ...), custom_call_target="tpu_custom_call" | custom-call | flops 800000000 | bytes 8000000 | tf_op jit(solution)/shard_map/grads/pallas_call | solution.py:416
  80.9 2.6 %all-to-all-done.2 = f32[32,1,128]{2,1,0:T(1,128)S(1)} async-done(((f32[32,1,128]{2,1,0:T(1,128)}), f32[32,1,128]{2,1,0:T(1,128)S(1)}, u32[]{:S(2)}, u32[]{:S(2)}) %all-to-all-start.2) | async-done | bytes 16416 | tf_op jit(solution)/shard_map/all_to_all | solution.py:415
  83.4 0.7 finish.1
  (1 shorter events, 0.0 us)
Async XLA Ops:
  1.6 8.4 %collective-permute-start = (bf16[32,16,128]{2,1,0:T(8,128)(2,1)S(1)}, bf16[32,16,128]{2,1,0:T(8,128)(2,1)S(1)}, u32[]{:S(2)}, u32[]{:S(2)}) collective-permute-start(bf16[32,16,128]{2,1,0:T(8,128)(2,1)S(1)} %get-tuple-element.22), channel_id=1, source_target_pairs={{0,1},{1,0},{2,3},{3,2},{4,5},{5,4},{6,7},{7,6},{8,9},{9,8},{10,11... | collective-permute-start | bytes 393224 | tf_op jit(solution)/shard_map/ppermute | solution.py:365
  6.0 4.1 %collective-permute-start.1 = (bf16[32,16,128]{2,1,0:T(8,128)(2,1)S(1)}, bf16[32,16,128]{2,1,0:T(8,128)(2,1)S(1)}, u32[]{:S(2)}, u32[]{:S(2)}) collective-permute-start(bf16[32,16,128]{2,1,0:T(8,128)(2,1)S(1)} %get-tuple-element.23), channel_id=1, source_target_pairs={{1,2},{2,1},{3,4},{4,3},{5,6},{6,5},{7,8},{8,7},{9,10},{10,9},{11,... | collective-permute-start | bytes 393224 | tf_op jit(solution)/shard_map/ppermute | solution.py:366
  10.0 3.1 %copy-start = (bf16[2,64,2048]{2,1,0:T(8,128)(2,1)}, bf16[2,64,2048]{2,1,0:T(8,128)(2,1)S(1)}, u32[]{:S(2)}) copy-start(bf16[2,64,2048]{2,1,0:T(8,128)(2,1)S(1)} %get-tuple-element.30.inner_ref) | copy-start | bytes 1572868
  31.9 30.9 %all-to-all-start.1 = ((f32[16,24,128]{2,1,0:T(8,128)}), f32[16,24,128]{2,1,0:T(8,128)S(1)}, u32[]{:S(2)}, u32[]{:S(2)}) async-start(f32[16,24,128]{2,1,0:T(8,128)} %broadcast_in_dim.9), calls=%async_computation.1 | async-start | bytes 393216 | tf_op jit(solution)/shard_map/all_to_all | solution.py:397
  49.8 26.6 %collective-permute-start.2 = (bf16[64,2048]{1,0:T(8,128)(2,1)S(1)}, bf16[64,2048]{1,0:T(8,128)(2,1)S(1)}, u32[]{:S(2)}, u32[]{:S(2)}) collective-permute-start(bf16[64,2048]{1,0:T(8,128)(2,1)S(1)} %get-tuple-element.28.last_ref), channel_id=1, source_target_pairs={{0,1},{1,2},{2,3},{3,4},{4,5},{5,6},{6,7},{7,8},{8,9},{9,10},{10,1... | collective-permute-start | bytes 786440 | tf_op jit(solution)/shard_map/ppermute | solution.py:393
  53.1 23.4 %collective-permute-start.3 = (bf16[64,2048]{1,0:T(8,128)(2,1)S(1)}, bf16[64,2048]{1,0:T(8,128)(2,1)S(1)}, u32[]{:S(2)}, u32[]{:S(2)}) collective-permute-start(bf16[64,2048]{1,0:T(8,128)(2,1)S(1)} %get-tuple-element.29.first_ref), channel_id=1, source_target_pairs={{1,0},{2,1},{3,2},{4,3},{5,4},{6,5},{7,6},{8,7},{9,8},{10,9},{11,1... | collective-permute-start | bytes 786440 | tf_op jit(solution)/shard_map/ppermute | solution.py:394
  55.0 21.4 %copy-start.1 = (bf16[2,64,2048]{2,1,0:T(8,128)(2,1)S(1)}, bf16[2,64,2048]{2,1,0:T(8,128)(2,1)}, u32[]{:S(2)}) copy-start(bf16[2,64,2048]{2,1,0:T(8,128)(2,1)} %copy-done) | copy-start | bytes 1572868
  66.9 16.5 %all-to-all-start.2 = ((f32[32,1,128]{2,1,0:T(1,128)}), f32[32,1,128]{2,1,0:T(1,128)S(1)}, u32[]{:S(2)}, u32[]{:S(2)}) async-start(f32[32,1,128]{2,1,0:T(1,128)} %bitcast.9), calls=%async_computation.2 | async-start | bytes 32768 | tf_op jit(solution)/shard_map/all_to_all | solution.py:415

commit v7 on v6

--- a/solution.py
+++ b/solution.py
@@ -18,6 +18,7 @@
 PW = (H + 2) * W
 SPAN = 512
 ROWS = 24
+HALF = 7
 HIGH = lax.Precision.HIGHEST
 F32 = jnp.float32
 BF16 = jnp.bfloat16
@@ -177,7 +178,7 @@
         counts = counts + pltpu.roll(own, 3 * ab, 1)
     counts = counts + pltpu.roll(jnp.where(lane == 65, tile1[9], 0.0), 26, 1)
     put(14, counts)
-    put(15, jnp.zeros((C, W), F32))
+    put(23, jnp.zeros((C, W), F32))
     row = iota((C, W), 0)
     stats = pltpu.roll(acc_ref[320:352, 0:128], 64, 1)
     second = pltpu.roll(stats, 96, 1)
@@ -188,13 +189,21 @@
     for q in range(1, 4):
         packed = packed + pltpu.roll(table[8 * q : 8 * q + 8], 32 * q, 1)
     for r in range(8):
-        put(16 + r, jnp.broadcast_to(packed[r : r + 1], (C, W)))
+        put(15 + r, jnp.broadcast_to(packed[r : r + 1], (C, W)))
+
+
+def fold_kernel(parts_ref, out_ref):
+    total = jnp.sum(parts_ref[...], axis=0)
+    for slab in range(out_ref.shape[0]):
+        half = HALF * (slab % 2)
+        out_ref[slab, 0:HALF] = total[half : half + HALF]
+        out_ref[slab, HALF : HALF + 9] = total[2 * HALF : 2 * HALF + 9]
 
 
 def whiten_terms(stats, count):
-    gf_row = stats[14:15, 0:C]
-    first_row = stats[14:15, C : 2 * C]
-    packed = stats[16:24]
+    gf_row = stats[HALF : HALF + 1, 0:C]
+    first_row = stats[HALF : HALF + 1, C : 2 * C]
+    packed = stats[HALF + 1 : HALF + 9]
     table = jnp.concatenate([pltpu.roll(packed, (W - 32 * q) % W, 1) for q in range(4)], axis=0)
     table = table[:, 0:C]
     row = iota((C, C), 0)
@@ -263,29 +272,33 @@
     shift_ref[C : 2 * C] = jnp.broadcast_to(-offset_col, (C, W))
 
     mine = place_ref[0]
+    half = place_ref[3]
     pick = (iota((C, 1), 0) == mine).astype(F32)
     chosen = jnp.sum(pick * hidden_mat, axis=0, keepdims=True)
     chosen_bias = jnp.sum(pick * bias_col, axis=0, keepdims=True)
-    prod = stats[0:16] * jnp.concatenate([chosen, chosen], axis=1)
-    lane16 = iota((16, W), 1)
-    row16 = iota((16, W), 0)
-    low = jnp.sum(jnp.where(lane16 < 64, prod, 0.0), axis=1, keepdims=True)
-    high = jnp.sum(jnp.where(lane16 < 64, 0.0, prod), axis=1, keepdims=True)
-    to_low = jnp.where(row16 < 9, C + 3 * row16, C + 3 * (row16 - 9) + 2)
-    to_low = jnp.where(row16 == 13, C + 26, jnp.where(row16 > 13, -1, to_low))
-    to_high = jnp.where(row16 < 9, C + 3 * row16 + 1, C + 3 * (row16 - 5) + 2)
-    to_high = jnp.where(row16 > 12, -1, to_high)
-    taps_row = jnp.where(lane16 == to_low, low, 0.0) + jnp.where(lane16 == to_high, high, 0.0)
+    lane8 = iota((8, W), 1)
+    slot = iota((8, W), 0)
+    prod = stats[0:8] * jnp.concatenate([chosen, chosen], axis=1)
+    prod = jnp.where(slot < HALF, prod, 0.0)
+    low = jnp.sum(jnp.where(lane8 < 64, prod, 0.0), axis=1, keepdims=True)
+    high = jnp.sum(jnp.where(lane8 < 64, 0.0, prod), axis=1, keepdims=True)
+    line = slot + HALF * half
+    to_low = jnp.where(line < 9, C + 3 * line, C + 3 * (line - 9) + 2)
+    to_low = jnp.where(line == 13, C + 26, to_low)
+    to_high = jnp.where(line < 9, C + 3 * line + 1, C + 3 * (line - 5) + 2)
+    to_high = jnp.where(line == 13, -1, to_high)
+    taps_row = jnp.where(lane8 == to_low, low, 0.0) + jnp.where(lane8 == to_high, high, 0.0)
     taps_row = jnp.sum(taps_row, axis=0, keepdims=True)
     lane = iota((1, W), 1)
-    ones_row = jnp.where((lane >= 64) & (lane < 91), stats[14:15], 0.0)
-    taps_row = taps_row + chosen_bias * pltpu.roll(ones_row, W - 32, 1)
-    hidden_sum = jnp.sum(jnp.where(lane == 91, stats[14:15], 0.0), axis=1, keepdims=True)
-    pair = pltpu.roll(stats[13:14], 64, 1)[:, 0:64]
+    counts = stats[HALF : HALF + 1]
+    ones_row = jnp.where((lane >= 64) & (lane < 91), counts, 0.0)
+    ones_row = chosen_bias * pltpu.roll(ones_row, W - 32, 1)
+    hidden_sum = jnp.sum(jnp.where(lane == 91, counts, 0.0), axis=1, keepdims=True)
+    pair = pltpu.roll(stats[6:7], 64, 1)[:, 0:64]
     point = dot_high(pair, jnp.concatenate([whiten, symmetric], axis=0)) + hidden_sum * d_first
     point = jnp.concatenate([point, jnp.zeros((1, W - C), F32)], axis=1)
-    row = (taps_row + point) * (1.0 / math.sqrt(count))
-    row_ref[...] = jnp.broadcast_to(row, (C, W))
+    row = (taps_row + jnp.where(half == 1, point + ones_row, 0.0)) * (1.0 / math.sqrt(count))
+    row_ref[...] = jnp.broadcast_to(row, (2 * C, W))
 
 
 def grads_kernel(place_ref, left_ref, shift_ref, lo_ref, first_ref, inner_ref, last_ref, hi_ref,
@@ -330,7 +343,7 @@
 
 
 def finish_kernel(rows_ref, point_ref, taps_ref):
-    rows = rows_ref[...]
+    rows = rows_ref[pl.ds(0, C, stride=2), :] + rows_ref[pl.ds(1, C, stride=2), :]
     point_ref[...] = rows[:, 0:C].T
     taps_ref[...] = rows[:, C : C + 27]
 
@@ -393,13 +406,19 @@
     gm_lo = lax.ppermute(gm_last, "space", forward)
     gm_hi = lax.ppermute(gm_first, "space", backward)
     parts = lax.all_to_all(send.reshape(C, ROWS, W), "sample", 0, 0)
-    part = jnp.broadcast_to(jnp.sum(parts, axis=0), (slabs, ROWS, W))
+    part = pl.pallas_call(
+        fold_kernel,
+        in_specs=[vmem],
+        out_shape=pltpu.VMEM((slabs, HALF + 9, W), F32),
+        name="fold",
+    )(near(parts))
     pay = lax.all_to_all(part, "space", 0, 0)
     slab = lax.axis_index("space")
     place = jnp.stack([
         lax.axis_index("sample"),
         (slab > 0).astype(jnp.int32),
         (slab < slabs - 1).astype(jnp.int32),
+        slab % 2,
     ])
     left, shift, row = pl.pallas_call(
         lambda *refs: terms_kernel(count, *refs),
@@ -407,12 +426,18 @@
         out_shape=(
             pltpu.VMEM((2 * C, 4 * C), BF16),
             pltpu.VMEM((2 * C, W), F32),
-            pltpu.VMEM((C, W), F32),
+            pltpu.VMEM((2 * C, W), F32),
         ),
         cost_estimate=cost(4),
         name="terms",
     )(place, near(pay), point_weight)
-    rows = lax.all_to_all(row.reshape(C, 1, W), "sample", 0, 0).reshape(C, W)
+    groups = [
+        [sample * slabs + slab + i for sample in range(samples) for i in range(2)]
+        for slab in range(0, slabs, 2)
+    ]
+    rows = lax.all_to_all(
+        row.reshape(2 * C, 1, W), ("sample", "space"), 0, 0, axis_index_groups=groups
+    ).reshape(2 * C, W)
     white, d_volume = pl.pallas_call(
         grads_kernel,
         in_specs=[smem] + [vmem] * 8,

time: 84.8 us -> 83.6 us (0.986)
  starting transfers between devices: 36.9 us -> 35.8 us
    all_to_all x1, starting transfers between devices: 9.48 us -> 8.41 us  [whole_step(): lax.all_to_all(row.reshape(2 * C, 1, W), ('sample', 'space'), 0, 0, axis_...]
    all_to_all x1, waiting for transfers between devices: 2.55 us -> 3.42 us  [whole_step(): lax.all_to_all(row.reshape(2 * C, 1, W), ('sample', 'space'), 0, 0, axis_...]
where the time goes in v7:
time: 83.6 us; the launch traced here: 83 us
  starting transfers between devices  35.8 us (43%)
  blocking collectives  18.1 us (22%)
  Pallas kernels  17.3 us (21%)
  waiting for transfers between devices  10.4 us (12%)
    all_to_all x1, blocking collectives, whole_step(): parts = lax.all_to_all(send.reshape(C, ROWS, W), 'sample', 0, 0)  18.1 us
    all_to_all x1, starting transfers between devices, whole_step(): pay = lax.all_to_all(part, 'space', 0, 0)  17.8 us
    all_to_all x1, starting transfers between devices, whole_step(): lax.all_to_all(row.reshape(2 * C, 1, W), ('sample', 'space'), 0, 0, axis_...  8.41 us
    all_to_all x1, waiting for transfers between devices, whole_step(): pay = lax.all_to_all(part, 'space', 0, 0)  6.96 us
    pallas_call x1, Pallas kernels, whole_step(): pl.pallas_call(grads_kernel, in_specs=[smem] + [vmem] * 8, out_shape=(sha...  4.43 us
    ppermute x1, starting transfers between devices, whole_step(): near_plane = lax.ppermute(near_plane, 'space', partners)  4.36 us
    pallas_call x1, Pallas kernels, whole_step(): pl.pallas_call(lambda *refs: terms_kernel(count, *refs), in_specs=[smem]...  4.12 us
    all_to_all x1, waiting for transfers between devices, whole_step(): lax.all_to_all(row.reshape(2 * C, 1, W), ('sample', 'space'), 0, 0, axis_...  3.42 us
  transfers between devices with their start and end apart: 6, of which 2 were waited for; matrix products, arithmetic and copies ran while one was open for 1% of the time, Pallas kernels for 14%

profile of v7, /device:TPU:1, one launch (start us, length us, event | category | flops | bytes accessed | tf_op | source)
XLA Modules:
  0.0 83.0 jit_solution(18402111668890934831)
XLA Ops:
  0.6 1.0 %edges.1 = (bf16[32,16,128]{2,1,0:T(8,128)(2,1)S(1)}, bf16[32,16,128]{2,1,0:T(8,128)(2,1)S(1)}) custom-call(bf16[32,4,16,128]{3,2,1,0:T(8,128)(2,1)} %bitcast.15), custom_call_target="tpu_custom_call" | custom-call | tf_op jit(solution)/shard_map/edges/pallas_call | solution.py:369
  1.6 4.4 %collective-permute-start = (bf16[32,16,128]{2,1,0:T(8,128)(2,1)S(1)}, bf16[32,16,128]{2,1,0:T(8,128)(2,1)S(1)}, u32[]{:S(2)}, u32[]{:S(2)}) collective-permute-start(bf16[32,16,128]{2,1,0:T(8,128)(2,1)S(1)} %get-tuple-element.22), channel_id=1, source_target_pairs={{0,1},{1,0},{2,3},{3,2},{4,5},{5,4},{6,7},{7,6},{8,9},{9,8},{10,11... | collective-permute-start | bytes 393224 | tf_op jit(solution)/shard_map/ppermute | solution.py:378
  6.0 0.7 collective-permute-start.1
  6.7 3.3 %inner.1 = (bf16[2,64,2048]{2,1,0:T(8,128)(2,1)S(1)}, f32[368,256]{1,0:T(8,128)S(1)}, bf16[4,32,2304]{2,1,0:T(8,128)(2,1)S(1)}, bf16[2,32,2048]{2,1,0:T(8,128)(2,1)S(1)}) custom-call(bf16[32,4,16,128]{3,2,1,0:T(8,128)(2,1)} %bitcast.16, bf16[32,4,16,128]{3,2,1,0:T(8,128)(2,1)} %bitcast.17, f32[32,27]{1,0:T(8,128)} %dk_ref.5, bf16[32,32]{1,0:T(8,128)(2,1)} %refs_2_.1), custom_call_target="tpu_custom_call" | custom-call | flops 600000000 | bytes 6000000 | tf_op jit(solution)/shard_map/inner/pallas_call | solution.py:380
  10.0 0.0 copy-start
  10.0 0.0 collective-permute-done.near_ref
  10.1 0.0 collective-permute-done.1.far_ref
  10.1 3.0 %outer.1 = (bf16[64,2048]{1,0:T(8,128)(2,1)S(1)}, bf16[64,2048]{1,0:T(8,128)(2,1)S(1)}, f32[768,128]{1,0:T(8,128)S(1)}) custom-call(bf16[4,32,2304]{2,1,0:T(8,128)(2,1)S(1)} %get-tuple-element.20.own_ref, bf16[2,32,2048]{2,1,0:T(8,128)(2,1)S(1)} %get-tuple-element.21.edge_ref, bf16[32,16,128]{2,1,0:T(8,128)(2,1)S(1)} %collective-permute-done.near_ref, ...), custom_call_target="tpu_custom_call" | custom-call | flops 600000000 | bytes 6000000 | tf_op jit(solution)/shard_map/outer/pallas_call | solution.py:392
  13.1 0.0 copy-done
  13.1 18.1 %all_to_all.15.parts_ref = f32[32,24,128]{2,1,0:T(8,128)S(1)} all-to-all(f32[32,24,128]{2,1,0:T(8,128)S(1)} %bitcast.13), channel_id=1, replica_groups=mesh['sample'=32,'space'=16] {'sample'}, dimensions={0} | all-to-all | bytes 786432 | tf_op jit(solution)/shard_map/all_to_all | solution.py:408
  31.2 0.7 fold.1
  31.9 17.8 %all-to-all-start.1 = ((f32[16,16,128]{2,1,0:T(8,128)}), f32[16,16,128]{2,1,0:T(8,128)S(1)}, u32[]{:S(2)}, u32[]{:S(2)}) async-start(f32[16,16,128]{2,1,0:T(8,128)} %fold.1), calls=%async_computation.1 | async-start | bytes 262144 | tf_op jit(solution)/shard_map/all_to_all | solution.py:415
  49.8 3.3 %collective-permute-start.2 = (bf16[64,2048]{1,0:T(8,128)(2,1)S(1)}, bf16[64,2048]{1,0:T(8,128)(2,1)S(1)}, u32[]{:S(2)}, u32[]{:S(2)}) collective-permute-start(bf16[64,2048]{1,0:T(8,128)(2,1)S(1)} %get-tuple-element.28.last_ref), channel_id=1, source_target_pairs={{0,1},{1,2},{2,3},{3,4},{4,5},{5,6},{6,7},{7,8},{8,9},{9,10},{10,1... | collective-permute-start | bytes 786440 | tf_op jit(solution)/shard_map/ppermute | solution.py:406
  53.1 1.3 %collective-permute-start.3 = (bf16[64,2048]{1,0:T(8,128)(2,1)S(1)}, bf16[64,2048]{1,0:T(8,128)(2,1)S(1)}, u32[]{:S(2)}, u32[]{:S(2)}) collective-permute-start(bf16[64,2048]{1,0:T(8,128)(2,1)S(1)} %get-tuple-element.29.first_ref), channel_id=1, source_target_pairs={{1,0},{2,1},{3,2},{4,3},{5,4},{6,5},{7,6},{8,7},{9,8},{10,9},{11,1... | collective-permute-start | bytes 786440 | tf_op jit(solution)/shard_map/ppermute | solution.py:407
  54.4 0.6 pad_add_fusion.refs_0_.place_ref
  54.9 0.0 copy-start.1
  54.9 7.0 %all-to-all-done.1.refs_1_ = f32[16,16,128]{2,1,0:T(8,128)S(1)} async-done(((f32[16,16,128]{2,1,0:T(8,128)}), f32[16,16,128]{2,1,0:T(8,128)S(1)}, u32[]{:S(2)}, u32[]{:S(2)}) %all-to-all-start.1) | async-done | bytes 131104 | tf_op jit(solution)/shard_map/all_to_all | solution.py:415
  61.9 4.1 %terms.1 = (bf16[64,128]{1,0:T(8,128)(2,1)S(1)}, f32[64,128]{1,0:T(8,128)S(1)}, f32[64,128]{1,0:T(8,128)}) custom-call(s32[4]{0:T(128)} %pad_add_fusion.refs_0_.place_ref, f32[16,16,128]{2,1,0:T(8,128)S(1)} %all-to-all-done.1.refs_1_, bf16[32,32]{1,0:T(8,128)(2,1)} %refs_2_.1), custom_call_target="tpu_custom_call" | custom-call | flops 400000000 | bytes 4000000 | tf_op jit(solution)/shard_map/terms/pallas_call | solution.py:423
  66.0 8.4 %all-to-all-start.2 = ((f32[64,1,128]{2,1,0:T(1,128)}), f32[64,1,128]{2,1,0:T(1,128)S(1)}, u32[]{:S(2)}, u32[]{:S(2)}) async-start(f32[64,1,128]{2,1,0:T(1,128)} %bitcast.10), calls=%async_computation.2 | async-start | bytes 65536 | tf_op jit(solution)/shard_map/all_to_all | solution.py:438
  74.4 0.0 collective-permute-done.2.lo_ref
  74.4 0.0 collective-permute-done.3.hi_ref
  74.4 0.0 copy-done.1
  74.4 4.4 %grads.1 = (bf16[32,4,16,128]{3,2,1,0:T(8,128)(2,1)}, bf16[32,4,16,128]{3,2,1,0:T(8,128)(2,1)}) custom-call(s32[4]{0:T(128)} %pad_add_fusion.refs_0_.place_ref, bf16[64,128]{1,0:T(8,128)(2,1)S(1)} %get-tuple-element.26.left_ref, f32[64,128]{1,0:T(8,128)S(1)} %get-tuple-element.27.shift_ref, bf16[64,2048]{1,0:T(8,128)(2,1)S(1)} %collective-permute-done.2.lo_ref, ...), custom_call_target="tpu_custom_call" | custom-call | flops 800000000 | bytes 8000000 | tf_op jit(solution)/shard_map/grads/pallas_call | solution.py:441
  78.9 3.4 %all-to-all-done.2 = f32[64,1,128]{2,1,0:T(1,128)S(1)} async-done(((f32[64,1,128]{2,1,0:T(1,128)}), f32[64,1,128]{2,1,0:T(1,128)S(1)}, u32[]{:S(2)}, u32[]{:S(2)}) %all-to-all-start.2) | async-done | bytes 32800 | tf_op jit(solution)/shard_map/all_to_all | solution.py:438
  82.3 0.7 finish.1
Async XLA Ops:
  1.6 8.4 %collective-permute-start = (bf16[32,16,128]{2,1,0:T(8,128)(2,1)S(1)}, bf16[32,16,128]{2,1,0:T(8,128)(2,1)S(1)}, u32[]{:S(2)}, u32[]{:S(2)}) collective-permute-start(bf16[32,16,128]{2,1,0:T(8,128)(2,1)S(1)} %get-tuple-element.22), channel_id=1, source_target_pairs={{0,1},{1,0},{2,3},{3,2},{4,5},{5,4},{6,7},{7,6},{8,9},{9,8},{10,11... | collective-permute-start | bytes 393224 | tf_op jit(solution)/shard_map/ppermute | solution.py:378
  6.0 4.1 %collective-permute-start.1 = (bf16[32,16,128]{2,1,0:T(8,128)(2,1)S(1)}, bf16[32,16,128]{2,1,0:T(8,128)(2,1)S(1)}, u32[]{:S(2)}, u32[]{:S(2)}) collective-permute-start(bf16[32,16,128]{2,1,0:T(8,128)(2,1)S(1)} %get-tuple-element.23), channel_id=1, source_target_pairs={{1,2},{2,1},{3,4},{4,3},{5,6},{6,5},{7,8},{8,7},{9,10},{10,9},{11,... | collective-permute-start | bytes 393224 | tf_op jit(solution)/shard_map/ppermute | solution.py:379
  10.0 3.1 %copy-start = (bf16[2,64,2048]{2,1,0:T(8,128)(2,1)}, bf16[2,64,2048]{2,1,0:T(8,128)(2,1)S(1)}, u32[]{:S(2)}) copy-start(bf16[2,64,2048]{2,1,0:T(8,128)(2,1)S(1)} %get-tuple-element.30.inner_ref) | copy-start | bytes 1572868
  31.9 30.0 %all-to-all-start.1 = ((f32[16,16,128]{2,1,0:T(8,128)}), f32[16,16,128]{2,1,0:T(8,128)S(1)}, u32[]{:S(2)}, u32[]{:S(2)}) async-start(f32[16,16,128]{2,1,0:T(8,128)} %fold.1), calls=%async_computation.1 | async-start | bytes 262144 | tf_op jit(solution)/shard_map/all_to_all | solution.py:415
  49.8 24.6 %collective-permute-start.2 = (bf16[64,2048]{1,0:T(8,128)(2,1)S(1)}, bf16[64,2048]{1,0:T(8,128)(2,1)S(1)}, u32[]{:S(2)}, u32[]{:S(2)}) collective-permute-start(bf16[64,2048]{1,0:T(8,128)(2,1)S(1)} %get-tuple-element.28.last_ref), channel_id=1, source_target_pairs={{0,1},{1,2},{2,3},{3,4},{4,5},{5,6},{6,7},{7,8},{8,9},{9,10},{10,1... | collective-permute-start | bytes 786440 | tf_op jit(solution)/shard_map/ppermute | solution.py:406
  53.1 21.4 %collective-permute-start.3 = (bf16[64,2048]{1,0:T(8,128)(2,1)S(1)}, bf16[64,2048]{1,0:T(8,128)(2,1)S(1)}, u32[]{:S(2)}, u32[]{:S(2)}) collective-permute-start(bf16[64,2048]{1,0:T(8,128)(2,1)S(1)} %get-tuple-element.29.first_ref), channel_id=1, source_target_pairs={{1,0},{2,1},{3,2},{4,3},{5,4},{6,5},{7,6},{8,7},{9,8},{10,9},{11,1... | collective-permute-start | bytes 786440 | tf_op jit(solution)/shard_map/ppermute | solution.py:407
  54.9 19.5 %copy-start.1 = (bf16[2,64,2048]{2,1,0:T(8,128)(2,1)S(1)}, bf16[2,64,2048]{2,1,0:T(8,128)(2,1)}, u32[]{:S(2)}) copy-start(bf16[2,64,2048]{2,1,0:T(8,128)(2,1)} %copy-done) | copy-start | bytes 1572868
  66.0 16.3 %all-to-all-start.2 = ((f32[64,1,128]{2,1,0:T(1,128)}), f32[64,1,128]{2,1,0:T(1,128)S(1)}, u32[]{:S(2)}, u32[]{:S(2)}) async-start(f32[64,1,128]{2,1,0:T(1,128)} %bitcast.10), calls=%async_computation.2 | async-start | bytes 65536 | tf_op jit(solution)/shard_map/all_to_all | solution.py:438

commit v8 on v6

--- a/solution.py
+++ b/solution.py
@@ -89,7 +89,7 @@
 def slab_sums(triples, gs, dk_ref, w_ref, gm_refs, acc_ref, hid_ref, right_ref):
     matrix, last_taps = tap_matrices(dk_ref, False)
     matrix = jnp.concatenate(two_terms(matrix), axis=0)
-    for i in range(2):
+    for i in range(len(triples)):
         for start in range(0, HW, SPAN):
             cells = offsets(triples[i], start, SPAN)
             both = dot(matrix, jnp.concatenate(cells[:8], axis=0))
@@ -108,7 +108,7 @@
     for h in range(H):
         right_ref[192:208, h * W : (h + 1) * W] = ones
     first = jnp.where(iota((16, HW), 0) == 0, 1.0, 0.0).astype(BF16)
-    for i in range(2):
+    for i in range(len(triples)):
         hidden = hid_ref[i]
         mixed = dot(w_ref[...], hidden).astype(BF16)
         gm_refs[i][0:C, :] = gs[i]()
@@ -147,18 +147,31 @@
     slab_sums(triples, gs, dk_ref, w_ref, (gm_ref.at[0], gm_ref.at[1]), acc_ref, *scratch)
 
 
-def outer_kernel(own_ref, edge_ref, near_ref, far_ref, dk_ref, w_ref, part_ref,
-                 gm_lo_ref, gm_hi_ref, send_ref, acc_ref, halo_ref, *scratch):
+def outer_sums(on_partner, own_ref, edge_ref, halo_ref, dk_ref, w_ref, part_ref,
+               gm_ref, acc_ref, planes_ref, *scratch):
     acc_ref[...] = part_ref[...]
-    even = lax.rem(lax.axis_index("space"), 2) == 0
-    fill_plane(halo_ref.at[0], jnp.where(even, far_ref[...], near_ref[...]))
-    fill_plane(halo_ref.at[1], jnp.where(even, near_ref[...], far_ref[...]))
-    triples = [
-        [halo_ref.at[0], own_ref.at[0], own_ref.at[1]],
-        [own_ref.at[2], own_ref.at[3], halo_ref.at[1]],
-    ]
-    gs = [lambda i=i: edge_ref[i] for i in range(2)]
-    slab_sums(triples, gs, dk_ref, w_ref, (gm_lo_ref, gm_hi_ref), acc_ref, *scratch)
+    even = lax.rem(lax.axis_index("space"), 2)
+    even = 1 - even if on_partner else even
+    top = even == 1
+    source = jnp.where(top, D - 2, 0)
+    target = jnp.where(top, 0, 1)
+    for i in range(2):
+        planes_ref[target + i] = own_ref[source + i]
+    fill_plane(planes_ref.at[jnp.where(top, 2, 0)], halo_ref[...])
+    triple = [planes_ref.at[a] for a in range(3)]
+    gs = [lambda: edge_ref[jnp.where(top, 1, 0)]]
+    slab_sums([triple], gs, dk_ref, w_ref, (gm_ref,), acc_ref, *scratch)
+
+
+def near_kernel(*refs):
+    outer_sums(True, *refs)
+
+
+def far_kernel(own_ref, edge_ref, halo_ref, dk_ref, w_ref, part_ref, gm_ref, send_ref, acc_ref,
+               *scratch):
+    outer_sums(
+        False, own_ref, edge_ref, halo_ref, dk_ref, w_ref, part_ref, gm_ref, acc_ref, *scratch
+    )
 
     def put(row, slab):
         send_ref[pl.ds(row, C, stride=ROWS), :] = slab
@@ -288,7 +301,7 @@
     row_ref[...] = jnp.broadcast_to(row, (C, W))
 
 
-def grads_kernel(place_ref, left_ref, shift_ref, lo_ref, first_ref, inner_ref, last_ref, hi_ref,
+def grads_kernel(place_ref, left_ref, shift_ref, near_in_ref, near_ref, inner_ref, far_ref, far_in_ref,
                  dk_ref, white_ref, dvol_ref, coarse_ref, fine_ref, out_ref):
     zeros = jnp.zeros((D + 2, C, W), BF16)
     for ref in (coarse_ref, fine_ref):
@@ -299,9 +312,17 @@
     left = left_ref[...]
     bias = shift_ref[0:C, 0:1]
     minus_offset = shift_ref[C : 2 * C, 0:1]
-    planes = [lo_ref, first_ref, inner_ref.at[0], inner_ref.at[1], last_ref, hi_ref]
+    even = lax.rem(lax.axis_index("space"), 2) == 0
+    planes = [
+        lambda: jnp.where(even, far_in_ref[...], near_in_ref[...]),
+        lambda: jnp.where(even, far_ref[...], near_ref[...]),
+        lambda: inner_ref[0],
+        lambda: inner_ref[1],
+        lambda: jnp.where(even, near_ref[...], far_ref[...]),
+        lambda: jnp.where(even, near_in_ref[...], far_in_ref[...]),
+    ]
     for p in range(D + 2):
-        cells = planes[p][...]
+        cells = planes[p]()
         both = dot(left, jnp.concatenate([cells, cells], axis=0))
         d_hidden = both[0:C] + bias
         if p == 0:
@@ -345,8 +366,6 @@
     samples = lax.axis_size("sample")
     slabs = lax.axis_size("space")
     count = float(D * HW * samples * slabs)
-    forward = [(i, i + 1) for i in range(slabs - 1)]
-    backward = [(i + 1, i) for i in range(slabs - 1)]
     scratch = [pltpu.VMEM((2, C, HW), BF16), pltpu.VMEM((208, HW), BF16)]
     vmem = pl.BlockSpec(memory_space=pltpu.VMEM)
     smem = pl.BlockSpec(memory_space=pltpu.SMEM)
@@ -376,22 +395,25 @@
         cost_estimate=cost(6),
         name="inner",
     )(x, g, depth_kernel, point_weight)
-    gm_first, gm_last, send = pl.pallas_call(
-        outer_kernel,
-        out_shape=(
-            pltpu.VMEM((2 * C, HW), BF16),
-            pltpu.VMEM((2 * C, HW), BF16),
-            pltpu.VMEM((C * ROWS, W), F32),
-        ),
-        scratch_shapes=[pltpu.VMEM((368, 256), F32), pltpu.VMEM((2, C, PW), BF16)] + scratch,
-        cost_estimate=cost(6),
-        name="outer",
-    )(
-        near(own), near(edge), near(near_plane), near(far_plane), depth_kernel, point_weight,
-        near(acc),
-    )
-    gm_lo = lax.ppermute(gm_last, "space", forward)
-    gm_hi = lax.ppermute(gm_first, "space", backward)
+    scratch = [pltpu.VMEM((3, C, PW), BF16), pltpu.VMEM((1, C, HW), BF16), scratch[1]]
+    gm_near, acc = pl.pallas_call(
+        near_kernel,
+        out_shape=(pltpu.VMEM((2 * C, HW), BF16), pltpu.VMEM((368, 256), F32)),
+        scratch_shapes=scratch,
+        cost_estimate=cost(3),
+        compiler_params=pltpu.CompilerParams(vmem_limit_bytes=48 << 20),
+        name="near",
+    )(near(own), near(edge), near(near_plane), depth_kernel, point_weight, near(acc))
+    gm_far, send = pl.pallas_call(
+        far_kernel,
+        out_shape=(pltpu.VMEM((2 * C, HW), BF16), pltpu.VMEM((C * ROWS, W), F32)),
+        scratch_shapes=[pltpu.VMEM((368, 256), F32)] + scratch,
+        cost_estimate=cost(3),
+        compiler_params=pltpu.CompilerParams(vmem_limit_bytes=48 << 20),
+        name="far",
+    )(near(own), near(edge), near(far_plane), depth_kernel, point_weight, near(acc))
+    near_in = lax.ppermute(gm_near, "space", partners)
+    far_in = lax.ppermute(gm_far, "space", others)
     parts = lax.all_to_all(send.reshape(C, ROWS, W), "sample", 0, 0)
     part = jnp.broadcast_to(jnp.sum(parts, axis=0), (slabs, ROWS, W))
     pay = lax.all_to_all(part, "space", 0, 0)
@@ -425,8 +447,8 @@
         cost_estimate=cost(8),
         name="grads",
     )(
-        place, near(left), near(shift), near(gm_lo), near(gm_first), near(gm_inner),
-        near(gm_last), near(gm_hi), depth_kernel,
+        place, near(left), near(shift), near(near_in), near(gm_near), near(gm_inner),
+        near(gm_far), near(far_in), depth_kernel,
     )
     d_point, d_kernel = pl.pallas_call(
         finish_kernel,

time: 84.8 us -> 83.2 us (0.981)
  waiting for transfers between devices: 10.3 us -> 8.49 us
    ppermute x2, starting transfers between devices: 4.57 us -> 6.35 us  [the longest x1 5.68 us: whole_step(): near_in = lax.ppermute(gm_near, 'space', partners)]
    all_to_all x1, waiting for transfers between devices: 7.78 us -> 6 us  [whole_step(): pay = lax.all_to_all(part, 'space', 0, 0)]
    all_to_all x1, starting transfers between devices: 17.8 us -> 16.4 us  [whole_step(): pay = lax.all_to_all(part, 'space', 0, 0)]
    pallas_call x1 -> x2, Pallas kernels: 3.03 us -> 3.03 us  [the longest x1 1.62 us: whole_step(): pl.pallas_call(far_kernel, out_shape=(pltpu.VMEM((2 * C, HW), BF16), pltp...]
  transfers between devices with their start and end apart: 6 -> 6, of which waited for: 2 -> 2; matrix products, arithmetic and copies ran while one was open for 1% -> 1% of each run, Pallas kernels for 14% -> 16%
where the time goes in v8:
time: 83.2 us; the launch traced here: 82.7 us
  starting transfers between devices  37.2 us (45%)
  blocking collectives  18.1 us (22%)
  Pallas kernels  16.7 us (20%)
  waiting for transfers between devices  8.49 us (10%)
    all_to_all x1, blocking collectives, whole_step(): parts = lax.all_to_all(send.reshape(C, ROWS, W), 'sample', 0, 0)  18.1 us
    all_to_all x1, starting transfers between devices, whole_step(): pay = lax.all_to_all(part, 'space', 0, 0)  16.4 us
    all_to_all x1, starting transfers between devices, whole_step(): rows = lax.all_to_all(row.reshape(C, 1, W), 'sample', 0, 0).reshape(C, W)  9.36 us
    all_to_all x1, waiting for transfers between devices, whole_step(): pay = lax.all_to_all(part, 'space', 0, 0)  6 us
    ppermute x1, starting transfers between devices, whole_step(): near_in = lax.ppermute(gm_near, 'space', partners)  5.68 us
    pallas_call x1, Pallas kernels, whole_step(): pl.pallas_call(grads_kernel, in_specs=[smem] + [vmem] * 8, out_shape=(sha...  4.5 us
    ppermute x1, starting transfers between devices, whole_step(): near_plane = lax.ppermute(near_plane, 'space', partners)  4.36 us
    pallas_call x1, Pallas kernels, whole_step(): pl.pallas_call(lambda *refs: terms_kernel(count, *refs), in_specs=[smem]...  4.16 us
  transfers between devices with their start and end apart: 6, of which 2 were waited for; matrix products, arithmetic and copies ran while one was open for 1% of the time, Pallas kernels for 16%

profile of v8, /device:TPU:1, one launch (start us, length us, event | category | flops | bytes accessed | tf_op | source)
XLA Modules:
  0.0 82.7 jit_solution(7649767915296673331)
XLA Ops:
  0.6 1.0 %edges.1 = (bf16[32,16,128]{2,1,0:T(8,128)(2,1)S(1)}, bf16[32,16,128]{2,1,0:T(8,128)(2,1)S(1)}) custom-call(bf16[32,4,16,128]{3,2,1,0:T(8,128)(2,1)} %bitcast.14), custom_call_target="tpu_custom_call" | custom-call | tf_op jit(solution)/shard_map/edges/pallas_call | solution.py:375
  1.6 4.4 %collective-permute-start.1 = (bf16[32,16,128]{2,1,0:T(8,128)(2,1)S(1)}, bf16[32,16,128]{2,1,0:T(8,128)(2,1)S(1)}, u32[]{:S(2)}, u32[]{:S(2)}) collective-permute-start(bf16[32,16,128]{2,1,0:T(8,128)(2,1)S(1)} %get-tuple-element.24), channel_id=1, source_target_pairs={{0,1},{1,0},{2,3},{3,2},{4,5},{5,4},{6,7},{7,6},{8,9},{9,8},{10,11... | collective-permute-start | bytes 393224 | tf_op jit(solution)/shard_map/ppermute | solution.py:384
  6.0 0.7 collective-permute-start
  6.7 0.0 copy-start
  6.7 0.0 copy-start.1
  6.7 3.4 %inner.1 = (bf16[2,64,2048]{2,1,0:T(8,128)(2,1)S(1)}, f32[368,256]{1,0:T(8,128)S(1)}, bf16[4,32,2304]{2,1,0:T(8,128)(2,1)S(1)}, bf16[2,32,2048]{2,1,0:T(8,128)(2,1)S(1)}) custom-call(bf16[32,4,16,128]{3,2,1,0:T(8,128)(2,1)} %bitcast.15, bf16[32,4,16,128]{3,2,1,0:T(8,128)(2,1)} %bitcast.16, f32[32,27]{1,0:T(8,128)} %dk_ref.5, bf16[32,32]{1,0:T(8,128)(2,1)} %refs_2_.1), custom_call_target="tpu_custom_call" | custom-call | flops 600000000 | bytes 6000000 | tf_op jit(solution)/shard_map/inner/pallas_call | solution.py:386
  10.1 0.0 collective-permute-done.1.refs_2_
  10.1 0.0 copy-done
  10.1 0.0 copy-done.1
  10.1 1.4 %near.1 = (bf16[64,2048]{1,0:T(8,128)(2,1)S(1)}, f32[368,256]{1,0:T(8,128)S(1)}) custom-call(bf16[4,32,2304]{2,1,0:T(8,128)(2,1)S(1)} %get-tuple-element.21.refs_0_.own_ref, bf16[2,32,2048]{2,1,0:T(8,128)(2,1)S(1)} %get-tuple-element.22.refs_1_.edge_ref, bf16[32,16,128]{2,1,0:T(8,128)(2,1)S(1)} %collective-permute-done.1.refs_2_, f32[32,27]{1,0:T(8,128)S(1)} %copy-done, ...), custom_call_target="tpu_custom_call" | custom-call | flops 300000000 | bytes 3000000 | tf_op jit(solution)/shard_map/near/pallas_call | solution.py:399
  11.5 0.0 collective-permute-done.halo_ref
  11.5 1.6 %far.1 = (bf16[64,2048]{1,0:T(8,128)(2,1)S(1)}, f32[768,128]{1,0:T(8,128)S(1)}) custom-call(bf16[4,32,2304]{2,1,0:T(8,128)(2,1)S(1)} %get-tuple-element.21.refs_0_.own_ref, bf16[2,32,2048]{2,1,0:T(8,128)(2,1)S(1)} %get-tuple-element.22.refs_1_.edge_ref, bf16[32,16,128]{2,1,0:T(8,128)(2,1)S(1)} %collective-permute-done.halo_ref, f32[32,27]{1,0:T(8,128)S(1)} %copy-done, ...), custom_call_target="tpu_custom_call" | custom-call | flops 300000000 | bytes 3000000 | tf_op jit(solution)/shard_map/far/pallas_call | solution.py:407
  13.2 18.1 %all_to_all.15 = f32[32,24,128]{2,1,0:T(8,128)S(1)} all-to-all(f32[32,24,128]{2,1,0:T(8,128)S(1)} %bitcast.12), channel_id=1, replica_groups=mesh['sample'=32,'space'=16] {'sample'}, dimensions={0} | all-to-all | bytes 786432 | tf_op jit(solution)/shard_map/all_to_all | solution.py:417
  31.3 0.7 broadcast_in_dim.9
  32.0 16.4 %all-to-all-start.1 = ((f32[16,24,128]{2,1,0:T(8,128)}), f32[16,24,128]{2,1,0:T(8,128)S(1)}, u32[]{:S(2)}, u32[]{:S(2)}) async-start(f32[16,24,128]{2,1,0:T(8,128)} %broadcast_in_dim.9), calls=%async_computation.1 | async-start | bytes 393216 | tf_op jit(solution)/shard_map/all_to_all | solution.py:419
  48.5 0.7 collective-permute-start.3
  49.1 5.7 %collective-permute-start.2 = (bf16[64,2048]{1,0:T(8,128)(2,1)S(1)}, bf16[64,2048]{1,0:T(8,128)(2,1)S(1)}, u32[]{:S(2)}, u32[]{:S(2)}) collective-permute-start(bf16[64,2048]{1,0:T(8,128)(2,1)S(1)} %get-tuple-element.30.near_ref), channel_id=1, source_target_pairs={{0,1},{1,0},{2,3},{3,2},{4,5},{5,4},{6,7},{7,6},{8,9},{9,8},{10,11... | collective-permute-start | bytes 786440 | tf_op jit(solution)/shard_map/ppermute | solution.py:415
  54.8 0.6 pad_add_fusion.refs_0_.place_ref
  55.5 6.0 %all-to-all-done.1.refs_1_ = f32[16,24,128]{2,1,0:T(8,128)S(1)} async-done(((f32[16,24,128]{2,1,0:T(8,128)}), f32[16,24,128]{2,1,0:T(8,128)S(1)}, u32[]{:S(2)}, u32[]{:S(2)}) %all-to-all-start.1) | async-done | bytes 196640 | tf_op jit(solution)/shard_map/all_to_all | solution.py:419
  61.5 4.2 %terms.1 = (bf16[64,128]{1,0:T(8,128)(2,1)S(1)}, f32[64,128]{1,0:T(8,128)S(1)}, f32[32,128]{1,0:T(8,128)}) custom-call(s32[3]{0:T(128)} %pad_add_fusion.refs_0_.place_ref, f32[16,24,128]{2,1,0:T(8,128)S(1)} %all-to-all-done.1.refs_1_, bf16[32,32]{1,0:T(8,128)(2,1)} %refs_2_.1), custom_call_target="tpu_custom_call" | custom-call | flops 400000000 | bytes 4000000 | tf_op jit(solution)/shard_map/terms/pallas_call | solution.py:426
  65.6 9.4 %all-to-all-start.2 = ((f32[32,1,128]{2,1,0:T(1,128)}), f32[32,1,128]{2,1,0:T(1,128)S(1)}, u32[]{:S(2)}, u32[]{:S(2)}) async-start(f32[32,1,128]{2,1,0:T(1,128)} %bitcast.9), calls=%async_computation.2 | async-start | bytes 32768 | tf_op jit(solution)/shard_map/all_to_all | solution.py:437
  75.0 0.0 collective-permute-done.3.far_in_ref
  75.0 0.0 collective-permute-done.2.near_in_ref
  75.0 4.5 %grads.1 = (bf16[32,4,16,128]{3,2,1,0:T(8,128)(2,1)}, bf16[32,4,16,128]{3,2,1,0:T(8,128)(2,1)}) custom-call(s32[3]{0:T(128)} %pad_add_fusion.refs_0_.place_ref, bf16[64,128]{1,0:T(8,128)(2,1)S(1)} %get-tuple-element.28.left_ref, f32[64,128]{1,0:T(8,128)S(1)} %get-tuple-element.29.shift_ref, bf16[64,2048]{1,0:T(8,128)(2,1)S(1)} %collective-permute-done.2.near_in_ref, ...), custom_call_target="tpu_custom_call" | custom-call | flops 800000000 | bytes 8000000 | tf_op jit(solution)/shard_map/grads/pallas_call | solution.py:438
  79.5 2.5 %all-to-all-done.2 = f32[32,1,128]{2,1,0:T(1,128)S(1)} async-done(((f32[32,1,128]{2,1,0:T(1,128)}), f32[32,1,128]{2,1,0:T(1,128)S(1)}, u32[]{:S(2)}, u32[]{:S(2)}) %all-to-all-start.2) | async-done | bytes 16416 | tf_op jit(solution)/shard_map/all_to_all | solution.py:437
  82.0 0.7 finish.1
  (1 shorter events, 0.0 us)
Async XLA Ops:
  1.6 8.4 %collective-permute-start.1 = (bf16[32,16,128]{2,1,0:T(8,128)(2,1)S(1)}, bf16[32,16,128]{2,1,0:T(8,128)(2,1)S(1)}, u32[]{:S(2)}, u32[]{:S(2)}) collective-permute-start(bf16[32,16,128]{2,1,0:T(8,128)(2,1)S(1)} %get-tuple-element.24), channel_id=1, source_target_pairs={{0,1},{1,0},{2,3},{3,2},{4,5},{5,4},{6,7},{7,6},{8,9},{9,8},{10,11... | collective-permute-start | bytes 393224 | tf_op jit(solution)/shard_map/ppermute | solution.py:384
  6.0 5.5 %collective-permute-start = (bf16[32,16,128]{2,1,0:T(8,128)(2,1)S(1)}, bf16[32,16,128]{2,1,0:T(8,128)(2,1)S(1)}, u32[]{:S(2)}, u32[]{:S(2)}) collective-permute-start(bf16[32,16,128]{2,1,0:T(8,128)(2,1)S(1)} %get-tuple-element.23), channel_id=1, source_target_pairs={{1,2},{2,1},{3,4},{4,3},{5,6},{6,5},{7,8},{8,7},{9,10},{10,9},{11,... | collective-permute-start | bytes 393224 | tf_op jit(solution)/shard_map/ppermute | solution.py:385
  6.7 3.4 %copy-start = (f32[32,27]{1,0:T(8,128)S(1)}, f32[32,27]{1,0:T(8,128)}, u32[]{:S(2)}) copy-start(f32[32,27]{1,0:T(8,128)} %dk_ref.5) | copy-start | bytes 10372
  6.7 3.4 %copy-start.1 = (bf16[32,32]{1,0:T(8,128)(2,1)S(1)}, bf16[32,32]{1,0:T(8,128)(2,1)}, u32[]{:S(2)}) copy-start(bf16[32,32]{1,0:T(8,128)(2,1)} %refs_2_.1) | copy-start | bytes 6148
  32.0 29.4 %all-to-all-start.1 = ((f32[16,24,128]{2,1,0:T(8,128)}), f32[16,24,128]{2,1,0:T(8,128)S(1)}, u32[]{:S(2)}, u32[]{:S(2)}) async-start(f32[16,24,128]{2,1,0:T(8,128)} %broadcast_in_dim.9), calls=%async_computation.1 | async-start | bytes 393216 | tf_op jit(solution)/shard_map/all_to_all | solution.py:419
  48.5 26.5 %collective-permute-start.3 = (bf16[64,2048]{1,0:T(8,128)(2,1)S(1)}, bf16[64,2048]{1,0:T(8,128)(2,1)S(1)}, u32[]{:S(2)}, u32[]{:S(2)}) collective-permute-start(bf16[64,2048]{1,0:T(8,128)(2,1)S(1)} %get-tuple-element.32.far_ref), channel_id=1, source_target_pairs={{1,2},{2,1},{3,4},{4,3},{5,6},{6,5},{7,8},{8,7},{9,10},{10,9},{11,... | collective-permute-start | bytes 786440 | tf_op jit(solution)/shard_map/ppermute | solution.py:416
  49.1 25.9 %collective-permute-start.2 = (bf16[64,2048]{1,0:T(8,128)(2,1)S(1)}, bf16[64,2048]{1,0:T(8,128)(2,1)S(1)}, u32[]{:S(2)}, u32[]{:S(2)}) collective-permute-start(bf16[64,2048]{1,0:T(8,128)(2,1)S(1)} %get-tuple-element.30.near_ref), channel_id=1, source_target_pairs={{0,1},{1,0},{2,3},{3,2},{4,5},{5,4},{6,7},{7,6},{8,9},{9,8},{10,11... | collective-permute-start | bytes 786440 | tf_op jit(solution)/shard_map/ppermute | solution.py:415
  65.6 16.4 %all-to-all-start.2 = ((f32[32,1,128]{2,1,0:T(1,128)}), f32[32,1,128]{2,1,0:T(1,128)S(1)}, u32[]{:S(2)}, u32[]{:S(2)}) async-start(f32[32,1,128]{2,1,0:T(1,128)} %bitcast.9), calls=%async_computation.2 | async-start | bytes 32768 | tf_op jit(solution)/shard_map/all_to_all | solution.py:437

commit v9 on v8

--- a/solution.py
+++ b/solution.py
@@ -86,9 +86,7 @@
     ref[:, W : W + HW] = cells.reshape(C, HW)
 
 
-def slab_sums(triples, gs, dk_ref, w_ref, gm_refs, acc_ref, hid_ref, right_ref):
-    matrix, last_taps = tap_matrices(dk_ref, False)
-    matrix = jnp.concatenate(two_terms(matrix), axis=0)
+def slab_sums(triples, gs, matrix, last_taps, w_ref, gm_refs, base, acc_ref, hid_ref, right_ref):
     for i in range(len(triples)):
         for start in range(0, HW, SPAN):
             cells = offsets(triples[i], start, SPAN)
@@ -120,36 +118,45 @@
             right_ref[64:128, span] = cells
             right_ref[128:192, span] = pltpu.roll(cells, 1, 1) * keep2
         left = offsets(triples[i], 0, HW) + [hidden, mixed, first]
-        acc_ref[:, 0:208] += dot(
-            jnp.concatenate(left, axis=0), right_ref[...], ((1,), (1,))
-        )
+        product = dot(jnp.concatenate(left, axis=0), right_ref[...], ((1,), (1,)))
+        acc_ref[:, 0:208] = product if base is None else base[:, 0:208] + product
+        base = acc_ref
 
 
 def edges_kernel(x_ref, near_ref, far_ref, sems):
     even = lax.rem(lax.axis_index("space"), 2) == 0
     plane = jnp.where(even, D - 1, 0)
-    first = pltpu.make_async_copy(x_ref.at[:, plane], near_ref, sems.at[0])
-    last = pltpu.make_async_copy(x_ref.at[:, D - 1 - plane], far_ref, sems.at[1])
-    first.start()
-    last.start()
-    first.wait()
-    last.wait()
-
-
-def inner_kernel(x_ref, g_ref, dk_ref, w_ref, gm_ref, acc_ref, own_ref, edge_ref, *scratch):
-    acc_ref[...] = jnp.zeros(acc_ref.shape, F32)
+    copies = []
+    for i in range(4):
+        part = pl.ds(8 * i, 8)
+        for side, (ref, p) in enumerate(((near_ref, plane), (far_ref, D - 1 - plane))):
+            copies.append(
+                pltpu.make_async_copy(x_ref.at[part, p], ref.at[part], sems.at[2 * i + side])
+            )
+    for copy in copies:
+        copy.start()
+    for copy in copies:
+        copy.wait()
+
+
+def inner_kernel(x_ref, g_ref, dk_ref, w_ref, gm_ref, acc_ref, own_ref, edge_ref, matrix_ref,
+                 last_ref, *scratch):
+    matrix, last_taps = tap_matrices(dk_ref, False)
+    matrix_ref[...] = jnp.concatenate(two_terms(matrix), axis=0)
+    for e in range(3):
+        last_ref[e] = last_taps[e]
     for p in range(D):
         fill_plane(own_ref.at[p], x_ref[:, p])
     for i, p in enumerate((0, D - 1)):
         edge_ref[i] = g_ref[:, p].reshape(C, HW)
     triples = [[own_ref.at[i + a] for a in range(3)] for i in range(2)]
     gs = [lambda p=p: g_ref[:, p].reshape(C, HW) for p in (1, 2)]
-    slab_sums(triples, gs, dk_ref, w_ref, (gm_ref.at[0], gm_ref.at[1]), acc_ref, *scratch)
-
-
-def outer_sums(on_partner, own_ref, edge_ref, halo_ref, dk_ref, w_ref, part_ref,
+    gm_refs = (gm_ref.at[0], gm_ref.at[1])
+    slab_sums(triples, gs, matrix_ref[...], last_taps, w_ref, gm_refs, None, acc_ref, *scratch)
+
+
+def outer_sums(on_partner, own_ref, edge_ref, halo_ref, matrix_ref, last_ref, w_ref, part_ref,
                gm_ref, acc_ref, planes_ref, *scratch):
-    acc_ref[...] = part_ref[...]
     even = lax.rem(lax.axis_index("space"), 2)
     even = 1 - even if on_partner else even
     top = even == 1
@@ -160,17 +167,21 @@
     fill_plane(planes_ref.at[jnp.where(top, 2, 0)], halo_ref[...])
     triple = [planes_ref.at[a] for a in range(3)]
     gs = [lambda: edge_ref[jnp.where(top, 1, 0)]]
-    slab_sums([triple], gs, dk_ref, w_ref, (gm_ref,), acc_ref, *scratch)
+    last_taps = [last_ref[e] for e in range(3)]
+    slab_sums(
+        [triple], gs, matrix_ref[...], last_taps, w_ref, (gm_ref,), part_ref, acc_ref, *scratch
+    )
 
 
 def near_kernel(*refs):
     outer_sums(True, *refs)
 
 
-def far_kernel(own_ref, edge_ref, halo_ref, dk_ref, w_ref, part_ref, gm_ref, send_ref, acc_ref,
-               *scratch):
+def far_kernel(own_ref, edge_ref, halo_ref, matrix_ref, last_ref, w_ref, part_ref, gm_ref,
+               send_ref, acc_ref, *scratch):
     outer_sums(
-        False, own_ref, edge_ref, halo_ref, dk_ref, w_ref, part_ref, gm_ref, acc_ref, *scratch
+        False, own_ref, edge_ref, halo_ref, matrix_ref, last_ref, w_ref, part_ref, gm_ref,
+        acc_ref, *scratch,
     )
 
     def put(row, slab):
@@ -376,20 +387,22 @@
         edges_kernel,
         in_specs=[pl.BlockSpec(memory_space=pl.ANY)],
         out_shape=(pltpu.VMEM((C, H, W), BF16), pltpu.VMEM((C, H, W), BF16)),
-        scratch_shapes=[pltpu.SemaphoreType.DMA((2,))],
+        scratch_shapes=[pltpu.SemaphoreType.DMA((8,))],
         name="edges",
     )(x)
     partners = [(i, i ^ 1) for i in range(slabs) if i ^ 1 < slabs]
     others = [(i, i + 1 if i % 2 else i - 1) for i in range(1, slabs) if i % 2 == 0 or i + 1 < slabs]
     near_plane = lax.ppermute(near_plane, "space", partners)
     far_plane = lax.ppermute(far_plane, "space", others)
-    gm_inner, acc, own, edge = pl.pallas_call(
+    gm_inner, acc, own, edge, matrix, last = pl.pallas_call(
         inner_kernel,
         out_shape=(
             pltpu.VMEM((2, 2 * C, HW), BF16),
             pltpu.VMEM((368, 256), F32),
             pltpu.VMEM((D, C, PW), BF16),
             pltpu.VMEM((2, C, HW), BF16),
+            pltpu.VMEM((6 * C, 8 * C), BF16),
+            pltpu.VMEM((3, C, W), F32),
         ),
         scratch_shapes=scratch,
         cost_estimate=cost(6),
@@ -403,7 +416,9 @@
         cost_estimate=cost(3),
         compiler_params=pltpu.CompilerParams(vmem_limit_bytes=48 << 20),
         name="near",
-    )(near(own), near(edge), near(near_plane), depth_kernel, point_weight, near(acc))
+    )(
+        near(own), near(edge), near(near_plane), near(matrix), near(last), point_weight, near(acc)
+    )
     gm_far, send = pl.pallas_call(
         far_kernel,
         out_shape=(pltpu.VMEM((2 * C, HW), BF16), pltpu.VMEM((C * ROWS, W), F32)),
@@ -411,7 +426,9 @@
         cost_estimate=cost(3),
         compiler_params=pltpu.CompilerParams(vmem_limit_bytes=48 << 20),
         name="far",
-    )(near(own), near(edge), near(far_plane), depth_kernel, point_weight, near(acc))
+    )(
+        near(own), near(edge), near(far_plane), near(matrix), near(last), point_weight, near(acc)
+    )
     near_in = lax.ppermute(gm_near, "space", partners)
     far_in = lax.ppermute(gm_far, "space", others)
     parts = lax.all_to_all(send.reshape(C, ROWS, W), "sample", 0, 0)

time: 83.2 us -> 83.1 us (level)
  no operation moved by 1% of the time
where the time goes in v9:
time: 83.1 us; the launch traced here: 82.5 us
  starting transfers between devices  36.8 us (44%)
  blocking collectives  18 us (22%)
  Pallas kernels  16.4 us (20%)
  waiting for transfers between devices  8.53 us (10%)
  local copies, waits for them, and re-layouts  1.37 us (2%)
    all_to_all x1, blocking collectives, whole_step(): parts = lax.all_to_all(send.reshape(C, ROWS, W), 'sample', 0, 0)  18 us
    all_to_all x1, starting transfers between devices, whole_step(): pay = lax.all_to_all(part, 'space', 0, 0)  16.1 us
    all_to_all x1, starting transfers between devices, whole_step(): rows = lax.all_to_all(row.reshape(C, 1, W), 'sample', 0, 0).reshape(C, W)  9.38 us
    all_to_all x1, waiting for transfers between devices, whole_step(): pay = lax.all_to_all(part, 'space', 0, 0)  6.03 us
    ppermute x1, starting transfers between devices, whole_step(): near_in = lax.ppermute(gm_near, 'space', partners)  5.68 us
    pallas_call x1, Pallas kernels, whole_step(): pl.pallas_call(grads_kernel, in_specs=[smem] + [vmem] * 8, out_shape=(sha...  4.49 us
    ppermute x1, starting transfers between devices, whole_step(): near_plane = lax.ppermute(near_plane, 'space', partners)  4.36 us
    pallas_call x1, Pallas kernels, whole_step(): pl.pallas_call(lambda *refs: terms_kernel(count, *refs), in_specs=[smem]...  4.15 us
  transfers between devices with their start and end apart: 6, of which 2 were waited for; matrix products, arithmetic and copies ran while one was open for 1% of the time, Pallas kernels for 16%

profile of v9, /device:TPU:1, one launch (start us, length us, event | category | flops | bytes accessed | tf_op | source)
XLA Modules:
  0.0 82.5 jit_solution(14852849394993870268)
XLA Ops:
  0.6 1.0 %edges.1 = (bf16[32,16,128]{2,1,0:T(8,128)(2,1)S(1)}, bf16[32,16,128]{2,1,0:T(8,128)(2,1)S(1)}) custom-call(bf16[32,4,16,128]{3,2,1,0:T(8,128)(2,1)} %bitcast.14), custom_call_target="tpu_custom_call" | custom-call | tf_op jit(solution)/shard_map/edges/pallas_call | solution.py:386
  1.6 4.4 %collective-permute-start.1 = (bf16[32,16,128]{2,1,0:T(8,128)(2,1)S(1)}, bf16[32,16,128]{2,1,0:T(8,128)(2,1)S(1)}, u32[]{:S(2)}, u32[]{:S(2)}) collective-permute-start(bf16[32,16,128]{2,1,0:T(8,128)(2,1)S(1)} %get-tuple-element.28), channel_id=1, source_target_pairs={{0,1},{1,0},{2,3},{3,2},{4,5},{5,4},{6,7},{7,6},{8,9},{9,8},{10,11... | collective-permute-start | bytes 393224 | tf_op jit(solution)/shard_map/ppermute | solution.py:395
  6.0 0.7 collective-permute-start
  6.6 3.3 %inner.1 = (bf16[2,64,2048]{2,1,0:T(8,128)(2,1)S(1)}, f32[368,256]{1,0:T(8,128)S(1)}, bf16[4,32,2304]{2,1,0:T(8,128)(2,1)S(1)}, bf16[2,32,2048]{2,1,0:T(8,128)(2...) custom-call(bf16[32,4,16,128]{3,2,1,0:T(8,128)(2,1)} %bitcast.15, bf16[32,4,16,128]{3,2,1,0:T(8,128)(2,1)} %bitcast.16, ...), custom_call_target="tpu_custom_call" | custom-call | flops 600000000 | bytes 6000000 | tf_op jit(solution)/shard_map/inner/pallas_call | solution.py:397
  10.0 0.0 copy-start
  10.0 0.0 collective-permute-done.1.refs_2_
  10.0 0.7 copy-done
  10.7 1.3 %near.1 = (bf16[64,2048]{1,0:T(8,128)(2,1)S(1)}, f32[368,256]{1,0:T(8,128)S(1)}) custom-call(bf16[4,32,2304]{2,1,0:T(8,128)(2,1)S(1)} %get-tuple-element.23.refs_0_.own_ref, bf16[2,32,2048]{2,1,0:T(8,128)(2,1)S(1)} %get-tuple-element.24.refs_1_.edge_ref, bf16[32,16,128]{2,1,0:T(8,128)(2,1)S(1)} %collective-permute-done.1.refs_2_, ...), custom_call_target="tpu_custom_call" | custom-call | flops 300000000 | bytes 3000000 | tf_op jit(solution)/shard_map/near/pallas_call | solution.py:412
  12.0 0.0 collective-permute-done.halo_ref
  12.0 1.5 %far.1 = (bf16[64,2048]{1,0:T(8,128)(2,1)S(1)}, f32[768,128]{1,0:T(8,128)S(1)}) custom-call(bf16[4,32,2304]{2,1,0:T(8,128)(2,1)S(1)} %get-tuple-element.23.refs_0_.own_ref, bf16[2,32,2048]{2,1,0:T(8,128)(2,1)S(1)} %get-tuple-element.24.refs_1_.edge_ref, bf16[32,16,128]{2,1,0:T(8,128)(2,1)S(1)} %collective-permute-done.halo_ref, ...), custom_call_target="tpu_custom_call" | custom-call | flops 300000000 | bytes 3000000 | tf_op jit(solution)/shard_map/far/pallas_call | solution.py:422
  13.5 18.0 %all_to_all.15 = f32[32,24,128]{2,1,0:T(8,128)S(1)} all-to-all(f32[32,24,128]{2,1,0:T(8,128)S(1)} %bitcast.12), channel_id=1, replica_groups=mesh['sample'=32,'space'=16] {'sample'}, dimensions={0} | all-to-all | bytes 786432 | tf_op jit(solution)/shard_map/all_to_all | solution.py:434
  31.5 0.7 broadcast_in_dim.9
  32.2 16.1 %all-to-all-start.1 = ((f32[16,24,128]{2,1,0:T(8,128)}), f32[16,24,128]{2,1,0:T(8,128)S(1)}, u32[]{:S(2)}, u32[]{:S(2)}) async-start(f32[16,24,128]{2,1,0:T(8,128)} %broadcast_in_dim.9), calls=%async_computation.1 | async-start | bytes 393216 | tf_op jit(solution)/shard_map/all_to_all | solution.py:436
  48.3 0.7 collective-permute-start.3
  49.0 5.7 %collective-permute-start.2 = (bf16[64,2048]{1,0:T(8,128)(2,1)S(1)}, bf16[64,2048]{1,0:T(8,128)(2,1)S(1)}, u32[]{:S(2)}, u32[]{:S(2)}) collective-permute-start(bf16[64,2048]{1,0:T(8,128)(2,1)S(1)} %get-tuple-element.34.near_ref), channel_id=1, source_target_pairs={{0,1},{1,0},{2,3},{3,2},{4,5},{5,4},{6,7},{7,6},{8,9},{9,8},{10,11... | collective-permute-start | bytes 786440 | tf_op jit(solution)/shard_map/ppermute | solution.py:432
  54.7 0.6 pad_add_fusion.refs_0_.place_ref
  55.3 6.0 %all-to-all-done.1.refs_1_ = f32[16,24,128]{2,1,0:T(8,128)S(1)} async-done(((f32[16,24,128]{2,1,0:T(8,128)}), f32[16,24,128]{2,1,0:T(8,128)S(1)}, u32[]{:S(2)}, u32[]{:S(2)}) %all-to-all-start.1) | async-done | bytes 196640 | tf_op jit(solution)/shard_map/all_to_all | solution.py:436
  61.3 4.1 %terms.1 = (bf16[64,128]{1,0:T(8,128)(2,1)S(1)}, f32[64,128]{1,0:T(8,128)S(1)}, f32[32,128]{1,0:T(8,128)}) custom-call(s32[3]{0:T(128)} %pad_add_fusion.refs_0_.place_ref, f32[16,24,128]{2,1,0:T(8,128)S(1)} %all-to-all-done.1.refs_1_, bf16[32,32]{1,0:T(8,128)(2,1)} %refs_2_.1), custom_call_target="tpu_custom_call" | custom-call | flops 400000000 | bytes 4000000 | tf_op jit(solution)/shard_map/terms/pallas_call | solution.py:443
  65.4 9.4 %all-to-all-start.2 = ((f32[32,1,128]{2,1,0:T(1,128)}), f32[32,1,128]{2,1,0:T(1,128)S(1)}, u32[]{:S(2)}, u32[]{:S(2)}) async-start(f32[32,1,128]{2,1,0:T(1,128)} %bitcast.9), calls=%async_computation.2 | async-start | bytes 32768 | tf_op jit(solution)/shard_map/all_to_all | solution.py:454
  74.8 0.0 collective-permute-done.3.far_in_ref
  74.8 0.0 collective-permute-done.2.near_in_ref
  74.8 4.5 %grads.1 = (bf16[32,4,16,128]{3,2,1,0:T(8,128)(2,1)}, bf16[32,4,16,128]{3,2,1,0:T(8,128)(2,1)}) custom-call(s32[3]{0:T(128)} %pad_add_fusion.refs_0_.place_ref, bf16[64,128]{1,0:T(8,128)(2,1)S(1)} %get-tuple-element.32.left_ref, f32[64,128]{1,0:T(8,128)S(1)} %get-tuple-element.33.shift_ref, bf16[64,2048]{1,0:T(8,128)(2,1)S(1)} %collective-permute-done.2.near_in_ref, ...), custom_call_target="tpu_custom_call" | custom-call | flops 800000000 | bytes 8000000 | tf_op jit(solution)/shard_map/grads/pallas_call | solution.py:455
  79.3 2.5 %all-to-all-done.2 = f32[32,1,128]{2,1,0:T(1,128)S(1)} async-done(((f32[32,1,128]{2,1,0:T(1,128)}), f32[32,1,128]{2,1,0:T(1,128)S(1)}, u32[]{:S(2)}, u32[]{:S(2)}) %all-to-all-start.2) | async-done | bytes 16416 | tf_op jit(solution)/shard_map/all_to_all | solution.py:454
  81.8 0.7 finish.1
  (1 shorter events, 0.0 us)
Async XLA Ops:
  1.6 8.4 %collective-permute-start.1 = (bf16[32,16,128]{2,1,0:T(8,128)(2,1)S(1)}, bf16[32,16,128]{2,1,0:T(8,128)(2,1)S(1)}, u32[]{:S(2)}, u32[]{:S(2)}) collective-permute-start(bf16[32,16,128]{2,1,0:T(8,128)(2,1)S(1)} %get-tuple-element.28), channel_id=1, source_target_pairs={{0,1},{1,0},{2,3},{3,2},{4,5},{5,4},{6,7},{7,6},{8,9},{9,8},{10,11... | collective-permute-start | bytes 393224 | tf_op jit(solution)/shard_map/ppermute | solution.py:395
  6.0 6.0 %collective-permute-start = (bf16[32,16,128]{2,1,0:T(8,128)(2,1)S(1)}, bf16[32,16,128]{2,1,0:T(8,128)(2,1)S(1)}, u32[]{:S(2)}, u32[]{:S(2)}) collective-permute-start(bf16[32,16,128]{2,1,0:T(8,128)(2,1)S(1)} %get-tuple-element.25), channel_id=1, source_target_pairs={{1,2},{2,1},{3,4},{4,3},{5,6},{6,5},{7,8},{8,7},{9,10},{10,9},{11,... | collective-permute-start | bytes 393224 | tf_op jit(solution)/shard_map/ppermute | solution.py:396
  10.0 0.7 copy-start
  32.2 29.1 %all-to-all-start.1 = ((f32[16,24,128]{2,1,0:T(8,128)}), f32[16,24,128]{2,1,0:T(8,128)S(1)}, u32[]{:S(2)}, u32[]{:S(2)}) async-start(f32[16,24,128]{2,1,0:T(8,128)} %broadcast_in_dim.9), calls=%async_computation.1 | async-start | bytes 393216 | tf_op jit(solution)/shard_map/all_to_all | solution.py:436
  48.3 26.5 %collective-permute-start.3 = (bf16[64,2048]{1,0:T(8,128)(2,1)S(1)}, bf16[64,2048]{1,0:T(8,128)(2,1)S(1)}, u32[]{:S(2)}, u32[]{:S(2)}) collective-permute-start(bf16[64,2048]{1,0:T(8,128)(2,1)S(1)} %get-tuple-element.36.far_ref), channel_id=1, source_target_pairs={{1,2},{2,1},{3,4},{4,3},{5,6},{6,5},{7,8},{8,7},{9,10},{10,9},{11,... | collective-permute-start | bytes 786440 | tf_op jit(solution)/shard_map/ppermute | solution.py:433
  49.0 25.9 %collective-permute-start.2 = (bf16[64,2048]{1,0:T(8,128)(2,1)S(1)}, bf16[64,2048]{1,0:T(8,128)(2,1)S(1)}, u32[]{:S(2)}, u32[]{:S(2)}) collective-permute-start(bf16[64,2048]{1,0:T(8,128)(2,1)S(1)} %get-tuple-element.34.near_ref), channel_id=1, source_target_pairs={{0,1},{1,0},{2,3},{3,2},{4,5},{5,4},{6,7},{7,6},{8,9},{9,8},{10,11... | collective-permute-start | bytes 786440 | tf_op jit(solution)/shard_map/ppermute | solution.py:432
  65.4 16.4 %all-to-all-start.2 = ((f32[32,1,128]{2,1,0:T(1,128)}), f32[32,1,128]{2,1,0:T(1,128)S(1)}, u32[]{:S(2)}, u32[]{:S(2)}) async-start(f32[32,1,128]{2,1,0:T(1,128)} %bitcast.9), calls=%async_computation.2 | async-start | bytes 32768 | tf_op jit(solution)/shard_map/all_to_all | solution.py:454
